TPU v7x, 128 devices: a whole 4x4x4 slice. The times are simulated.
128 devices in a mesh: row: 8 (over x, z_hi), col: 16 (over z_lo, y, core).
Axes of the slice: x: 4, y: 4, z: 4 (z_hi: 2, z_lo: 2; z = z_hi * 2 + z_lo), core: 2. Of those that a mesh axis runs over, the one named last changes fastest.
Arguments:
- vector: float32 [8192, 16384], P('row', 'col'), may hold values from -6 to 6
- links_alpha: int32 [64, 2], replicated, may hold values from 0 to 63, as said below
- alpha_values: float32 [64, 2, 128, 128], P('row'), may hold values from -0.375 to 0.375
- links_beta: int32 [128, 2], replicated, may hold values from 0 to 127, as said below
- beta_values: float32 [128, 2, 128, 128], P('col'), may hold values from -0.375 to 0.375
Outputs:
- sigma: float32 [8192, 16384], P('row', 'col')
Inputs may be any that keep to these rules, and one draw needn't show every extreme that they name: Row g of links_alpha belongs to the index of row that owns alpha block g, which is g // 8; each entry names a block owned by index e // 8. Among the 16 entries in the rows of one index of row, at most 3 name blocks owned by any one index of row, and for each index some owner supplies exactly 3. Entries may repeat. Row h of links_beta belongs to the index of col that owns beta block h, which is h // 8; each entry names a block owned by index e // 8. Among the 16 entries in the rows of one index of col, at most 2 name blocks owned by any one index of col, and for each index some owner supplies exactly 2. Entries may repeat.
All inputs are finite; a program needn't handle non-finite values.
Results may differ from a plain program's by a relative error of at most 0.000053.
Values sent between devices are 32-bit elements; how exact they have to be, the bound alone decides.
No kernel may reach another device: no remote copies, remote signals or barrier semaphores. Data moves between devices by JAX's collectives and lax.ppermute only.
A program may use at most 128 MiB of HBM per device.

v0:
```python
import jax
import jax.numpy as jnp
from jax import lax
from jax.sharding import PartitionSpec as P


def route_tables(links, peers, groups, myself):
    entries = links.size // peers
    capacity = entries // peers + 1
    entry_lists = links.reshape(peers, entries)
    source = entry_lists // groups
    local_block = entry_lists % groups
    devices = jnp.arange(peers, dtype=jnp.int32)
    matches = (source[:, :, None] == devices[None, None, :]).astype(jnp.int32)
    before = jnp.cumsum(matches, axis=1) - matches
    rank_in = jnp.sum(matches * before, axis=2)
    slots = jnp.arange(capacity, dtype=jnp.int32)
    wanted = jnp.logical_and(
        (source == myself)[:, None, :], rank_in[:, None, :] == slots[None, :, None]
    )
    block_ids = jnp.arange(groups, dtype=jnp.int32)
    local_hot = (local_block[:, :, None] == block_ids[None, None, :]).astype(jnp.float32)
    select = jnp.sum(wanted.astype(jnp.float32)[:, :, :, None] * local_hot[:, None, :, :], axis=2)
    my_source = lax.dynamic_index_in_dim(source, myself, 0, keepdims=False)
    my_rank = lax.dynamic_index_in_dim(rank_in, myself, 0, keepdims=False)
    slot_index = my_source * capacity + my_rank
    all_slots = jnp.arange(peers * capacity, dtype=jnp.int32)
    chooser = (slot_index[:, None] == all_slots[None, :]).astype(jnp.float32)
    return (select, chooser, capacity)


def per_device(vector, links_alpha, alpha_values, links_beta, beta_values):
    highest = lax.Precision.HIGHEST
    rows_here, cols_here = vector.shape
    block_size = alpha_values.shape[2]
    groups_alpha = rows_here // block_size
    groups_beta = cols_here // block_size
    conn_alpha = alpha_values.shape[1]
    conn_beta = beta_values.shape[1]
    peers_row = lax.axis_size("row")
    select_a, chooser_a, capacity_a = route_tables(
        links_alpha, peers_row, groups_alpha, lax.axis_index("row")
    )
    row_blocks = vector.reshape(groups_alpha, block_size, cols_here)
    outgoing_a = jnp.einsum("nrg,gik->nrik", select_a, row_blocks, precision=highest)
    arrived = lax.all_to_all(outgoing_a, "row", split_axis=0, concat_axis=0, tiled=True)
    width = arrived.shape[3]
    slots_flat = arrived.reshape(peers_row * capacity_a, block_size, width)
    picked = jnp.einsum("es,sik->eik", chooser_a, slots_flat, precision=highest)
    picked = picked.reshape(groups_alpha, conn_alpha, block_size, width)
    sigma_alpha = jnp.einsum("gcij,gcjk->gik", alpha_values, picked, precision=highest)
    sigma_alpha = sigma_alpha.reshape(rows_here, cols_here)
    peers_col = lax.axis_size("col")
    select_b, chooser_b, capacity_b = route_tables(
        links_beta, peers_col, groups_beta, lax.axis_index("col")
    )
    col_blocks = vector.reshape(rows_here, groups_beta, block_size)
    outgoing_b = jnp.einsum("nrg,agk->nrak", select_b, col_blocks, precision=highest)
    arrived = lax.all_to_all(outgoing_b, "col", split_axis=0, concat_axis=0, tiled=True)
    height = arrived.shape[2]
    slots_flat = arrived.reshape(peers_col * capacity_b, height, block_size)
    picked = jnp.einsum("es,sak->eak", chooser_b, slots_flat, precision=highest)
    picked = picked.reshape(groups_beta, conn_beta, height, block_size)
    sigma_beta = jnp.einsum("hcak,hcik->ahi", picked, beta_values, precision=highest)
    sigma_beta = sigma_beta.reshape(rows_here, cols_here)
    return sigma_alpha + sigma_beta


def solution(mesh):
    placed = (P("row", "col"), P(), P("row", None, None, None), P(), P("col", None, None, None))
    return jax.shard_map(
        per_device, mesh=mesh, in_specs=placed, out_specs=P("row", "col"), check_vma=False
    )
```

profile of v0, /device:TPU:9, one launch (start us, length us, event | category | flops | bytes accessed | tf_op | source)
XLA Modules:
  0.0 492.1 jit_solution(14695941578879506991)
XLA Ops:
  0.0 0.0 copy-start
  0.0 0.9 copy.75
  0.9 0.1 reshape.274
  1.0 0.1 copy.76
  1.0 0.4 fusion.40
  1.5 0.1 copy.77
  1.6 0.1 multiply_reduce_fusion.1
  1.7 16.2 %fusion.10 = f32[8,3,128,1024]{3,0,2,1:T(8,128)} fusion(f32[8,128,1024]{2,1,0:T(8,128)} %bitcast.48, f32[8,3,8,1]{2,1,0,3:T(4,128)S(1)} %bitcast.51), kind=kOutput, calls=%fused_computation.11 | convolution fusion | flops 301989888 | bytes 16777984 | tf_op jit(solution)/shard_map/nrg,gik->nrik/dot_general | solution.py:45
  17.9 16.4 %copy.82 = f32[8,3,128,1024]{3,2,1,0:T(8,128)} copy(f32[8,3,128,1024]{3,0,2,1:T(8,128)} %fusion.10) | data formatting | bytes 25165824 | tf_op jit(solution)/shard_map/nrg,gik->nrik/dot_general | solution.py:45
  34.3 0.0 copy-start.2
  34.3 7.9 %all-to-all-start = ((f32[8,3,128,1024]{3,2,1,0:T(8,128)}), f32[8,3,128,1024]{3,2,1,0:T(8,128)}, u32[]{:S(2)}, u32[]{:S(2)}) async-start(f32[8,3,128,1024]{3,2,1,0:T(8,128)} %copy.82), calls=%async_computation | async-start | bytes 25165824 | tf_op jit(solution)/shard_map/all_to_all | solution.py:46
  42.2 0.0 copy-done.2
  42.2 0.1 copy.85
  42.4 0.1 reshape.278
  42.4 0.1 copy.86
  42.5 0.5 fusion.39
  43.0 0.1 copy.92
  43.1 0.1 copy.91
  43.2 0.1 copy.93
  43.2 3.2 copy.109
  46.5 0.1 multiply_reduce_fusion
  46.6 13.3 %fusion.21 = f32[16,2,1024,128]{3,0,2,1:T(8,128)S(1)} fusion(f32[1024,8,128,1]{2,1,0,3:T(8,128)S(1)} %bitcast.46, f32[16,2,8,1]{2,1,0,3:T(2,128)S(1)} %bitcast.50), kind=kOutput, calls=%fused_computation.31 | convolution fusion | flops 402653184 | bytes 20972544 | tf_op jit(solution)/shard_map/nrg,agk->nrak/dot_general | solution.py:58
  60.0 10.7 %copy.95 = f32[16,2,1024,128]{3,2,1,0:T(8,128)} copy(f32[16,2,1024,128]{3,0,2,1:T(8,128)S(1)} %fusion.21) | data formatting | bytes 33554432 | tf_op jit(solution)/shard_map/nrg,agk->nrak/dot_general | solution.py:58
  70.6 142.5 %all-to-all-done = f32[8,3,128,1024]{3,2,1,0:T(8,128)} async-done(((f32[8,3,128,1024]{3,2,1,0:T(8,128)}), f32[8,3,128,1024]{3,2,1,0:T(8,128)}, u32[]{:S(2)}, u32[]{:S(2)}) %all-to-all-start) | async-done | bytes 12582944 | tf_op jit(solution)/shard_map/all_to_all | solution.py:46
  213.1 6.6 %all-to-all-start.1 = ((f32[16,2,1024,128]{3,2,1,0:T(8,128)}), f32[16,2,1024,128]{3,2,1,0:T(8,128)}, u32[]{:S(2)}, u32[]{:S(2)}) async-start(f32[16,2,1024,128]{3,2,1,0:T(8,128)} %copy.95), calls=%async_computation.1 | async-start | bytes 33554432 | tf_op jit(solution)/shard_map/all_to_all | solution.py:59
  219.7 0.2 add_reduce_fusion
  219.9 0.1 add.77
  220.0 0.1 copy.90
  220.1 0.1 add.73
  220.2 0.1 copy.78
  220.2 17.4 %fusion.3 = f32[8,2,128,1024]{3,0,2,1:T(8,128)S(1)} fusion(f32[24,128,1024]{2,1,0:T(8,128)} %bitcast.6, s32[8,2]{0,1:T(2,128)S(1)} %copy.78), kind=kOutput, calls=%fused_computation.3 | convolution fusion | flops 603980160 | bytes 20971584 | tf_op jit(solution)/shard_map/es,sik->eik/dot_general | solution.py:49
  237.7 0.0 copy-done
  237.7 9.5 %fusion.8 = f32[8,1024,128,1]{1,2,3,0:T(8,128)} fusion(f32[8,2,128,128]{3,2,1,0:T(8,128)S(1)} %copy-done, f32[8,2,128,1024]{3,0,2,1:T(8,128)S(1)} %fusion.3), kind=kOutput, calls=%fused_computation.8 | convolution fusion | flops 3221225472 | bytes 13631488 | tf_op jit(solution)/shard_map/gcij,gcjk->gik/dot_general | solution.py:51
  247.2 197.6 %all-to-all-done.1 = f32[16,2,1024,128]{3,2,1,0:T(8,128)} async-done(((f32[16,2,1024,128]{3,2,1,0:T(8,128)}), f32[16,2,1024,128]{3,2,1,0:T(8,128)}, u32[]{:S(2)}, u32[]{:S(2)}) %all-to-all-start.1) | async-done | bytes 16777248 | tf_op jit(solution)/shard_map/all_to_all | solution.py:59
  444.8 0.0 copy-start.1
  444.8 23.8 %fusion = f32[8,2,1024,128]{3,0,2,1:T(8,128)S(1)} fusion(f32[32,1024,128]{2,1,0:T(8,128)} %bitcast.16, s32[8,2]{0,1:T(2,128)S(1)} %copy.90), kind=kOutput, calls=%fused_computation | convolution fusion | flops 805306880 | bytes 25165888 | tf_op jit(solution)/shard_map/es,sak->eak/dot_general | solution.py:62
  468.7 0.0 copy-done.1
  468.7 10.8 %fusion.6 = f32[8,1024,128,1]{1,2,3,0:T(8,128)} fusion(f32[8,2,128,128]{3,2,1,0:T(8,128)S(1)} %copy-done.1, f32[8,2,1024,128]{3,0,2,1:T(8,128)S(1)} %fusion), kind=kOutput, calls=%fused_computation.6 | convolution fusion | flops 3221225472 | bytes 13631488 | tf_op jit(solution)/shard_map/hcak,hcik->ahi/dot_general | solution.py:64
  479.5 5.3 %copy.98 = f32[1024,1024]{1,0:T(8,128)} copy(f32[1024,1024]{0,1:T(8,128)} %bitcast.47) | data formatting | bytes 8388608 | tf_op jit(solution)/shard_map/reshape | solution.py:65
  484.8 6.8 %bitcast_add_fusion = f32[1024,1024]{1,0:T(8,128)} fusion(f32[1024,1024]{1,0:T(8,128)} %copy.98, f32[8,1024,128,1]{1,2,3,0:T(8,128)} %fusion.8), kind=kLoop, calls=%fused_computation.10 | loop fusion | flops 1048576 | bytes 12582912 | tf_op jit(solution)/shard_map/add | solution.py:66
  (9 shorter events, 0.1 us)
Async XLA Ops:
  0.0 237.7 %copy-start = (f32[8,2,128,128]{3,2,1,0:T(8,128)S(1)}, f32[8,2,128,128]{3,2,1,0:T(8,128)}, u32[]{:S(2)}) copy-start(f32[8,2,128,128]{3,2,1,0:T(8,128)} %param.7) | copy-start | bytes 3145732
  34.3 7.9 %copy-start.2 = (s32[128,2]{0,1:T(2,128)S(1)}, s32[128,2]{0,1:T(2,128)}, u32[]{:S(2)}) copy-start(s32[128,2]{0,1:T(2,128)} %param.8) | copy-start | bytes 3076
  34.3 178.8 %all-to-all-start = ((f32[8,3,128,1024]{3,2,1,0:T(8,128)}), f32[8,3,128,1024]{3,2,1,0:T(8,128)}, u32[]{:S(2)}, u32[]{:S(2)}) async-start(f32[8,3,128,1024]{3,2,1,0:T(8,128)} %copy.82), calls=%async_computation | async-start | bytes 25165824 | tf_op jit(solution)/shard_map/all_to_all | solution.py:46
  213.1 231.7 %all-to-all-start.1 = ((f32[16,2,1024,128]{3,2,1,0:T(8,128)}), f32[16,2,1024,128]{3,2,1,0:T(8,128)}, u32[]{:S(2)}, u32[]{:S(2)}) async-start(f32[16,2,1024,128]{3,2,1,0:T(8,128)} %copy.95), calls=%async_computation.1 | async-start | bytes 33554432 | tf_op jit(solution)/shard_map/all_to_all | solution.py:59
  444.8 23.8 %copy-start.1 = (f32[8,2,128,128]{3,2,1,0:T(8,128)S(1)}, f32[8,2,128,128]{3,2,1,0:T(8,128)}, u32[]{:S(2)}) copy-start(f32[8,2,128,128]{3,2,1,0:T(8,128)} %param.9) | copy-start | bytes 3145732
where the time goes:
time: 498 us; the launch traced here: 492 us
  waiting for transfers between devices  340 us (68%)
  matrix products  91.1 us (18%)
  local copies, waits for them, and re-layouts  37.5 us (8%)
  starting transfers between devices  14.5 us (3%)
  other arithmetic  8.26 us (2%)
    all_to_all x1, waiting for transfers between devices, per_device(): lax.all_to_all(outgoing_b, 'col', split_axis=0, concat_axis=0, tiled=True)  198 us
    all_to_all x1, waiting for transfers between devices, per_device(): lax.all_to_all(outgoing_a, 'row', split_axis=0, concat_axis=0, tiled=True)  143 us
    dot_general x1, matrix products, per_device(): picked = jnp.einsum('es,sak->eak', chooser_b, slots_flat, precision=highest)  23.8 us
    dot_general x1, matrix products, per_device(): picked = jnp.einsum('es,sik->eik', chooser_a, slots_flat, precision=highest)  17.4 us
    dot_general x1, local copies, waits for them, and re-layouts, per_device(): jnp.einsum('nrg,gik->nrik', select_a, row_blocks, precision=highest)  16.4 us
    dot_general x1, matrix products, per_device(): jnp.einsum('nrg,gik->nrik', select_a, row_blocks, precision=highest)  16.2 us
    dot_general x1, matrix products, per_device(): jnp.einsum('nrg,agk->nrak', select_b, col_blocks, precision=highest)  13.3 us
    dot_general x1, matrix products, per_device(): jnp.einsum('hcak,hcik->ahi', picked, beta_values, precision=highest)  10.8 us
  transfers between devices with their start and end apart: 2, of which 2 were waited for; matrix products, arithmetic and copies ran while one was open for 11% of the time, Pallas kernels for 0%

commit v1 on v0

v1 whole, which is shorter than its diff:
```python
import jax
import jax.numpy as jnp
from jax import lax
from jax.experimental import pallas as pl
from jax.experimental.pallas import tpu as pltpu
from jax.sharding import PartitionSpec as P


B = 128
AXES = ("row", "col")
HOPS = (1, 2, 3)
NX, NZH, NZL, NY, NK = 4, 2, 2, 4, 2


def _index(x, zh, zl, y, k):
    return (x * NZH + zh) * (NZL * NY * NK) + (zl * NY + y) * NK + k


def _pairs(move):
    pairs = []
    for x in range(NX):
        for zh in range(NZH):
            for zl in range(NZL):
                for y in range(NY):
                    for k in range(NK):
                        here = (x, zh, zl, y, k)
                        pairs.append((_index(*here), _index(*move(*here))))
    return pairs


def _z_next(x, zh, zl, y, k):
    z = (2 * zh + zl + (1 if zl == 1 else -1)) % 4
    return (x, z // 2, z % 2, y, k)


TO_CORE = _pairs(lambda x, zh, zl, y, k: (x, zh, zl, y, 1 - k))
TO_ZL = _pairs(lambda x, zh, zl, y, k: (x, zh, 1 - zl, y, k))
TO_ZNEXT = _pairs(_z_next)
TO_X = {d: _pairs(lambda x, zh, zl, y, k, d=d: ((x + d) % NX, zh, zl, y, k)) for d in HOPS}
TO_Y = {d: _pairs(lambda x, zh, zl, y, k, d=d: (x, zh, zl, (y + d) % NY, k)) for d in HOPS}


def _send(value, pairs):
    return lax.ppermute(value, AXES, pairs)


def _send_all(payloads, routes):
    return [_send(value, routes[d]) for d, value in zip(HOPS, payloads)]


def _ranks(mask):
    n = mask.shape[-1]
    earlier = jnp.arange(n)[:, None] < jnp.arange(n)[None, :]
    return jnp.sum(mask[..., :, None] * earlier.astype(jnp.int32), axis=-2)


def _lists(mask, pos, slots):
    n = mask.shape[-1]
    hit = mask[..., :, None] * (pos[..., :, None] == jnp.arange(slots)).astype(jnp.int32)
    return jnp.sum(hit * jnp.arange(n, dtype=jnp.int32)[:, None], axis=-2)


def _members(entries, blocks):
    hit = entries[:, :, None] == jnp.arange(blocks, dtype=jnp.int32)
    return jnp.max(hit.astype(jnp.int32), axis=1)


def alpha_tables(links, x, zh):
    wanted = links.reshape(NX * NZH, 16)
    mask = _members(wanted, 64).reshape(NX, NZH, NX, NZH, 8)
    mask = jnp.stack([mask[:, 0], mask[:, 1][:, :, ::-1]], axis=1)
    rank = _ranks(mask)
    mask = lax.dynamic_index_in_dim(mask, zh, 1, keepdims=False)
    rank = lax.dynamic_index_in_dim(rank, zh, 1, keepdims=False)
    sent_mask = lax.dynamic_index_in_dim(mask, x, 1, keepdims=False)
    sent_rank = lax.dynamic_index_in_dim(rank, x, 1, keepdims=False)
    lists = _lists(sent_mask, sent_rank, 3)
    lists = jnp.roll(lists, -x, axis=0)[1:]
    mine = lax.dynamic_index_in_dim(wanted, x * NZH + zh, 0, keepdims=False)
    source, block = mine // 8, mine % 8
    source_x, other = source // NZH, jnp.abs(source % NZH - zh)
    my_rank = lax.dynamic_index_in_dim(rank, x, 0, keepdims=False).reshape(-1)
    key = (source_x * 2 + other) * 8 + block
    slot = jnp.sum((key[:, None] == jnp.arange(my_rank.size)) * my_rank, axis=1)
    hop = (x - source_x) % NX
    place = jnp.where(hop == 0, other, 1 + hop + 3 * other)
    code = place * 32 + jnp.where(hop == 0, block, slot)
    return lists[:, 0].reshape(-1), lists[:, 1].reshape(-1), code.astype(jnp.int32)


def beta_tables(links, zl, y, k, first, second):
    wanted = links.reshape(NZL * NY, 32)
    mask = _members(wanted, 128).reshape(NZL, NY, NZL, NY, 16)
    mask = jnp.stack([mask[0], mask[1][:, ::-1]], axis=0)
    mask = jnp.swapaxes(mask, 2, 3)
    rank = _ranks(mask)
    own_count = jnp.sum(mask[:, :, :, 0], axis=-1)
    base = jnp.maximum(own_count, first)[..., None]
    pos = jnp.stack([rank[:, :, :, 0], base + rank[:, :, :, 1]], axis=3)
    mask = mask.reshape(NZL, NY, NY, 32)
    pos = pos.reshape(NZL, NY, NY, 32)
    far = (jnp.arange(NY)[:, None] != jnp.arange(NY)[None, :]).astype(jnp.int32)
    fits = jnp.max(mask * (pos + 1) * far[None, :, :, None]) <= first + second
    mask = lax.dynamic_index_in_dim(mask, zl, 0, keepdims=False)
    pos = lax.dynamic_index_in_dim(pos, zl, 0, keepdims=False)
    sent = _lists(
        lax.dynamic_index_in_dim(mask, y, 1, keepdims=False),
        lax.dynamic_index_in_dim(pos, y, 1, keepdims=False),
        first + second,
    )
    sent = jnp.roll(sent, -y, axis=0)[1:]
    core = (sent // 8) % 2
    sent = ((sent // 16) * 2 + jnp.abs(core - k)) * 32 + sent % 8
    mine = lax.dynamic_index_in_dim(wanted, zl * NY + y, 0, keepdims=False)
    chip, block = mine // 16, mine % 16
    source_y, other = chip % NY, jnp.abs(chip // NY - zl)
    my_pos = lax.dynamic_index_in_dim(pos, y, 0, keepdims=False).reshape(-1)
    key = (source_y * 2 + other) * 16 + block
    slot = jnp.sum((key[:, None] == jnp.arange(my_pos.size)) * my_pos, axis=1)
    hop = (y - source_y) % NY
    late = (slot >= first).astype(jnp.int32)
    near = (other * 2 + jnp.abs(block // 8 - k)) * 32 + block % 8
    code = jnp.where(hop == 0, near, (3 + hop + 3 * late) * 32 + slot - first * late)
    code = jnp.roll(code.reshape(2, 16), -k, axis=0).reshape(-1)
    return sent[:, :first].reshape(-1), sent[:, first:].reshape(-1), code.astype(jnp.int32), fits


def _rows(i):
    return pl.ds(pl.multiple_of(i * B, B), B)


def _core():
    return lax.rem(lax.axis_index("col"), NK).reshape(1)


def _fetch(code, options, dst, sem):
    place, at = code // 32, code % 32
    for number, source, half in options:
        test = place == number
        if half is not None:
            test = jnp.logical_and(test, at // 4 == half)

        @pl.when(test)
        def _(source=source):
            pltpu.make_async_copy(source(at), dst, sem).start()


def _wait(ref, sem):
    pltpu.make_async_copy(ref, ref, sem).wait()


ANY = pl.BlockSpec(memory_space=pl.ANY)
SMEM = pl.BlockSpec(memory_space=pltpu.SMEM)
VMEM = pl.BlockSpec(memory_space=pltpu.VMEM)


def _f32(*shape):
    return jax.ShapeDtypeStruct(shape, jnp.float32)


def _params():
    return pltpu.CompilerParams(vmem_limit_bytes=63 * 2**20)


def _cost(bytes_, flops=0):
    return pl.CostEstimate(flops=flops, bytes_accessed=bytes_, transcendentals=0)


def _gather(codes, slot_shape, slots, sources, options_of):
    count = 3 * slots

    def kernel(code_ref, k_ref, *refs):
        ins, outs = refs[: len(sources)], refs[len(sources) : len(sources) + 3]
        buf, in_sem, out_sem = refs[len(sources) + 3 :]
        options = options_of(ins, k_ref[0])
        for s in range(count):
            _fetch(code_ref[s], options, buf.at[s], in_sem.at[s])
        copies = []
        for s in range(count):
            _wait(buf.at[s], in_sem.at[s])
            copy = pltpu.make_async_copy(buf.at[s], outs[s // slots].at[s % slots], out_sem.at[s])
            copy.start()
            copies.append(copy)
        for copy in copies:
            copy.wait()

    size = 4 * count
    for n in slot_shape:
        size *= n
    return pl.pallas_call(
        kernel,
        out_shape=[_f32(slots, *slot_shape)] * 3,
        in_specs=[SMEM, SMEM] + [ANY] * len(sources),
        out_specs=[ANY] * 3,
        scratch_shapes=[
            pltpu.VMEM((count, *slot_shape), jnp.float32),
            pltpu.SemaphoreType.DMA((count,)),
            pltpu.SemaphoreType.DMA((count,)),
        ],
        compiler_params=_params(),
        cost_estimate=_cost(2 * size),
    )(codes, _core(), *sources)


def _pick(shapes, sources, picks_of):
    def kernel(k_ref, *refs):
        ins, outs = refs[: len(sources)], refs[len(sources) : len(sources) + len(shapes)]
        bufs = refs[len(sources) + len(shapes) : -2]
        in_sem, out_sem = refs[-2:]
        loads, stores = [], []
        for n, (source, number, at) in enumerate(picks_of(ins, k_ref[0])):
            buf, out = bufs[number], outs[number]
            if at is not None:
                buf, out = buf.at[at], out.at[at]
            loads.append(pltpu.make_async_copy(source, buf, in_sem.at[n]))
            stores.append(pltpu.make_async_copy(buf, out, out_sem.at[n]))
        for copy in loads:
            copy.start()
        for load, store in zip(loads, stores):
            load.wait()
            store.start()
        for copy in stores:
            copy.wait()

    size = 0
    for shape in shapes:
        words = 1
        for n in shape:
            words *= n
        size += 8 * words
    return pl.pallas_call(
        kernel,
        out_shape=[_f32(*shape) for shape in shapes],
        in_specs=[SMEM] + [ANY] * len(sources),
        out_specs=[ANY] * len(shapes),
        scratch_shapes=[pltpu.VMEM(shape, jnp.float32) for shape in shapes]
        + [pltpu.SemaphoreType.DMA((4,)), pltpu.SemaphoreType.DMA((4,))],
        compiler_params=_params(),
        cost_estimate=_cost(size),
    )(_core(), *sources)


def _split(v):
    high = v.astype(jnp.bfloat16)
    return high, (v - high.astype(jnp.float32)).astype(jnp.bfloat16)


def _dot3(a, b, dims):
    ah, al = _split(a)
    bh, bl = _split(b)

    def dot(p, q):
        return lax.dot_general(p, q, (dims, ((), ())), preferred_element_type=jnp.float32)

    return dot(ah, bh) + (dot(ah, bl) + dot(al, bh))


def _my_rows(r, k):
    return pl.ds(pl.multiple_of(r * 512 + k * 256, 256), 256)


def _half_rows(k):
    return pl.ds(pl.multiple_of(k * 256, 256), 256)


def _near(r, k, v, x0, q0, q1, x1):
    return [
        (0, lambda j: v.at[_my_rows(r, k), _rows(j)], None),
        (1, lambda j: x0.at[r, :, _rows(j)], None),
        (2, lambda j: q0.at[_half_rows(k), _rows(j % 4)], 0),
        (2, lambda j: q1.at[_half_rows(k), _rows(j % 4)], 1),
        (3, lambda j: x1.at[j // 4, :, _rows(j % 4)], None),
    ]


def beta_product(r, codes, mine, other, v, x0, q0, q1, x1, early, late):
    def kernel(code_ref, k_ref, mine_ref, other_ref, *refs):
        out_mine, out_other, buf, sem = refs[11:]
        options = _near(r, k_ref[0], *refs[0:5])
        options += [(4 + i, lambda s, i=i: refs[5 + i].at[s, r], None) for i in range(3)]
        options += [(7 + i, lambda s, i=i: refs[8 + i].at[s], None) for i in range(3)]
        for n in range(32):
            _fetch(code_ref[n], options, buf.at[n], sem.at[n])
        for h in range(16):
            w_ref, out = (mine_ref, out_mine) if h < 8 else (other_ref, out_other)
            w = jnp.concatenate([w_ref[h % 8, 0], w_ref[h % 8, 1]], axis=1)
            _wait(buf.at[2 * h], sem.at[2 * h])
            _wait(buf.at[2 * h + 1], sem.at[2 * h + 1])
            blocks = jnp.concatenate([buf[2 * h], buf[2 * h + 1]], axis=1)
            out[:, (h % 8) * B : (h % 8 + 1) * B] = _dot3(blocks, w, ((1,), (1,)))

    return pl.pallas_call(
        kernel,
        out_shape=[_f32(256, 1024)] * 2,
        in_specs=[SMEM, SMEM, VMEM, VMEM] + [ANY] * 11,
        out_specs=[VMEM, VMEM],
        scratch_shapes=[pltpu.VMEM((32, 256, B), jnp.float32), pltpu.SemaphoreType.DMA((32,))],
        compiler_params=_params(),
        cost_estimate=_cost(8 * 2**20, 3 * 32 * 2 * 256 * B * B),
    )(codes, _core(), mine, other, v, x0, q0, q1, x1, *early, *late)


def alpha_product(c, codes, values, v, q0, q1, own, late, tail=None):
    def kernel(code_ref, k_ref, w_ref, *refs):
        rest = refs[9:]
        out, buf, sem = rest[-3:]
        columns = pl.ds(c * 512, 512)
        v_ref, q0_ref, q1_ref = refs[0:3]
        options = [
            (0, lambda j: v_ref.at[_rows(j), columns], None),
            (1, lambda j: q0_ref.at[_rows(j % 4)], 0),
            (1, lambda j: q1_ref.at[_rows(j % 4)], 1),
        ]
        options += [(2 + i, lambda s, i=i: refs[3 + i].at[s, :, columns], None) for i in range(3)]
        options += [(5 + i, lambda s, i=i: refs[6 + i].at[s], None) for i in range(3)]
        for n in range(16):
            _fetch(code_ref[n], options, buf.at[n], sem.at[n])
        k = k_ref[0]
        for g in range(8):
            w = jnp.concatenate([w_ref[g, 0], w_ref[g, 1]], axis=1)
            _wait(buf.at[2 * g], sem.at[2 * g])
            _wait(buf.at[2 * g + 1], sem.at[2 * g + 1])
            product = _dot3(w, jnp.concatenate([buf[2 * g], buf[2 * g + 1]], axis=0), ((1,), (0,)))
            here = slice(g * B, (g + 1) * B)
            if tail is None:
                out[here] = product
                continue
            half, share, part = g // 4, (g % 4) // 2, slice((g % 2) * B, (g % 2 + 1) * B)

            def finish(beta_ref, product=product, here=here, part=part):
                for n in range(2):
                    there = slice(n * 512, (n + 1) * 512)
                    alpha = product if n == c else rest[0][here]
                    out[here, there] = alpha + beta_ref[part, there]

            @pl.when(k == share)
            def _(half=half, finish=finish):
                finish(rest[1 + half])

            @pl.when(k != share)
            def _(half=half, finish=finish):
                finish(rest[3 + half])

    extra = [] if tail is None else [tail[0], *tail[1], *tail[2]]
    return pl.pallas_call(
        kernel,
        out_shape=_f32(1024, 512 if tail is None else 1024),
        in_specs=[SMEM, SMEM, VMEM] + [ANY] * 9 + [VMEM] * len(extra),
        out_specs=VMEM,
        scratch_shapes=[pltpu.VMEM((16, B, 512), jnp.float32), pltpu.SemaphoreType.DMA((16,))],
        compiler_params=_params(),
        cost_estimate=_cost((7 if tail is None else 15) * 2**20, 3 * 16 * 2 * B * B * 512),
    )(codes, _core(), values, v, q0, q1, *own, *late, *extra)


def sigma_here(first, second, v, alpha_values, beta_values, alpha, beta):
    alpha_own, alpha_late, alpha_code = alpha
    beta_early, beta_late, beta_code = beta

    quadrants = [(0, 0), (1, 0), (0, 1), (1, 1)]
    (half,) = _pick(
        [(2, 256, 1024)],
        [v],
        lambda ins, k: [(ins[0].at[_my_rows(r, 1 - k)], 0, r) for r in range(2)],
    )
    x0 = _send(half, TO_CORE)
    pieces = _pick(
        [(512, 512)] * 4,
        [v],
        lambda ins, k: [
            (ins[0].at[r * 512 : (r + 1) * 512, c * 512 : (c + 1) * 512], n, None)
            for n, (r, c) in enumerate(quadrants)
        ],
    )
    zl = {(r, c): _send(piece, TO_ZL) for (r, c), piece in zip(quadrants, pieces)}
    other_values = _send(beta_values, TO_CORE)

    out = _gather(
        alpha_own, (B, 1024), 3, [v], lambda ins, k: [(0, lambda j: ins[0].at[_rows(j)], None)]
    )
    own = _send_all(out, TO_X)

    def early_options(ins, k):
        def of_v(j):
            return ins[0].at[:, _half_rows(k), _rows(j)]

        return [(0, of_v, None), (1, lambda j: ins[1].at[:, :, _rows(j)], None)]

    out = _gather(beta_early, (2, 256, B), first, [v.reshape(2, 512, 1024), x0], early_options)
    early = _send_all(out, TO_Y)

    zh = {(r, c): _send(zl[(r, c)], TO_ZNEXT) for r, c in quadrants}

    x1, late, x_late = {}, {}, {}
    for r in range(2):
        (half,) = _pick(
            [(2, 256, 512)],
            [zl[(r, 0)], zl[(r, 1)]],
            lambda ins, k: [(ins[c].at[_half_rows(1 - k)], 0, c) for c in range(2)],
        )
        x1[r] = _send(half, TO_CORE)
    for n in range(2):
        out = _gather(
            alpha_late,
            (B, 512),
            3,
            [zh[(0, n)], zh[(1, n)]],
            lambda ins, k: [(0, lambda j, i=i: ins[i].at[_rows(j % 4)], i) for i in range(2)],
        )
        x_late[n] = _send_all(out, TO_X)
        out = _gather(
            beta_late,
            (256, B),
            second,
            [v, x0, zl[(n, 0)], zl[(n, 1)], x1[n]],
            lambda ins, k, n=n: _near(n, k, *ins),
        )
        late[n] = _send_all(out, TO_Y)

    ours, theirs = [], []
    for r in range(2):
        a, b = beta_product(
            r, beta_code, beta_values, other_values, v, x0, zl[(r, 0)], zl[(r, 1)], x1[r], early, late[r]
        )
        ours.append(a)
        theirs.append(_send(b, TO_CORE))
    part = alpha_product(0, alpha_code, alpha_values, v, zh[(0, 0)], zh[(1, 0)], own, x_late[0])
    return alpha_product(
        1, alpha_code, alpha_values, v, zh[(0, 1)], zh[(1, 1)], own, x_late[1], (part, ours, theirs)
    )


def per_device(vector, links_alpha, alpha_values, links_beta, beta_values):
    row, col = lax.axis_index("row"), lax.axis_index("col")
    x, zh = row // NZH, row % NZH
    zl, y, k = col // (NY * NK), (col // NK) % NY, col % NK
    alpha = alpha_tables(links_alpha, x, zh)
    *beta, _ = beta_tables(links_beta, zl, y, k, 8, 8)
    return sigma_here(8, 8, vector, alpha_values, beta_values, alpha, beta)


def solution(mesh):
    placed = (P("row", "col"), P(), P("row", None, None, None), P(), P("col", None, None, None))
    return jax.shard_map(per_device, mesh=mesh, in_specs=placed, out_specs=P("row", "col"), check_vma=False)
```

time: 498 us -> 427 us (0.86)
  the two profiles are of different devices: /device:TPU:9 before, /device:TPU:1 now
where the time goes in v1:
time: 427 us; the launch traced here: 426 us
  waiting for transfers between devices  290 us (68%)
  Pallas kernels  74.6 us (17%)
  starting transfers between devices  53.6 us (13%)
  local copies, waits for them, and re-layouts  4.79 us (1%)
    ppermute x32, waiting for transfers between devices, _send(): return lax.ppermute(value, AXES, pairs)  290 us
    ppermute x32, starting transfers between devices, _send(): return lax.ppermute(value, AXES, pairs)  53.6 us
    pallas_call x6, Pallas kernels, _gather(): pl.pallas_call(kernel, out_shape=[_f32(slots, *slot_shape)] * 3, in_specs...  30.2 us
    pallas_call x2, Pallas kernels, beta_product(): pl.pallas_call(kernel, out_shape=[_f32(256, 1024)] * 2, in_specs=[SMEM, S...  19 us
    pallas_call x2, Pallas kernels, alpha_product(): pl.pallas_call(kernel, out_shape=_f32(1024, 512 if tail is None else 1024...  15.1 us
    pallas_call x4, Pallas kernels, _pick(): pl.pallas_call(kernel, out_shape=[_f32(*shape) for shape in shapes], in_s...  10.2 us
  transfers between devices with their start and end apart: 32, of which 13 were waited for; matrix products, arithmetic and copies ran while one was open for 2% of the time, Pallas kernels for 15%

profile of v1, /device:TPU:1, one launch (start us, length us, event | category | flops | bytes accessed | tf_op | source)
XLA Modules:
  0.0 426.3 jit_solution(4816982188544419780)
XLA Ops:
  0.0 3.3 shard_map.55
  3.3 2.5 collective-permute-start.12
  6.0 2.6 shard_map.60
  8.6 1.0 collective-permute-start.18
  9.6 1.6 collective-permute-start
  12.6 16.4 %collective-permute-done.12.refs_0_.refs_2_ = f32[512,512]{1,0:T(8,128)} collective-permute-done((f32[512,512]{1,0:T(8,128)}, f32[512,512]{1,0:T(8,128)}, u32[]{:S(2)}, u32[]{:S(2)}) %collective-permute-start.12) | collective-permute-done | bytes 1048608 | tf_op jit(solution)/shard_map/ppermute | solution.py:44
  29.0 2.1 collective-permute-start.17
  31.4 20.1 %collective-permute-done.2.refs_1_.refs_3_ = f32[512,512]{1,0:T(8,128)} collective-permute-done((f32[512,512]{1,0:T(8,128)}, f32[512,512]{1,0:T(8,128)}, u32[]{:S(2)}, u32[]{:S(2)}) %collective-permute-start.2) | collective-permute-done | bytes 1048608 | tf_op jit(solution)/shard_map/ppermute | solution.py:44
  51.5 2.1 shard_map.65
  53.6 2.2 collective-permute-start.26
  56.5 5.1 %shard_map.56 = (f32[3,128,1024]{2,1,0:T(8,128)}, f32[3,128,1024]{2,1,0:T(8,128)}, f32[3,128,1024]{2,1,0:T(8,128)}) custom-call(s32[9]{0:T(128)} %reshape_squeeze.6.code_ref, s32[1]{0:T(128)} %bitcast.3.k_ref, f32[1024,1024]{1,0:T(8,128)} %refs_0_.17), custom_call_target="tpu_custom_call" | custom-call | bytes 9437184 | tf_op jit(solution)/shard_map/pallas_call | solution.py:190
  61.9 12.1 %collective-permute-done.refs_1_.refs_3_ = f32[512,512]{1,0:T(8,128)} collective-permute-done((f32[512,512]{1,0:T(8,128)}, f32[512,512]{1,0:T(8,128)}, u32[]{:S(2)}, u32[]{:S(2)}) %collective-permute-start) | collective-permute-done | bytes 1048608 | tf_op jit(solution)/shard_map/ppermute | solution.py:44
  74.0 1.1 collective-permute-start.4
  75.1 21.4 %collective-permute-done.10.refs_0_.refs_2_ = f32[512,512]{1,0:T(8,128)} collective-permute-done((f32[512,512]{1,0:T(8,128)}, f32[512,512]{1,0:T(8,128)}, u32[]{:S(2)}, u32[]{:S(2)}) %collective-permute-start.10) | collective-permute-done | bytes 1048608 | tf_op jit(solution)/shard_map/ppermute | solution.py:44
  96.4 2.6 collective-permute-start.5
  99.3 2.2 shard_map.61
  101.5 1.7 collective-permute-start.19
  103.5 0.9 collective-permute-start.6
  104.7 3.7 collective-permute-start.11
  109.1 5.6 %shard_map.66 = (f32[8,256,128]{2,1,0:T(8,128)}, f32[8,256,128]{2,1,0:T(8,128)}, f32[8,256,128]{2,1,0:T(8,128)}) custom-call(s32[24]{0:T(128)} %reshape.276.code_ref, s32[1]{0:T(128)} %bitcast.3.k_ref, f32[1024,1024]{1,0:T(8,128)} %refs_0_.17, f32[2,256,1024]{2,1,0:T(8,128)} %collective-permute-done.18.refs_1_, ...), custom_call_target="tpu_custom_call" | custom-call | bytes 6291456 | tf_op jit(solution)/shard_map/pallas_call | solution.py:190
  114.8 28.9 %collective-permute-done.5.refs_4_ = f32[3,128,1024]{2,1,0:T(8,128)} collective-permute-done((f32[3,128,1024]{2,1,0:T(8,128)}, f32[3,128,1024]{2,1,0:T(8,128)}, u32[]{:S(2)}, u32[]{:S(2)}) %collective-permute-start.5) | collective-permute-done | bytes 1572896 | tf_op jit(solution)/shard_map/ppermute | solution.py:44
  143.7 1.3 collective-permute-start.27
  145.0 2.6 collective-permute-start.28
  147.7 5.0 %shard_map.63 = (f32[8,256,128]{2,1,0:T(8,128)}, f32[8,256,128]{2,1,0:T(8,128)}, f32[8,256,128]{2,1,0:T(8,128)}) custom-call(s32[24]{0:T(128)} %reshape.276.code_ref, s32[1]{0:T(128)} %bitcast.3.k_ref, f32[1024,1024]{1,0:T(8,128)} %refs_0_.17, f32[2,256,1024]{2,1,0:T(8,128)} %collective-permute-done.18.refs_1_, ...), custom_call_target="tpu_custom_call" | custom-call | bytes 6291456 | tf_op jit(solution)/shard_map/pallas_call | solution.py:190
  152.7 14.6 %collective-permute-done.6.refs_5_ = f32[3,128,1024]{2,1,0:T(8,128)} collective-permute-done((f32[3,128,1024]{2,1,0:T(8,128)}, f32[3,128,1024]{2,1,0:T(8,128)}, u32[]{:S(2)}, u32[]{:S(2)}) %collective-permute-start.6) | collective-permute-done | bytes 1572896 | tf_op jit(solution)/shard_map/ppermute | solution.py:44
  167.3 2.7 collective-permute-start.29
  170.7 6.3 %shard_map.62 = (f32[8,2,256,128]{3,2,1,0:T(8,128)}, f32[8,2,256,128]{3,2,1,0:T(8,128)}, f32[8,2,256,128]{3,2,1,0:T(8,128)}) custom-call(s32[24]{0:T(128)} %reshape.274.code_ref, s32[1]{0:T(128)} %bitcast.3.k_ref, f32[2,512,1024]{2,1,0:T(8,128)} %bitcast.43, f32[2,256,1024]{2,1,0:T(8,128)} %collective-permute-done.18.refs_1_), custom_call_target="tpu_custom_call" | custom-call | bytes 12582912 | tf_op jit(solution)/shard_map/pallas_call | solution.py:190
  177.2 4.0 collective-permute-start.21
  181.2 9.4 %collective-permute-done.28.refs_9_ = f32[8,256,128]{2,1,0:T(8,128)} collective-permute-done((f32[8,256,128]{2,1,0:T(8,128)}, f32[8,256,128]{2,1,0:T(8,128)}, u32[]{:S(2)}, u32[]{:S(2)}) %collective-permute-start.28) | collective-permute-done | bytes 1048608 | tf_op jit(solution)/shard_map/ppermute | solution.py:44
  190.6 1.8 collective-permute-done.29.refs_10_
  192.3 2.9 collective-permute-start.24
  195.2 20.3 %collective-permute-done.23.refs_8_ = f32[8,256,128]{2,1,0:T(8,128)} collective-permute-done((f32[8,256,128]{2,1,0:T(8,128)}, f32[8,256,128]{2,1,0:T(8,128)}, u32[]{:S(2)}, u32[]{:S(2)}) %collective-permute-start.23) | collective-permute-done | bytes 1048608 | tf_op jit(solution)/shard_map/ppermute | solution.py:44
  215.5 109.9 %collective-permute-done.24.refs_9_ = f32[8,256,128]{2,1,0:T(8,128)} collective-permute-done((f32[8,256,128]{2,1,0:T(8,128)}, f32[8,256,128]{2,1,0:T(8,128)}, u32[]{:S(2)}, u32[]{:S(2)}) %collective-permute-start.24) | collective-permute-done | bytes 1048608 | tf_op jit(solution)/shard_map/ppermute | solution.py:44
  325.4 2.7 collective-permute-start.1
  328.1 1.9 collective-permute-start.3
  331.0 4.0 shard_map.58
  335.0 2.9 collective-permute-start.14
  338.0 2.5 collective-permute-start.15
  341.3 9.6 %shard_map.67 = (f32[256,1024]{1,0:T(8,128)}, f32[256,1024]{1,0:T(8,128)}) custom-call(s32[32]{0:T(128)} %reshape.272.code_ref, s32[1]{0:T(128)} %bitcast.3.k_ref, f32[8,2,128,128]{3,2,1,0:T(8,128)} %mine_ref.3, f32[8,2,128,128]{3,2,1,0:T(8,128)} %collective-permute-done.17.other_ref, f32[1024,1024]{1,0:T(8,128)} %refs_0_.17, ...), custom_call_target="tpu_custom_call" | custom-call | flops 805306368 | bytes 8388608 | tf_op jit(solution)/shard_map/pallas_call | solution.py:292
  350.8 9.5 %shard_map.64 = (f32[256,1024]{1,0:T(8,128)}, f32[256,1024]{1,0:T(8,128)}) custom-call(s32[32]{0:T(128)} %reshape.272.code_ref, s32[1]{0:T(128)} %bitcast.3.k_ref, f32[8,2,128,128]{3,2,1,0:T(8,128)} %mine_ref.3, f32[8,2,128,128]{3,2,1,0:T(8,128)} %collective-permute-done.17.other_ref, f32[1024,1024]{1,0:T(8,128)} %refs_0_.17, ...), custom_call_target="tpu_custom_call" | custom-call | flops 805306368 | bytes 8388608 | tf_op jit(solution)/shard_map/pallas_call | solution.py:292
  360.3 2.2 collective-permute-start.31
  362.6 7.5 %collective-permute-done.3.refs_1_.refs_2_ = f32[512,512]{1,0:T(8,128)} collective-permute-done((f32[512,512]{1,0:T(8,128)}, f32[512,512]{1,0:T(8,128)}, u32[]{:S(2)}, u32[]{:S(2)}) %collective-permute-start.3) | collective-permute-done | bytes 1048608 | tf_op jit(solution)/shard_map/ppermute | solution.py:44
  370.0 4.9 %collective-permute-start.30 = (f32[256,1024]{1,0:T(8,128)}, f32[256,1024]{1,0:T(8,128)}, u32[]{:S(2)}, u32[]{:S(2)}) collective-permute-start(f32[256,1024]{1,0:T(8,128)} %get-tuple-element.55), channel_id=1, source_target_pairs={{0,1},{1,0},{2,3},{3,2},{4,5},{5,4},{6,7},{7,6},{8,9},{9,8},{10,11... | collective-permute-start | bytes 3145736 | tf_op jit(solution)/shard_map/ppermute | solution.py:44
  375.0 4.2 shard_map.57
  379.7 2.6 collective-permute-start.9
  383.1 6.1 %shard_map.59.refs_9_ = f32[1024,512]{1,0:T(8,128)} custom-call(s32[16]{0:T(128)} %fusion.19.code_ref, s32[1]{0:T(128)} %bitcast.3.k_ref, f32[8,2,128,128]{3,2,1,0:T(8,128)} %w_ref.3, f32[1024,1024]{1,0:T(8,128)} %refs_0_.17, f32[512,512]{1,0:T(8,128)} %collective-permute-done.11.refs_0_.refs_1_, f32[512,512]{1,0:T(8,128)} %collective-permute-done.13.refs_1_.refs_2_, ...), custom_call_target="tpu_custom_call" | custom-call | flops 805306368 | bytes 7340032 | tf_op jit(solution)/shard_map/pallas_call | solution.py:345
  389.3 27.5 %collective-permute-done.7.refs_6_ = f32[3,128,512]{2,1,0:T(8,128)} collective-permute-done((f32[3,128,512]{2,1,0:T(8,128)}, f32[3,128,512]{2,1,0:T(8,128)}, u32[]{:S(2)}, u32[]{:S(2)}) %collective-permute-start.7) | collective-permute-done | bytes 786464 | tf_op jit(solution)/shard_map/ppermute | solution.py:44
  417.1 9.0 %shard_map.68 = f32[1024,1024]{1,0:T(8,128)} custom-call(s32[16]{0:T(128)} %fusion.19.code_ref, s32[1]{0:T(128)} %bitcast.3.k_ref, f32[8,2,128,128]{3,2,1,0:T(8,128)} %w_ref.3, f32[1024,1024]{1,0:T(8,128)} %refs_0_.17, f32[512,512]{1,0:T(8,128)} %collective-permute-done.1.refs_0_.refs_1_, f32[512,512]{1,0:T(8,128)} %collective-permute-done.3.refs_1_.refs_2_, ...), custom_call_target="tpu_custom_call" | custom-call | flops 805306368 | bytes 15728640 | tf_op jit(solution)/shard_map/pallas_call | solution.py:345
  (98 shorter events, 8.5 us)
Async XLA Ops:
  3.3 25.7 %collective-permute-start.12 = (f32[512,512]{1,0:T(8,128)}, f32[512,512]{1,0:T(8,128)}, u32[]{:S(2)}, u32[]{:S(2)}) collective-permute-start(f32[512,512]{1,0:T(8,128)} %get-tuple-element.40), channel_id=1, source_target_pairs={{0,8},{1,9},{2,10},{3,11},{4,12},{5,13},{6,14},{7,15},{8,0},{9,1},... | collective-permute-start | bytes 3145736 | tf_op jit(solution)/shard_map/ppermute | solution.py:44
  5.9 5.4 %copy-start.1 = (s32[128,2]{0,1:T(2,128)S(1)}, s32[128,2]{0,1:T(2,128)}, u32[]{:S(2)}) copy-start(s32[128,2]{0,1:T(2,128)} %param.8) | copy-start | bytes 3076
  5.9 5.6 %copy-start.2 = (s32[64,2]{0,1:T(2,128)S(1)}, s32[64,2]{0,1:T(2,128)}, u32[]{:S(2)}) copy-start(s32[64,2]{0,1:T(2,128)} %param.6) | copy-start | bytes 1540
  5.9 45.6 %collective-permute-start.2 = (f32[512,512]{1,0:T(8,128)}, f32[512,512]{1,0:T(8,128)}, u32[]{:S(2)}, u32[]{:S(2)}) collective-permute-start(f32[512,512]{1,0:T(8,128)} %get-tuple-element.32), channel_id=1, source_target_pairs={{0,8},{1,9},{2,10},{3,11},{4,12},{5,13},{6,14},{7,15},{8,0},{9,1},... | collective-permute-start | bytes 3145736 | tf_op jit(solution)/shard_map/ppermute | solution.py:44
  8.6 96.1 %collective-permute-start.18 = (f32[2,256,1024]{2,1,0:T(8,128)}, f32[2,256,1024]{2,1,0:T(8,128)}, u32[]{:S(2)}, u32[]{:S(2)}) collective-permute-start(f32[2,256,1024]{2,1,0:T(8,128)} %shard_map.60), channel_id=1, source_target_pairs={{0,1},{1,0},{2,3},{3,2},{4,5},{5,4},{6,7},{7,6},{8,9},{9,8},{10,11... | collective-permute-start | bytes 6291464 | tf_op jit(solution)/shard_map/ppermute | solution.py:44
  9.6 64.4 %collective-permute-start = (f32[512,512]{1,0:T(8,128)}, f32[512,512]{1,0:T(8,128)}, u32[]{:S(2)}, u32[]{:S(2)}) collective-permute-start(f32[512,512]{1,0:T(8,128)} %get-tuple-element.31), channel_id=1, source_target_pairs={{0,8},{1,9},{2,10},{3,11},{4,12},{5,13},{6,14},{7,15},{8,0},{9,1},... | collective-permute-start | bytes 3145736 | tf_op jit(solution)/shard_map/ppermute | solution.py:44
  11.3 85.2 %collective-permute-start.10 = (f32[512,512]{1,0:T(8,128)}, f32[512,512]{1,0:T(8,128)}, u32[]{:S(2)}, u32[]{:S(2)}) collective-permute-start(f32[512,512]{1,0:T(8,128)} %get-tuple-element.39), channel_id=1, source_target_pairs={{0,8},{1,9},{2,10},{3,11},{4,12},{5,13},{6,14},{7,15},{8,0},{9,1},... | collective-permute-start | bytes 3145736 | tf_op jit(solution)/shard_map/ppermute | solution.py:44
  29.0 72.5 %collective-permute-start.17 = (f32[8,2,128,128]{3,2,1,0:T(8,128)}, f32[8,2,128,128]{3,2,1,0:T(8,128)}, u32[]{:S(2)}, u32[]{:S(2)}) collective-permute-start(f32[8,2,128,128]{3,2,1,0:T(8,128)} %mine_ref.3), channel_id=1, source_target_pairs={{0,1},{1,0},{2,3},{3,2},{4,5},{5,4},{6,7},{7,6},{8,9},{9,8},{10,11... | collective-permute-start | bytes 3145736 | tf_op jit(solution)/shard_map/ppermute | solution.py:44
  53.6 49.9 %collective-permute-start.26 = (f32[2,256,512]{2,1,0:T(8,128)}, f32[2,256,512]{2,1,0:T(8,128)}, u32[]{:S(2)}, u32[]{:S(2)}) collective-permute-start(f32[2,256,512]{2,1,0:T(8,128)} %shard_map.65), channel_id=1, source_target_pairs={{0,1},{1,0},{2,3},{3,2},{4,5},{5,4},{6,7},{7,6},{8,9},{9,8},{10,11... | collective-permute-start | bytes 3145736 | tf_op jit(solution)/shard_map/ppermute | solution.py:44
  74.0 40.7 %collective-permute-start.4 = (f32[3,128,1024]{2,1,0:T(8,128)}, f32[3,128,1024]{2,1,0:T(8,128)}, u32[]{:S(2)}, u32[]{:S(2)}) collective-permute-start(f32[3,128,1024]{2,1,0:T(8,128)} %get-tuple-element.33), channel_id=1, source_target_pairs={{0,32},{1,33},{2,34},{3,35},{4,36},{5,37},{6,38},{7,39},{8,40},{9,... | collective-permute-start | bytes 4718600 | tf_op jit(solution)/shard_map/ppermute | solution.py:44
  96.4 47.3 %collective-permute-start.5 = (f32[3,128,1024]{2,1,0:T(8,128)}, f32[3,128,1024]{2,1,0:T(8,128)}, u32[]{:S(2)}, u32[]{:S(2)}) collective-permute-start(f32[3,128,1024]{2,1,0:T(8,128)} %get-tuple-element.34), channel_id=1, source_target_pairs={{0,64},{1,65},{2,66},{3,67},{4,68},{5,69},{6,70},{7,71},{8,72},{9,... | collective-permute-start | bytes 4718600 | tf_op jit(solution)/shard_map/ppermute | solution.py:44
  101.5 43.5 %collective-permute-start.19 = (f32[2,256,512]{2,1,0:T(8,128)}, f32[2,256,512]{2,1,0:T(8,128)}, u32[]{:S(2)}, u32[]{:S(2)}) collective-permute-start(f32[2,256,512]{2,1,0:T(8,128)} %shard_map.61), channel_id=1, source_target_pairs={{0,1},{1,0},{2,3},{3,2},{4,5},{5,4},{6,7},{7,6},{8,9},{9,8},{10,11... | collective-permute-start | bytes 3145736 | tf_op jit(solution)/shard_map/ppermute | solution.py:44
  103.5 63.8 %collective-permute-start.6 = (f32[3,128,1024]{2,1,0:T(8,128)}, f32[3,128,1024]{2,1,0:T(8,128)}, u32[]{:S(2)}, u32[]{:S(2)}) collective-permute-start(f32[3,128,1024]{2,1,0:T(8,128)} %get-tuple-element.35), channel_id=1, source_target_pairs={{0,96},{1,97},{2,98},{3,99},{4,100},{5,101},{6,102},{7,103},{8,104... | collective-permute-start | bytes 4718600 | tf_op jit(solution)/shard_map/ppermute | solution.py:44
  104.7 65.3 %collective-permute-start.11 = (f32[512,512]{1,0:T(8,128)}, f32[512,512]{1,0:T(8,128)}, u32[]{:S(2)}, u32[]{:S(2)}) collective-permute-start(f32[512,512]{1,0:T(8,128)} %collective-permute-done.10.refs_0_.refs_2_), channel_id=1, source_target_pairs={{0,24},{1,25},{2,26},{3,27},{4,28},{5,29},{6,30},{7,31},{8,16},{9,... | collective-permute-start | bytes 3145736 | tf_op jit(solution)/shard_map/ppermute | solution.py:44
  114.7 62.4 %collective-permute-start.13 = (f32[512,512]{1,0:T(8,128)}, f32[512,512]{1,0:T(8,128)}, u32[]{:S(2)}, u32[]{:S(2)}) collective-permute-start(f32[512,512]{1,0:T(8,128)} %collective-permute-done.12.refs_0_.refs_2_), channel_id=1, source_target_pairs={{0,24},{1,25},{2,26},{3,27},{4,28},{5,29},{6,30},{7,31},{8,16},{9,... | collective-permute-start | bytes 3145736 | tf_op jit(solution)/shard_map/ppermute | solution.py:44
  143.7 33.4 %collective-permute-start.27 = (f32[8,256,128]{2,1,0:T(8,128)}, f32[8,256,128]{2,1,0:T(8,128)}, u32[]{:S(2)}, u32[]{:S(2)}) collective-permute-start(f32[8,256,128]{2,1,0:T(8,128)} %get-tuple-element.51), channel_id=1, source_target_pairs={{0,2},{1,3},{2,4},{3,5},{4,6},{5,7},{6,0},{7,1},{8,10},{9,11},{10,... | collective-permute-start | bytes 3145736 | tf_op jit(solution)/shard_map/ppermute | solution.py:44
  145.0 45.5 %collective-permute-start.28 = (f32[8,256,128]{2,1,0:T(8,128)}, f32[8,256,128]{2,1,0:T(8,128)}, u32[]{:S(2)}, u32[]{:S(2)}) collective-permute-start(f32[8,256,128]{2,1,0:T(8,128)} %get-tuple-element.52), channel_id=1, source_target_pairs={{0,4},{1,5},{2,6},{3,7},{4,0},{5,1},{6,2},{7,3},{8,12},{9,13},{10,... | collective-permute-start | bytes 3145736 | tf_op jit(solution)/shard_map/ppermute | solution.py:44
  167.3 25.0 %collective-permute-start.29 = (f32[8,256,128]{2,1,0:T(8,128)}, f32[8,256,128]{2,1,0:T(8,128)}, u32[]{:S(2)}, u32[]{:S(2)}) collective-permute-start(f32[8,256,128]{2,1,0:T(8,128)} %get-tuple-element.53), channel_id=1, source_target_pairs={{0,6},{1,7},{2,0},{3,1},{4,2},{5,3},{6,4},{7,5},{8,14},{9,15},{10,... | collective-permute-start | bytes 3145736 | tf_op jit(solution)/shard_map/ppermute | solution.py:44
  170.0 45.5 %collective-permute-start.23 = (f32[8,256,128]{2,1,0:T(8,128)}, f32[8,256,128]{2,1,0:T(8,128)}, u32[]{:S(2)}, u32[]{:S(2)}) collective-permute-start(f32[8,256,128]{2,1,0:T(8,128)} %get-tuple-element.47), channel_id=1, source_target_pairs={{0,2},{1,3},{2,4},{3,5},{4,6},{5,7},{6,0},{7,1},{8,10},{9,11},{10,... | collective-permute-start | bytes 3145736 | tf_op jit(solution)/shard_map/ppermute | solution.py:44
  177.1 157.9 %collective-permute-start.20 = (f32[8,2,256,128]{3,2,1,0:T(8,128)}, f32[8,2,256,128]{3,2,1,0:T(8,128)}, u32[]{:S(2)}, u32[]{:S(2)}) collective-permute-start(f32[8,2,256,128]{3,2,1,0:T(8,128)} %get-tuple-element.44), channel_id=1, source_target_pairs={{0,2},{1,3},{2,4},{3,5},{4,6},{5,7},{6,0},{7,1},{8,10},{9,11},{10,... | collective-permute-start | bytes 6291464 | tf_op jit(solution)/shard_map/ppermute | solution.py:44
  177.2 160.8 %collective-permute-start.21 = (f32[8,2,256,128]{3,2,1,0:T(8,128)}, f32[8,2,256,128]{3,2,1,0:T(8,128)}, u32[]{:S(2)}, u32[]{:S(2)}) collective-permute-start(f32[8,2,256,128]{3,2,1,0:T(8,128)} %get-tuple-element.45), channel_id=1, source_target_pairs={{0,4},{1,5},{2,6},{3,7},{4,0},{5,1},{6,2},{7,3},{8,12},{9,13},{10,... | collective-permute-start | bytes 6291464 | tf_op jit(solution)/shard_map/ppermute | solution.py:44
  190.6 149.9 %collective-permute-start.22 = (f32[8,2,256,128]{3,2,1,0:T(8,128)}, f32[8,2,256,128]{3,2,1,0:T(8,128)}, u32[]{:S(2)}, u32[]{:S(2)}) collective-permute-start(f32[8,2,256,128]{3,2,1,0:T(8,128)} %get-tuple-element.46), channel_id=1, source_target_pairs={{0,6},{1,7},{2,0},{3,1},{4,2},{5,3},{6,4},{7,5},{8,14},{9,15},{10,... | collective-permute-start | bytes 6291464 | tf_op jit(solution)/shard_map/ppermute | solution.py:44
  192.3 133.1 %collective-permute-start.24 = (f32[8,256,128]{2,1,0:T(8,128)}, f32[8,256,128]{2,1,0:T(8,128)}, u32[]{:S(2)}, u32[]{:S(2)}) collective-permute-start(f32[8,256,128]{2,1,0:T(8,128)} %get-tuple-element.48), channel_id=1, source_target_pairs={{0,4},{1,5},{2,6},{3,7},{4,0},{5,1},{6,2},{7,3},{8,12},{9,13},{10,... | collective-permute-start | bytes 3145736 | tf_op jit(solution)/shard_map/ppermute | solution.py:44
  215.5 112.6 %collective-permute-start.25 = (f32[8,256,128]{2,1,0:T(8,128)}, f32[8,256,128]{2,1,0:T(8,128)}, u32[]{:S(2)}, u32[]{:S(2)}) collective-permute-start(f32[8,256,128]{2,1,0:T(8,128)} %get-tuple-element.49), channel_id=1, source_target_pairs={{0,6},{1,7},{2,0},{3,1},{4,2},{5,3},{6,4},{7,5},{8,14},{9,15},{10,... | collective-permute-start | bytes 3145736 | tf_op jit(solution)/shard_map/ppermute | solution.py:44
  325.4 34.9 %collective-permute-start.1 = (f32[512,512]{1,0:T(8,128)}, f32[512,512]{1,0:T(8,128)}, u32[]{:S(2)}, u32[]{:S(2)}) collective-permute-start(f32[512,512]{1,0:T(8,128)} %collective-permute-done.refs_1_.refs_3_), channel_id=1, source_target_pairs={{0,24},{1,25},{2,26},{3,27},{4,28},{5,29},{6,30},{7,31},{8,16},{9,... | collective-permute-start | bytes 3145736 | tf_op jit(solution)/shard_map/ppermute | solution.py:44
  328.1 41.9 %collective-permute-start.3 = (f32[512,512]{1,0:T(8,128)}, f32[512,512]{1,0:T(8,128)}, u32[]{:S(2)}, u32[]{:S(2)}) collective-permute-start(f32[512,512]{1,0:T(8,128)} %collective-permute-done.2.refs_1_.refs_3_), channel_id=1, source_target_pairs={{0,24},{1,25},{2,26},{3,27},{4,28},{5,29},{6,30},{7,31},{8,16},{9,... | collective-permute-start | bytes 3145736 | tf_op jit(solution)/shard_map/ppermute | solution.py:44
  335.0 44.2 %collective-permute-start.14 = (f32[3,128,512]{2,1,0:T(8,128)}, f32[3,128,512]{2,1,0:T(8,128)S(1)}, u32[]{:S(2)}, u32[]{:S(2)}) collective-permute-start(f32[3,128,512]{2,1,0:T(8,128)} %get-tuple-element.41), channel_id=1, source_target_pairs={{0,32},{1,33},{2,34},{3,35},{4,36},{5,37},{6,38},{7,39},{8,40},{9,... | collective-permute-start | bytes 2359304 | tf_op jit(solution)/shard_map/ppermute | solution.py:44
  338.0 41.3 %collective-permute-start.15 = (f32[3,128,512]{2,1,0:T(8,128)}, f32[3,128,512]{2,1,0:T(8,128)}, u32[]{:S(2)}, u32[]{:S(2)}) collective-permute-start(f32[3,128,512]{2,1,0:T(8,128)} %get-tuple-element.42), channel_id=1, source_target_pairs={{0,64},{1,65},{2,66},{3,67},{4,68},{5,69},{6,70},{7,71},{8,72},{9,... | collective-permute-start | bytes 2359304 | tf_op jit(solution)/shard_map/ppermute | solution.py:44
  340.4 39.3 %collective-permute-start.16 = (f32[3,128,512]{2,1,0:T(8,128)}, f32[3,128,512]{2,1,0:T(8,128)}, u32[]{:S(2)}, u32[]{:S(2)}) collective-permute-start(f32[3,128,512]{2,1,0:T(8,128)} %get-tuple-element.43), channel_id=1, source_target_pairs={{0,96},{1,97},{2,98},{3,99},{4,100},{5,101},{6,102},{7,103},{8,104... | collective-permute-start | bytes 2359304 | tf_op jit(solution)/shard_map/ppermute | solution.py:44
  360.3 56.8 %collective-permute-start.31 = (f32[256,1024]{1,0:T(8,128)}, f32[256,1024]{1,0:T(8,128)}, u32[]{:S(2)}, u32[]{:S(2)}) collective-permute-start(f32[256,1024]{1,0:T(8,128)} %get-tuple-element.56), channel_id=1, source_target_pairs={{0,1},{1,0},{2,3},{3,2},{4,5},{5,4},{6,7},{7,6},{8,9},{9,8},{10,11... | collective-permute-start | bytes 3145736 | tf_op jit(solution)/shard_map/ppermute | solution.py:44
  370.0 47.1 %collective-permute-start.30 = (f32[256,1024]{1,0:T(8,128)}, f32[256,1024]{1,0:T(8,128)}, u32[]{:S(2)}, u32[]{:S(2)}) collective-permute-start(f32[256,1024]{1,0:T(8,128)} %get-tuple-element.55), channel_id=1, source_target_pairs={{0,1},{1,0},{2,3},{3,2},{4,5},{5,4},{6,7},{7,6},{8,9},{9,8},{10,11... | collective-permute-start | bytes 3145736 | tf_op jit(solution)/shard_map/ppermute | solution.py:44
  379.2 3.9 copy-start
  379.2 37.5 %collective-permute-start.7 = (f32[3,128,512]{2,1,0:T(8,128)}, f32[3,128,512]{2,1,0:T(8,128)}, u32[]{:S(2)}, u32[]{:S(2)}) collective-permute-start(f32[3,128,512]{2,1,0:T(8,128)} %get-tuple-element.36), channel_id=1, source_target_pairs={{0,32},{1,33},{2,34},{3,35},{4,36},{5,37},{6,38},{7,39},{8,40},{9,... | collective-permute-start | bytes 2359304 | tf_op jit(solution)/shard_map/ppermute | solution.py:44
  379.3 37.5 %collective-permute-start.8 = (f32[3,128,512]{2,1,0:T(8,128)}, f32[3,128,512]{2,1,0:T(8,128)}, u32[]{:S(2)}, u32[]{:S(2)}) collective-permute-start(f32[3,128,512]{2,1,0:T(8,128)} %get-tuple-element.37), channel_id=1, source_target_pairs={{0,64},{1,65},{2,66},{3,67},{4,68},{5,69},{6,70},{7,71},{8,72},{9,... | collective-permute-start | bytes 2359304 | tf_op jit(solution)/shard_map/ppermute | solution.py:44
  379.7 37.4 %collective-permute-start.9 = (f32[3,128,512]{2,1,0:T(8,128)}, f32[3,128,512]{2,1,0:T(8,128)}, u32[]{:S(2)}, u32[]{:S(2)}) collective-permute-start(f32[3,128,512]{2,1,0:T(8,128)} %get-tuple-element.38), channel_id=1, source_target_pairs={{0,96},{1,97},{2,98},{3,99},{4,100},{5,101},{6,102},{7,103},{8,104... | collective-permute-start | bytes 2359304 | tf_op jit(solution)/shard_map/ppermute | solution.py:44

commit v2 on v1

--- a/solution.py
+++ b/solution.py
@@ -9,6 +9,7 @@
 B = 128
 AXES = ("row", "col")
 HOPS = (1, 2, 3)
+EARLY, LATE = 5, 7
 NX, NZH, NZL, NY, NK = 4, 2, 2, 4, 2
 
 
@@ -88,25 +89,25 @@
     return lists[:, 0].reshape(-1), lists[:, 1].reshape(-1), code.astype(jnp.int32)
 
 
-def beta_tables(links, zl, y, k, first, second):
+def beta_tables(links, zl, y, k):
     wanted = links.reshape(NZL * NY, 32)
     mask = _members(wanted, 128).reshape(NZL, NY, NZL, NY, 16)
     mask = jnp.stack([mask[0], mask[1][:, ::-1]], axis=0)
     mask = jnp.swapaxes(mask, 2, 3)
     rank = _ranks(mask)
     own_count = jnp.sum(mask[:, :, :, 0], axis=-1)
-    base = jnp.maximum(own_count, first)[..., None]
+    base = jnp.maximum(own_count, EARLY)[..., None]
     pos = jnp.stack([rank[:, :, :, 0], base + rank[:, :, :, 1]], axis=3)
     mask = mask.reshape(NZL, NY, NY, 32)
     pos = pos.reshape(NZL, NY, NY, 32)
     far = (jnp.arange(NY)[:, None] != jnp.arange(NY)[None, :]).astype(jnp.int32)
-    fits = jnp.max(mask * (pos + 1) * far[None, :, :, None]) <= first + second
+    fits = jnp.max(mask * (pos + 1) * far[None, :, :, None]) <= EARLY + LATE
     mask = lax.dynamic_index_in_dim(mask, zl, 0, keepdims=False)
     pos = lax.dynamic_index_in_dim(pos, zl, 0, keepdims=False)
     sent = _lists(
         lax.dynamic_index_in_dim(mask, y, 1, keepdims=False),
         lax.dynamic_index_in_dim(pos, y, 1, keepdims=False),
-        first + second,
+        16,
     )
     sent = jnp.roll(sent, -y, axis=0)[1:]
     core = (sent // 8) % 2
@@ -118,11 +119,12 @@
     key = (source_y * 2 + other) * 16 + block
     slot = jnp.sum((key[:, None] == jnp.arange(my_pos.size)) * my_pos, axis=1)
     hop = (y - source_y) % NY
-    late = (slot >= first).astype(jnp.int32)
+    late, extra = (slot >= EARLY).astype(jnp.int32), (slot >= EARLY + LATE).astype(jnp.int32)
     near = (other * 2 + jnp.abs(block // 8 - k)) * 32 + block % 8
-    code = jnp.where(hop == 0, near, (3 + hop + 3 * late) * 32 + slot - first * late)
+    code = jnp.where(hop == 0, near, (3 + hop + 3 * late + 3 * extra) * 32 + slot - EARLY * late - LATE * extra)
     code = jnp.roll(code.reshape(2, 16), -k, axis=0).reshape(-1)
-    return sent[:, :first].reshape(-1), sent[:, first:].reshape(-1), code.astype(jnp.int32), fits
+    lists = [part.reshape(-1) for part in jnp.split(sent, [EARLY, EARLY + LATE], axis=1)]
+    return (*lists, code.astype(jnp.int32), fits)
 
 
 def _rows(i):
@@ -173,16 +175,24 @@
         ins, outs = refs[: len(sources)], refs[len(sources) : len(sources) + 3]
         buf, in_sem, out_sem = refs[len(sources) + 3 :]
         options = options_of(ins, k_ref[0])
-        for s in range(count):
+
+        def load(s, _):
             _fetch(code_ref[s], options, buf.at[s], in_sem.at[s])
-        copies = []
-        for s in range(count):
-            _wait(buf.at[s], in_sem.at[s])
-            copy = pltpu.make_async_copy(buf.at[s], outs[s // slots].at[s % slots], out_sem.at[s])
-            copy.start()
-            copies.append(copy)
-        for copy in copies:
-            copy.wait()
+
+        lax.fori_loop(0, count, load, None)
+        for hop, out in enumerate(outs):
+
+            def store(s, _, hop=hop, out=out):
+                n = hop * slots + s
+                _wait(buf.at[n], in_sem.at[n])
+                pltpu.make_async_copy(buf.at[n], out.at[s], out_sem.at[n]).start()
+
+            lax.fori_loop(0, slots, store, None)
+
+        def finish(s, _):
+            _wait(buf.at[s], out_sem.at[s])
+
+        lax.fori_loop(0, count, finish, None)
 
     size = 4 * count
     for n in slot_shape:
@@ -273,31 +283,39 @@
     ]
 
 
-def beta_product(r, codes, mine, other, v, x0, q0, q1, x1, early, late):
+def beta_product(r, codes, mine, other, v, x0, q0, q1, x1, early, late, extra):
     def kernel(code_ref, k_ref, mine_ref, other_ref, *refs):
-        out_mine, out_other, buf, sem = refs[11:]
+        out_mine, out_other, buf, sem = refs[14:]
         options = _near(r, k_ref[0], *refs[0:5])
         options += [(4 + i, lambda s, i=i: refs[5 + i].at[s, r], None) for i in range(3)]
         options += [(7 + i, lambda s, i=i: refs[8 + i].at[s], None) for i in range(3)]
-        for n in range(32):
+        options += [(10 + i, lambda s, i=i: refs[11 + i].at[s, r], None) for i in range(3)]
+
+        def load(n, _):
             _fetch(code_ref[n], options, buf.at[n], sem.at[n])
-        for h in range(16):
-            w_ref, out = (mine_ref, out_mine) if h < 8 else (other_ref, out_other)
-            w = jnp.concatenate([w_ref[h % 8, 0], w_ref[h % 8, 1]], axis=1)
-            _wait(buf.at[2 * h], sem.at[2 * h])
-            _wait(buf.at[2 * h + 1], sem.at[2 * h + 1])
-            blocks = jnp.concatenate([buf[2 * h], buf[2 * h + 1]], axis=1)
-            out[:, (h % 8) * B : (h % 8 + 1) * B] = _dot3(blocks, w, ((1,), (1,)))
+
+        lax.fori_loop(0, 32, load, None)
+        for first, w_ref, out in ((0, mine_ref, out_mine), (16, other_ref, out_other)):
+
+            def block(h, _, first=first, w_ref=w_ref, out=out):
+                n = first + 2 * h
+                w = jnp.concatenate([w_ref[h, 0], w_ref[h, 1]], axis=1)
+                _wait(buf.at[n], sem.at[n])
+                _wait(buf.at[n + 1], sem.at[n + 1])
+                blocks = jnp.concatenate([buf[n], buf[n + 1]], axis=1)
+                out[:, _rows(h)] = _dot3(blocks, w, ((1,), (1,)))
+
+            lax.fori_loop(0, 8, block, None, unroll=2)
 
     return pl.pallas_call(
         kernel,
         out_shape=[_f32(256, 1024)] * 2,
-        in_specs=[SMEM, SMEM, VMEM, VMEM] + [ANY] * 11,
+        in_specs=[SMEM, SMEM, VMEM, VMEM] + [ANY] * 14,
         out_specs=[VMEM, VMEM],
         scratch_shapes=[pltpu.VMEM((32, 256, B), jnp.float32), pltpu.SemaphoreType.DMA((32,))],
         compiler_params=_params(),
         cost_estimate=_cost(8 * 2**20, 3 * 32 * 2 * 256 * B * B),
-    )(codes, _core(), mine, other, v, x0, q0, q1, x1, *early, *late)
+    )(codes, _core(), mine, other, v, x0, q0, q1, x1, *early, *late, *extra)
 
 
 def alpha_product(c, codes, values, v, q0, q1, own, late, tail=None):
@@ -313,8 +331,11 @@
         ]
         options += [(2 + i, lambda s, i=i: refs[3 + i].at[s, :, columns], None) for i in range(3)]
         options += [(5 + i, lambda s, i=i: refs[6 + i].at[s], None) for i in range(3)]
-        for n in range(16):
+
+        def load(n, _):
             _fetch(code_ref[n], options, buf.at[n], sem.at[n])
+
+        lax.fori_loop(0, 16, load, None)
         k = k_ref[0]
         for g in range(8):
             w = jnp.concatenate([w_ref[g, 0], w_ref[g, 1]], axis=1)
@@ -353,16 +374,12 @@
     )(codes, _core(), values, v, q0, q1, *own, *late, *extra)
 
 
-def sigma_here(first, second, v, alpha_values, beta_values, alpha, beta):
+def sigma_here(v, alpha_values, beta_values, alpha, beta):
     alpha_own, alpha_late, alpha_code = alpha
-    beta_early, beta_late, beta_code = beta
-
-    quadrants = [(0, 0), (1, 0), (0, 1), (1, 1)]
-    (half,) = _pick(
-        [(2, 256, 1024)],
-        [v],
-        lambda ins, k: [(ins[0].at[_my_rows(r, 1 - k)], 0, r) for r in range(2)],
-    )
+    beta_early, beta_late, beta_extra, beta_code, fits = beta
+
+    quadrants = [(0, 0), (0, 1), (1, 0), (1, 1)]
+    (half,) = _pick([(2, 256, 1024)], [v], lambda ins, k: [(ins[0].at[_my_rows(r, 1 - k)], 0, r) for r in range(2)])
     x0 = _send(half, TO_CORE)
     pieces = _pick(
         [(512, 512)] * 4,
@@ -375,9 +392,7 @@
     zl = {(r, c): _send(piece, TO_ZL) for (r, c), piece in zip(quadrants, pieces)}
     other_values = _send(beta_values, TO_CORE)
 
-    out = _gather(
-        alpha_own, (B, 1024), 3, [v], lambda ins, k: [(0, lambda j: ins[0].at[_rows(j)], None)]
-    )
+    out = _gather(alpha_own, (B, 1024), 3, [v], lambda ins, k: [(0, lambda j: ins[0].at[_rows(j)], None)])
     own = _send_all(out, TO_X)
 
     def early_options(ins, k):
@@ -386,7 +401,7 @@
 
         return [(0, of_v, None), (1, lambda j: ins[1].at[:, :, _rows(j)], None)]
 
-    out = _gather(beta_early, (2, 256, B), first, [v.reshape(2, 512, 1024), x0], early_options)
+    out = _gather(beta_early, (2, 256, B), EARLY, [v.reshape(2, 512, 1024), x0], early_options)
     early = _send_all(out, TO_Y)
 
     zh = {(r, c): _send(zl[(r, c)], TO_ZNEXT) for r, c in quadrants}
@@ -409,18 +424,33 @@
         )
         x_late[n] = _send_all(out, TO_X)
         out = _gather(
-            beta_late,
-            (256, B),
-            second,
-            [v, x0, zl[(n, 0)], zl[(n, 1)], x1[n]],
-            lambda ins, k, n=n: _near(n, k, *ins),
+            beta_late, (256, B), LATE, [v, x0, zl[(n, 0)], zl[(n, 1)], x1[n]], lambda ins, k, n=n: _near(n, k, *ins)
         )
         late[n] = _send_all(out, TO_Y)
+
+    def send_extra():
+        halves = []
+        for r in range(2):
+            halves.append(
+                _gather(
+                    beta_extra,
+                    (256, B),
+                    16 - EARLY - LATE,
+                    [v, x0, zl[(r, 0)], zl[(r, 1)], x1[r]],
+                    lambda ins, k, r=r: _near(r, k, *ins),
+                )
+            )
+        return tuple(_send_all([jnp.stack(pair, axis=1) for pair in zip(*halves)], TO_Y))
+
+    def skip_extra():
+        return tuple(jnp.zeros((16 - EARLY - LATE, 2, 256, B), jnp.float32) for _ in HOPS)
+
+    extra = lax.cond(fits, skip_extra, send_extra)
 
     ours, theirs = [], []
     for r in range(2):
         a, b = beta_product(
-            r, beta_code, beta_values, other_values, v, x0, zl[(r, 0)], zl[(r, 1)], x1[r], early, late[r]
+            r, beta_code, beta_values, other_values, v, x0, zl[(r, 0)], zl[(r, 1)], x1[r], early, late[r], extra
         )
         ours.append(a)
         theirs.append(_send(b, TO_CORE))
@@ -435,8 +465,8 @@
     x, zh = row // NZH, row % NZH
     zl, y, k = col // (NY * NK), (col // NK) % NY, col % NK
     alpha = alpha_tables(links_alpha, x, zh)
-    *beta, _ = beta_tables(links_beta, zl, y, k, 8, 8)
-    return sigma_here(8, 8, vector, alpha_values, beta_values, alpha, beta)
+    beta = beta_tables(links_beta, zl, y, k)
+    return sigma_here(vector, alpha_values, beta_values, alpha, beta)
 
 
 def solution(mesh):

time: 427 us -> 339 us (0.79)
  the two profiles are of different devices: /device:TPU:1 before, /device:TPU:9 now
where the time goes in v2:
time: 339 us; the launch traced here: 338 us
  waiting for transfers between devices  215 us (63%)
  Pallas kernels  72.8 us (21%)
  starting transfers between devices  37 us (11%)
  local copies, waits for them, and re-layouts  7.94 us (2%)
  other arithmetic  3.7 us (1%)
    ppermute x32, waiting for transfers between devices, _send(): return lax.ppermute(value, AXES, pairs)  215 us
    ppermute x32, starting transfers between devices, _send(): return lax.ppermute(value, AXES, pairs)  37 us
    pallas_call x6, Pallas kernels, _gather(): pl.pallas_call(kernel, out_shape=[_f32(slots, *slot_shape)] * 3, in_specs...  27.8 us
    pallas_call x2, Pallas kernels, beta_product(): pl.pallas_call(kernel, out_shape=[_f32(256, 1024)] * 2, in_specs=[SMEM, S...  19.7 us
    pallas_call x2, Pallas kernels, alpha_product(): pl.pallas_call(kernel, out_shape=_f32(1024, 512 if tail is None else 1024...  15.1 us
    pallas_call x4, Pallas kernels, _pick(): pl.pallas_call(kernel, out_shape=[_f32(*shape) for shape in shapes], in_s...  10.2 us
  transfers between devices with their start and end apart: 32, of which 16 were waited for; matrix products, arithmetic and copies ran while one was open for 3% of the time, Pallas kernels for 18%

profile of v2, /device:TPU:9, one launch (start us, length us, event | category | flops | bytes accessed | tf_op | source)
XLA Modules:
  0.0 337.8 jit_solution(1121494355121712467)
XLA Ops:
  0.0 3.4 shard_map.55
  3.4 1.7 collective-permute-start.15
  5.2 2.6 shard_map.60
  7.8 1.0 collective-permute-start.21
  8.9 1.6 collective-permute-start.13
  13.0 5.1 %shard_map.56 = (f32[3,128,1024]{2,1,0:T(8,128)}, f32[3,128,1024]{2,1,0:T(8,128)}, f32[3,128,1024]{2,1,0:T(8,128)}) custom-call(s32[9]{0:T(128)} %reshape_squeeze.6.code_ref, s32[1]{0:T(128)} %bitcast.10.k_ref, f32[1024,1024]{1,0:T(8,128)} %refs_0_.17), custom_call_target="tpu_custom_call" | custom-call | bytes 9437184 | tf_op jit(solution)/shard_map/pallas_call | solution.py:200
  19.1 9.1 %collective-permute-done.15.refs_0_.refs_2_ = f32[512,512]{1,0:T(8,128)} collective-permute-done((f32[512,512]{1,0:T(8,128)}, f32[512,512]{1,0:T(8,128)}, u32[]{:S(2)}, u32[]{:S(2)}) %collective-permute-start.15) | collective-permute-done | bytes 1048608 | tf_op jit(solution)/shard_map/ppermute | solution.py:45
  28.2 1.2 collective-permute-start.7
  29.4 21.3 %collective-permute-done.5.refs_1_.refs_3_ = f32[512,512]{1,0:T(8,128)} collective-permute-done((f32[512,512]{1,0:T(8,128)}, f32[512,512]{1,0:T(8,128)}, u32[]{:S(2)}, u32[]{:S(2)}) %collective-permute-start.5) | collective-permute-done | bytes 1048608 | tf_op jit(solution)/shard_map/ppermute | solution.py:45
  50.6 2.7 collective-permute-start.8
  53.4 2.1 shard_map.64
  55.5 17.6 %collective-permute-done.13.refs_0_.refs_2_ = f32[512,512]{1,0:T(8,128)} collective-permute-done((f32[512,512]{1,0:T(8,128)}, f32[512,512]{1,0:T(8,128)}, u32[]{:S(2)}, u32[]{:S(2)}) %collective-permute-start.13) | collective-permute-done | bytes 1048608 | tf_op jit(solution)/shard_map/ppermute | solution.py:45
  73.1 2.3 collective-permute-start.29
  75.4 20.2 %collective-permute-done.3.refs_1_.refs_3_ = f32[512,512]{1,0:T(8,128)} collective-permute-done((f32[512,512]{1,0:T(8,128)}, f32[512,512]{1,0:T(8,128)}, u32[]{:S(2)}, u32[]{:S(2)}) %collective-permute-start.3) | collective-permute-done | bytes 1048608 | tf_op jit(solution)/shard_map/ppermute | solution.py:45
  95.6 2.1 shard_map.61
  97.7 1.4 collective-permute-start.22
  101.8 3.3 conditional.1
  101.8 1.1 broadcast.405.clone
  102.9 1.1 broadcast.405.clone2
  104.0 1.1 broadcast.405.clone2.1
  105.0 2.5 collective-permute-start.9
  108.2 3.6 %collective-permute-start.14 = (f32[512,512]{1,0:T(8,128)}, f32[512,512]{1,0:T(8,128)}, u32[]{:S(2)}, u32[]{:S(2)}) collective-permute-start(f32[512,512]{1,0:T(8,128)} %collective-permute-done.13.refs_0_.refs_2_), channel_id=1, source_target_pairs={{0,24},{1,25},{2,26},{3,27},{4,28},{5,29},{6,30},{7,31},{8,16},{9,... | collective-permute-start | bytes 3145736 | tf_op jit(solution)/shard_map/ppermute | solution.py:45
  111.7 2.6 collective-permute-start.16
  115.0 5.3 %shard_map.66 = (f32[7,256,128]{2,1,0:T(8,128)}, f32[7,256,128]{2,1,0:T(8,128)}, f32[7,256,128]{2,1,0:T(8,128)}) custom-call(s32[21]{0:T(128)} %reshape.298.code_ref, s32[1]{0:T(128)} %bitcast.10.k_ref, f32[1024,1024]{1,0:T(8,128)} %refs_0_.17, f32[2,256,1024]{2,1,0:T(8,128)} %collective-permute-done.21.refs_1_, ...), custom_call_target="tpu_custom_call" | custom-call | bytes 5505024 | tf_op jit(solution)/shard_map/pallas_call | solution.py:200
  121.0 4.6 %shard_map.63 = (f32[7,256,128]{2,1,0:T(8,128)}, f32[7,256,128]{2,1,0:T(8,128)}, f32[7,256,128]{2,1,0:T(8,128)}) custom-call(s32[21]{0:T(128)} %reshape.298.code_ref, s32[1]{0:T(128)} %bitcast.10.k_ref, f32[1024,1024]{1,0:T(8,128)} %refs_0_.17, f32[2,256,1024]{2,1,0:T(8,128)} %collective-permute-done.21.refs_1_, ...), custom_call_target="tpu_custom_call" | custom-call | bytes 5505024 | tf_op jit(solution)/shard_map/pallas_call | solution.py:200
  126.5 14.7 %collective-permute-done.9.refs_5_ = f32[3,128,1024]{2,1,0:T(8,128)} collective-permute-done((f32[3,128,1024]{2,1,0:T(8,128)}, f32[3,128,1024]{2,1,0:T(8,128)}, u32[]{:S(2)}, u32[]{:S(2)}) %collective-permute-start.9) | collective-permute-done | bytes 1572896 | tf_op jit(solution)/shard_map/ppermute | solution.py:45
  141.4 1.3 collective-permute-start.26
  142.7 15.4 %collective-permute-done.16.refs_1_.refs_2_ = f32[512,512]{1,0:T(8,128)} collective-permute-done((f32[512,512]{1,0:T(8,128)}, f32[512,512]{1,0:T(8,128)}, u32[]{:S(2)}, u32[]{:S(2)}) %collective-permute-start.16) | collective-permute-done | bytes 1048608 | tf_op jit(solution)/shard_map/ppermute | solution.py:45
  158.1 2.0 collective-permute-start.27
  160.1 1.1 collective-permute-start.28
  161.7 4.5 %shard_map.62 = (f32[5,2,256,128]{3,2,1,0:T(8,128)}, f32[5,2,256,128]{3,2,1,0:T(8,128)}, f32[5,2,256,128]{3,2,1,0:T(8,128)}) custom-call(s32[15]{0:T(128)} %reshape.296.code_ref, s32[1]{0:T(128)} %bitcast.10.k_ref, f32[2,512,1024]{2,1,0:T(8,128)} %bitcast.50, f32[2,256,1024]{2,1,0:T(8,128)} %collective-permute-done.21.refs_1_), custom_call_target="tpu_custom_call" | custom-call | bytes 7864320 | tf_op jit(solution)/shard_map/pallas_call | solution.py:200
  166.7 3.3 collective-permute-done.32.refs_10_
  170.8 11.1 %collective-permute-done.26.refs_8_ = f32[7,256,128]{2,1,0:T(8,128)} collective-permute-done((f32[7,256,128]{2,1,0:T(8,128)}, f32[7,256,128]{2,1,0:T(8,128)}, u32[]{:S(2)}, u32[]{:S(2)}) %collective-permute-start.26) | collective-permute-done | bytes 917536 | tf_op jit(solution)/shard_map/ppermute | solution.py:45
  181.9 2.8 collective-permute-start.25
  184.7 4.0 %collective-permute-done.27.refs_9_ = f32[7,256,128]{2,1,0:T(8,128)} collective-permute-done((f32[7,256,128]{2,1,0:T(8,128)}, f32[7,256,128]{2,1,0:T(8,128)}, u32[]{:S(2)}, u32[]{:S(2)}) %collective-permute-start.27) | collective-permute-done | bytes 917536 | tf_op jit(solution)/shard_map/ppermute | solution.py:45
  188.7 20.6 %collective-permute-done.28.refs_10_ = f32[7,256,128]{2,1,0:T(8,128)} collective-permute-done((f32[7,256,128]{2,1,0:T(8,128)}, f32[7,256,128]{2,1,0:T(8,128)}, u32[]{:S(2)}, u32[]{:S(2)}) %collective-permute-start.28) | collective-permute-done | bytes 917536 | tf_op jit(solution)/shard_map/ppermute | solution.py:45
  210.3 4.1 %shard_map.58 = (f32[3,128,512]{2,1,0:T(8,128)}, f32[3,128,512]{2,1,0:T(8,128)}, f32[3,128,512]{2,1,0:T(8,128)}) custom-call(s32[9]{0:T(128)} %reshape_squeeze.7.code_ref, s32[1]{0:T(128)} %bitcast.10.k_ref, f32[512,512]{1,0:T(8,128)} %collective-permute-done.14.refs_0_.refs_1_, f32[512,512]{1,0:T(8,128)} %collective-permute-done.16.refs_1_.refs_2_), custom_call_target="tpu_custom_call" | custom-call | bytes 4718592 | tf_op jit(solution)/shard_map/pallas_call | solution.py:200
  214.4 15.2 %collective-permute-done.23.refs_5_ = f32[5,2,256,128]{3,2,1,0:T(8,128)} collective-permute-done((f32[5,2,256,128]{3,2,1,0:T(8,128)}, f32[5,2,256,128]{3,2,1,0:T(8,128)}, u32[]{:S(2)}, u32[]{:S(2)}) %collective-permute-start.23) | collective-permute-done | bytes 1310752 | tf_op jit(solution)/shard_map/ppermute | solution.py:45
  229.7 6.8 %collective-permute-done.24.refs_6_ = f32[5,2,256,128]{3,2,1,0:T(8,128)} collective-permute-done((f32[5,2,256,128]{3,2,1,0:T(8,128)}, f32[5,2,256,128]{3,2,1,0:T(8,128)}, u32[]{:S(2)}, u32[]{:S(2)}) %collective-permute-start.24) | collective-permute-done | bytes 1310752 | tf_op jit(solution)/shard_map/ppermute | solution.py:45
  237.0 28.0 %collective-permute-done.25.refs_7_ = f32[5,2,256,128]{3,2,1,0:T(8,128)} collective-permute-done((f32[5,2,256,128]{3,2,1,0:T(8,128)}, f32[5,2,256,128]{3,2,1,0:T(8,128)}, u32[]{:S(2)}, u32[]{:S(2)}) %collective-permute-start.25) | collective-permute-done | bytes 1310752 | tf_op jit(solution)/shard_map/ppermute | solution.py:45
  266.4 9.9 %shard_map.67 = (f32[256,1024]{1,0:T(8,128)}, f32[256,1024]{1,0:T(8,128)}) custom-call(s32[32]{0:T(128)} %reshape.294.code_ref, s32[1]{0:T(128)} %bitcast.10.k_ref, f32[8,2,128,128]{3,2,1,0:T(8,128)} %mine_ref.3, f32[8,2,128,128]{3,2,1,0:T(8,128)} %collective-permute-done.20.other_ref, f32[1024,1024]{1,0:T(8,128)} %refs_0_.17, ...), custom_call_target="tpu_custom_call" | custom-call | flops 805306368 | bytes 8388608 | tf_op jit(solution)/shard_map/pallas_call | solution.py:310
  276.3 9.8 %shard_map.65 = (f32[256,1024]{1,0:T(8,128)}, f32[256,1024]{1,0:T(8,128)}) custom-call(s32[32]{0:T(128)} %reshape.294.code_ref, s32[1]{0:T(128)} %bitcast.10.k_ref, f32[8,2,128,128]{3,2,1,0:T(8,128)} %mine_ref.3, f32[8,2,128,128]{3,2,1,0:T(8,128)} %collective-permute-done.20.other_ref, f32[1024,1024]{1,0:T(8,128)} %refs_0_.17, ...), custom_call_target="tpu_custom_call" | custom-call | flops 805306368 | bytes 8388608 | tf_op jit(solution)/shard_map/pallas_call | solution.py:310
  286.1 0.9 collective-permute-start.34
  287.1 4.1 %shard_map.57 = (f32[3,128,512]{2,1,0:T(8,128)}, f32[3,128,512]{2,1,0:T(8,128)}, f32[3,128,512]{2,1,0:T(8,128)}) custom-call(s32[9]{0:T(128)} %reshape_squeeze.7.code_ref, s32[1]{0:T(128)} %bitcast.10.k_ref, f32[512,512]{1,0:T(8,128)} %collective-permute-done.4.refs_0_.refs_1_, f32[512,512]{1,0:T(8,128)} %collective-permute-done.6.refs_1_.refs_2_), custom_call_target="tpu_custom_call" | custom-call | bytes 4718592 | tf_op jit(solution)/shard_map/pallas_call | solution.py:200
  292.5 2.0 collective-permute-start.12
  295.4 6.2 %shard_map.59.refs_9_ = f32[1024,512]{1,0:T(8,128)} custom-call(s32[16]{0:T(128)} %fusion.20.code_ref, s32[1]{0:T(128)} %bitcast.10.k_ref, f32[8,2,128,128]{3,2,1,0:T(8,128)} %w_ref.3, f32[1024,1024]{1,0:T(8,128)} %refs_0_.17, f32[512,512]{1,0:T(8,128)} %collective-permute-done.14.refs_0_.refs_1_, f32[512,512]{1,0:T(8,128)} %collective-permute-done.16.refs_1_.refs_2_, ...), custom_call_target="tpu_custom_call" | custom-call | flops 805306368 | bytes 7340032 | tf_op jit(solution)/shard_map/pallas_call | solution.py:366
  301.5 26.8 %collective-permute-done.10.refs_6_ = f32[3,128,512]{2,1,0:T(8,128)} collective-permute-done((f32[3,128,512]{2,1,0:T(8,128)}, f32[3,128,512]{2,1,0:T(8,128)}, u32[]{:S(2)}, u32[]{:S(2)}) %collective-permute-start.10) | collective-permute-done | bytes 786464 | tf_op jit(solution)/shard_map/ppermute | solution.py:45
  328.7 9.0 %shard_map.68 = f32[1024,1024]{1,0:T(8,128)} custom-call(s32[16]{0:T(128)} %fusion.20.code_ref, s32[1]{0:T(128)} %bitcast.10.k_ref, f32[8,2,128,128]{3,2,1,0:T(8,128)} %w_ref.3, f32[1024,1024]{1,0:T(8,128)} %refs_0_.17, f32[512,512]{1,0:T(8,128)} %collective-permute-done.4.refs_0_.refs_1_, f32[512,512]{1,0:T(8,128)} %collective-permute-done.6.refs_1_.refs_2_, ...), custom_call_target="tpu_custom_call" | custom-call | flops 805306368 | bytes 15728640 | tf_op jit(solution)/shard_map/pallas_call | solution.py:366
  (106 shorter events, 15.7 us)
Async XLA Ops:
  3.4 24.8 %collective-permute-start.15 = (f32[512,512]{1,0:T(8,128)}, f32[512,512]{1,0:T(8,128)}, u32[]{:S(2)}, u32[]{:S(2)}) collective-permute-start(f32[512,512]{1,0:T(8,128)} %get-tuple-element.78), channel_id=1, source_target_pairs={{0,8},{1,9},{2,10},{3,11},{4,12},{5,13},{6,14},{7,15},{8,0},{9,1},... | collective-permute-start | bytes 3145736 | tf_op jit(solution)/shard_map/ppermute | solution.py:45
  5.1 5.4 %copy-start.7 = (s32[128,2]{0,1:T(2,128)S(1)}, s32[128,2]{0,1:T(2,128)}, u32[]{:S(2)}) copy-start(s32[128,2]{0,1:T(2,128)} %param.10) | copy-start | bytes 3076
  5.1 6.1 %copy-start.8 = (s32[64,2]{0,1:T(2,128)S(1)}, s32[64,2]{0,1:T(2,128)}, u32[]{:S(2)}) copy-start(s32[64,2]{0,1:T(2,128)} %param.8) | copy-start | bytes 1540
  5.1 45.5 %collective-permute-start.5 = (f32[512,512]{1,0:T(8,128)}, f32[512,512]{1,0:T(8,128)}, u32[]{:S(2)}, u32[]{:S(2)}) collective-permute-start(f32[512,512]{1,0:T(8,128)} %get-tuple-element.70), channel_id=1, source_target_pairs={{0,8},{1,9},{2,10},{3,11},{4,12},{5,13},{6,14},{7,15},{8,0},{9,1},... | collective-permute-start | bytes 3145736 | tf_op jit(solution)/shard_map/ppermute | solution.py:45
  7.8 93.2 %collective-permute-start.21 = (f32[2,256,1024]{2,1,0:T(8,128)}, f32[2,256,1024]{2,1,0:T(8,128)}, u32[]{:S(2)}, u32[]{:S(2)}) collective-permute-start(f32[2,256,1024]{2,1,0:T(8,128)} %shard_map.60), channel_id=1, source_target_pairs={{0,1},{1,0},{2,3},{3,2},{4,5},{5,4},{6,7},{7,6},{8,9},{9,8},{10,11... | collective-permute-start | bytes 6291464 | tf_op jit(solution)/shard_map/ppermute | solution.py:45
  8.9 64.2 %collective-permute-start.13 = (f32[512,512]{1,0:T(8,128)}, f32[512,512]{1,0:T(8,128)}, u32[]{:S(2)}, u32[]{:S(2)}) collective-permute-start(f32[512,512]{1,0:T(8,128)} %get-tuple-element.77), channel_id=1, source_target_pairs={{0,8},{1,9},{2,10},{3,11},{4,12},{5,13},{6,14},{7,15},{8,0},{9,1},... | collective-permute-start | bytes 3145736 | tf_op jit(solution)/shard_map/ppermute | solution.py:45
  10.5 85.1 %collective-permute-start.3 = (f32[512,512]{1,0:T(8,128)}, f32[512,512]{1,0:T(8,128)}, u32[]{:S(2)}, u32[]{:S(2)}) collective-permute-start(f32[512,512]{1,0:T(8,128)} %get-tuple-element.69), channel_id=1, source_target_pairs={{0,8},{1,9},{2,10},{3,11},{4,12},{5,13},{6,14},{7,15},{8,0},{9,1},... | collective-permute-start | bytes 3145736 | tf_op jit(solution)/shard_map/ppermute | solution.py:45
  28.2 92.1 %collective-permute-start.7 = (f32[3,128,1024]{2,1,0:T(8,128)}, f32[3,128,1024]{2,1,0:T(8,128)}, u32[]{:S(2)}, u32[]{:S(2)}) collective-permute-start(f32[3,128,1024]{2,1,0:T(8,128)} %get-tuple-element.71), channel_id=1, source_target_pairs={{0,32},{1,33},{2,34},{3,35},{4,36},{5,37},{6,38},{7,39},{8,40},{9,... | collective-permute-start | bytes 4718600 | tf_op jit(solution)/shard_map/ppermute | solution.py:45
  50.6 75.0 %collective-permute-start.8 = (f32[3,128,1024]{2,1,0:T(8,128)}, f32[3,128,1024]{2,1,0:T(8,128)}, u32[]{:S(2)}, u32[]{:S(2)}) collective-permute-start(f32[3,128,1024]{2,1,0:T(8,128)} %get-tuple-element.72), channel_id=1, source_target_pairs={{0,64},{1,65},{2,66},{3,67},{4,68},{5,69},{6,70},{7,71},{8,72},{9,... | collective-permute-start | bytes 4718600 | tf_op jit(solution)/shard_map/ppermute | solution.py:45
  73.1 27.9 %collective-permute-start.29 = (f32[2,256,512]{2,1,0:T(8,128)}, f32[2,256,512]{2,1,0:T(8,128)}, u32[]{:S(2)}, u32[]{:S(2)}) collective-permute-start(f32[2,256,512]{2,1,0:T(8,128)} %shard_map.64), channel_id=1, source_target_pairs={{0,1},{1,0},{2,3},{3,2},{4,5},{5,4},{6,7},{7,6},{8,9},{9,8},{10,11... | collective-permute-start | bytes 3145736 | tf_op jit(solution)/shard_map/ppermute | solution.py:45
  97.7 4.1 %collective-permute-start.22 = (f32[2,256,512]{2,1,0:T(8,128)}, f32[2,256,512]{2,1,0:T(8,128)}, u32[]{:S(2)}, u32[]{:S(2)}) collective-permute-start(f32[2,256,512]{2,1,0:T(8,128)} %shard_map.61), channel_id=1, source_target_pairs={{0,1},{1,0},{2,3},{3,2},{4,5},{5,4},{6,7},{7,6},{8,9},{9,8},{10,11... | collective-permute-start | bytes 3145736 | tf_op jit(solution)/shard_map/ppermute | solution.py:45
  105.0 36.2 %collective-permute-start.9 = (f32[3,128,1024]{2,1,0:T(8,128)}, f32[3,128,1024]{2,1,0:T(8,128)}, u32[]{:S(2)}, u32[]{:S(2)}) collective-permute-start(f32[3,128,1024]{2,1,0:T(8,128)} %get-tuple-element.73), channel_id=1, source_target_pairs={{0,96},{1,97},{2,98},{3,99},{4,100},{5,101},{6,102},{7,103},{8,104... | collective-permute-start | bytes 4718600 | tf_op jit(solution)/shard_map/ppermute | solution.py:45
  107.5 4.2 %collective-permute-start.20 = (f32[8,2,128,128]{3,2,1,0:T(8,128)}, f32[8,2,128,128]{3,2,1,0:T(8,128)}, u32[]{:S(2)}, u32[]{:S(2)}) collective-permute-start(f32[8,2,128,128]{3,2,1,0:T(8,128)} %mine_ref.3), channel_id=1, source_target_pairs={{0,1},{1,0},{2,3},{3,2},{4,5},{5,4},{6,7},{7,6},{8,9},{9,8},{10,11... | collective-permute-start | bytes 3145736 | tf_op jit(solution)/shard_map/ppermute | solution.py:45
  108.2 33.2 %collective-permute-start.14 = (f32[512,512]{1,0:T(8,128)}, f32[512,512]{1,0:T(8,128)}, u32[]{:S(2)}, u32[]{:S(2)}) collective-permute-start(f32[512,512]{1,0:T(8,128)} %collective-permute-done.13.refs_0_.refs_2_), channel_id=1, source_target_pairs={{0,24},{1,25},{2,26},{3,27},{4,28},{5,29},{6,30},{7,31},{8,16},{9,... | collective-permute-start | bytes 3145736 | tf_op jit(solution)/shard_map/ppermute | solution.py:45
  111.7 46.3 %collective-permute-start.16 = (f32[512,512]{1,0:T(8,128)}, f32[512,512]{1,0:T(8,128)}, u32[]{:S(2)}, u32[]{:S(2)}) collective-permute-start(f32[512,512]{1,0:T(8,128)} %collective-permute-done.15.refs_0_.refs_2_), channel_id=1, source_target_pairs={{0,24},{1,25},{2,26},{3,27},{4,28},{5,29},{6,30},{7,31},{8,16},{9,... | collective-permute-start | bytes 3145736 | tf_op jit(solution)/shard_map/ppermute | solution.py:45
  120.3 39.8 %collective-permute-start.30 = (f32[7,256,128]{2,1,0:T(8,128)}, f32[7,256,128]{2,1,0:T(8,128)S(1)}, u32[]{:S(2)}, u32[]{:S(2)}) collective-permute-start(f32[7,256,128]{2,1,0:T(8,128)} %get-tuple-element.92), channel_id=1, source_target_pairs={{0,2},{1,3},{2,4},{3,5},{4,6},{5,7},{6,0},{7,1},{8,10},{9,11},{10,... | collective-permute-start | bytes 2752520 | tf_op jit(solution)/shard_map/ppermute | solution.py:45
  125.7 40.6 %collective-permute-start.31 = (f32[7,256,128]{2,1,0:T(8,128)}, f32[7,256,128]{2,1,0:T(8,128)}, u32[]{:S(2)}, u32[]{:S(2)}) collective-permute-start(f32[7,256,128]{2,1,0:T(8,128)} %get-tuple-element.93), channel_id=1, source_target_pairs={{0,4},{1,5},{2,6},{3,7},{4,0},{5,1},{6,2},{7,3},{8,12},{9,13},{10,... | collective-permute-start | bytes 2752520 | tf_op jit(solution)/shard_map/ppermute | solution.py:45
  141.2 28.8 %collective-permute-start.32 = (f32[7,256,128]{2,1,0:T(8,128)}, f32[7,256,128]{2,1,0:T(8,128)}, u32[]{:S(2)}, u32[]{:S(2)}) collective-permute-start(f32[7,256,128]{2,1,0:T(8,128)} %get-tuple-element.94), channel_id=1, source_target_pairs={{0,6},{1,7},{2,0},{3,1},{4,2},{5,3},{6,4},{7,5},{8,14},{9,15},{10,... | collective-permute-start | bytes 2752520 | tf_op jit(solution)/shard_map/ppermute | solution.py:45
  141.4 40.5 %collective-permute-start.26 = (f32[7,256,128]{2,1,0:T(8,128)}, f32[7,256,128]{2,1,0:T(8,128)}, u32[]{:S(2)}, u32[]{:S(2)}) collective-permute-start(f32[7,256,128]{2,1,0:T(8,128)} %get-tuple-element.85), channel_id=1, source_target_pairs={{0,2},{1,3},{2,4},{3,5},{4,6},{5,7},{6,0},{7,1},{8,10},{9,11},{10,... | collective-permute-start | bytes 2752520 | tf_op jit(solution)/shard_map/ppermute | solution.py:45
  158.1 30.6 %collective-permute-start.27 = (f32[7,256,128]{2,1,0:T(8,128)}, f32[7,256,128]{2,1,0:T(8,128)}, u32[]{:S(2)}, u32[]{:S(2)}) collective-permute-start(f32[7,256,128]{2,1,0:T(8,128)} %get-tuple-element.86), channel_id=1, source_target_pairs={{0,4},{1,5},{2,6},{3,7},{4,0},{5,1},{6,2},{7,3},{8,12},{9,13},{10,... | collective-permute-start | bytes 2752520 | tf_op jit(solution)/shard_map/ppermute | solution.py:45
  160.1 6.2 %copy-start = (f32[7,256,128]{2,1,0:T(8,128)}, f32[7,256,128]{2,1,0:T(8,128)S(1)}, u32[]{:S(2)}) copy-start(f32[7,256,128]{2,1,0:T(8,128)S(1)} %collective-permute-done.30.refs_8_) | copy-start | bytes 2752516
  160.1 49.2 %collective-permute-start.28 = (f32[7,256,128]{2,1,0:T(8,128)}, f32[7,256,128]{2,1,0:T(8,128)}, u32[]{:S(2)}, u32[]{:S(2)}) collective-permute-start(f32[7,256,128]{2,1,0:T(8,128)} %get-tuple-element.87), channel_id=1, source_target_pairs={{0,6},{1,7},{2,0},{3,1},{4,2},{5,3},{6,4},{7,5},{8,14},{9,15},{10,... | collective-permute-start | bytes 2752520 | tf_op jit(solution)/shard_map/ppermute | solution.py:45
  166.3 63.4 %collective-permute-start.23 = (f32[5,2,256,128]{3,2,1,0:T(8,128)}, f32[5,2,256,128]{3,2,1,0:T(8,128)}, u32[]{:S(2)}, u32[]{:S(2)}) collective-permute-start(f32[5,2,256,128]{3,2,1,0:T(8,128)} %get-tuple-element.82), channel_id=1, source_target_pairs={{0,2},{1,3},{2,4},{3,5},{4,6},{5,7},{6,0},{7,1},{8,10},{9,11},{10,... | collective-permute-start | bytes 3932168 | tf_op jit(solution)/shard_map/ppermute | solution.py:45
  170.0 66.5 %collective-permute-start.24 = (f32[5,2,256,128]{3,2,1,0:T(8,128)}, f32[5,2,256,128]{3,2,1,0:T(8,128)}, u32[]{:S(2)}, u32[]{:S(2)}) collective-permute-start(f32[5,2,256,128]{3,2,1,0:T(8,128)} %get-tuple-element.83), channel_id=1, source_target_pairs={{0,4},{1,5},{2,6},{3,7},{4,0},{5,1},{6,2},{7,3},{8,12},{9,13},{10,... | collective-permute-start | bytes 3932168 | tf_op jit(solution)/shard_map/ppermute | solution.py:45
  181.9 83.1 %collective-permute-start.25 = (f32[5,2,256,128]{3,2,1,0:T(8,128)}, f32[5,2,256,128]{3,2,1,0:T(8,128)}, u32[]{:S(2)}, u32[]{:S(2)}) collective-permute-start(f32[5,2,256,128]{3,2,1,0:T(8,128)} %get-tuple-element.84), channel_id=1, source_target_pairs={{0,6},{1,7},{2,0},{3,1},{4,2},{5,3},{6,4},{7,5},{8,14},{9,15},{10,... | collective-permute-start | bytes 3932168 | tf_op jit(solution)/shard_map/ppermute | solution.py:45
  188.7 97.4 %collective-permute-start.4 = (f32[512,512]{1,0:T(8,128)}, f32[512,512]{1,0:T(8,128)}, u32[]{:S(2)}, u32[]{:S(2)}) collective-permute-start(f32[512,512]{1,0:T(8,128)} %collective-permute-done.3.refs_1_.refs_3_), channel_id=1, source_target_pairs={{0,24},{1,25},{2,26},{3,27},{4,28},{5,29},{6,30},{7,31},{8,16},{9,... | collective-permute-start | bytes 3145736 | tf_op jit(solution)/shard_map/ppermute | solution.py:45
  209.3 77.7 %collective-permute-start.6 = (f32[512,512]{1,0:T(8,128)}, f32[512,512]{1,0:T(8,128)}, u32[]{:S(2)}, u32[]{:S(2)}) collective-permute-start(f32[512,512]{1,0:T(8,128)} %collective-permute-done.5.refs_1_.refs_3_), channel_id=1, source_target_pairs={{0,24},{1,25},{2,26},{3,27},{4,28},{5,29},{6,30},{7,31},{8,16},{9,... | collective-permute-start | bytes 3145736 | tf_op jit(solution)/shard_map/ppermute | solution.py:45
  229.7 61.5 %collective-permute-start.17 = (f32[3,128,512]{2,1,0:T(8,128)}, f32[3,128,512]{2,1,0:T(8,128)S(1)}, u32[]{:S(2)}, u32[]{:S(2)}) collective-permute-start(f32[3,128,512]{2,1,0:T(8,128)} %get-tuple-element.79), channel_id=1, source_target_pairs={{0,32},{1,33},{2,34},{3,35},{4,36},{5,37},{6,38},{7,39},{8,40},{9,... | collective-permute-start | bytes 2359304 | tf_op jit(solution)/shard_map/ppermute | solution.py:45
  236.5 55.5 %collective-permute-start.18 = (f32[3,128,512]{2,1,0:T(8,128)}, f32[3,128,512]{2,1,0:T(8,128)}, u32[]{:S(2)}, u32[]{:S(2)}) collective-permute-start(f32[3,128,512]{2,1,0:T(8,128)} %get-tuple-element.80), channel_id=1, source_target_pairs={{0,64},{1,65},{2,66},{3,67},{4,68},{5,69},{6,70},{7,71},{8,72},{9,... | collective-permute-start | bytes 2359304 | tf_op jit(solution)/shard_map/ppermute | solution.py:45
  265.0 27.5 %collective-permute-start.19 = (f32[3,128,512]{2,1,0:T(8,128)}, f32[3,128,512]{2,1,0:T(8,128)}, u32[]{:S(2)}, u32[]{:S(2)}) collective-permute-start(f32[3,128,512]{2,1,0:T(8,128)} %get-tuple-element.81), channel_id=1, source_target_pairs={{0,96},{1,97},{2,98},{3,99},{4,100},{5,101},{6,102},{7,103},{8,104... | collective-permute-start | bytes 2359304 | tf_op jit(solution)/shard_map/ppermute | solution.py:45
  286.1 42.6 %collective-permute-start.34 = (f32[256,1024]{1,0:T(8,128)}, f32[256,1024]{1,0:T(8,128)}, u32[]{:S(2)}, u32[]{:S(2)}) collective-permute-start(f32[256,1024]{1,0:T(8,128)} %get-tuple-element.97), channel_id=1, source_target_pairs={{0,1},{1,0},{2,3},{3,2},{4,5},{5,4},{6,7},{7,6},{8,9},{9,8},{10,11... | collective-permute-start | bytes 3145736 | tf_op jit(solution)/shard_map/ppermute | solution.py:45
  287.0 41.7 %collective-permute-start.33 = (f32[256,1024]{1,0:T(8,128)}, f32[256,1024]{1,0:T(8,128)}, u32[]{:S(2)}, u32[]{:S(2)}) collective-permute-start(f32[256,1024]{1,0:T(8,128)} %get-tuple-element.96), channel_id=1, source_target_pairs={{0,1},{1,0},{2,3},{3,2},{4,5},{5,4},{6,7},{7,6},{8,9},{9,8},{10,11... | collective-permute-start | bytes 3145736 | tf_op jit(solution)/shard_map/ppermute | solution.py:45
  291.2 4.2 %copy-start.1 = (f32[3,128,512]{2,1,0:T(8,128)}, f32[3,128,512]{2,1,0:T(8,128)S(1)}, u32[]{:S(2)}) copy-start(f32[3,128,512]{2,1,0:T(8,128)S(1)} %collective-permute-done.17.refs_6_) | copy-start | bytes 2359300
  291.2 37.1 %collective-permute-start.10 = (f32[3,128,512]{2,1,0:T(8,128)}, f32[3,128,512]{2,1,0:T(8,128)}, u32[]{:S(2)}, u32[]{:S(2)}) collective-permute-start(f32[3,128,512]{2,1,0:T(8,128)} %get-tuple-element.74), channel_id=1, source_target_pairs={{0,32},{1,33},{2,34},{3,35},{4,36},{5,37},{6,38},{7,39},{8,40},{9,... | collective-permute-start | bytes 2359304 | tf_op jit(solution)/shard_map/ppermute | solution.py:45
  292.0 36.3 %collective-permute-start.11 = (f32[3,128,512]{2,1,0:T(8,128)}, f32[3,128,512]{2,1,0:T(8,128)}, u32[]{:S(2)}, u32[]{:S(2)}) collective-permute-start(f32[3,128,512]{2,1,0:T(8,128)} %get-tuple-element.75), channel_id=1, source_target_pairs={{0,64},{1,65},{2,66},{3,67},{4,68},{5,69},{6,70},{7,71},{8,72},{9,... | collective-permute-start | bytes 2359304 | tf_op jit(solution)/shard_map/ppermute | solution.py:45
  292.5 36.2 %collective-permute-start.12 = (f32[3,128,512]{2,1,0:T(8,128)}, f32[3,128,512]{2,1,0:T(8,128)}, u32[]{:S(2)}, u32[]{:S(2)}) collective-permute-start(f32[3,128,512]{2,1,0:T(8,128)} %get-tuple-element.76), channel_id=1, source_target_pairs={{0,96},{1,97},{2,98},{3,99},{4,100},{5,101},{6,102},{7,103},{8,104... | collective-permute-start | bytes 2359304 | tf_op jit(solution)/shard_map/ppermute | solution.py:45

commit v3 on v2

--- a/solution.py
+++ b/solution.py
@@ -9,7 +9,10 @@
 B = 128
 AXES = ("row", "col")
 HOPS = (1, 2, 3)
-EARLY, LATE = 5, 7
+STARTS, SLOTS = (0, 5, 11, 12), (5, 6, 1, 4)
+EARLY, LATE, *EXTRA = SLOTS
+ALPHA_OWN, ALPHA_LATE, ALPHA_CODE, BETA_LISTS = 1, 10, 19, 35
+BETA_CODE = BETA_LISTS + 3 * 16
 NX, NZH, NZL, NY, NK = 4, 2, 2, 4, 2
 
 
@@ -101,7 +104,7 @@
     mask = mask.reshape(NZL, NY, NY, 32)
     pos = pos.reshape(NZL, NY, NY, 32)
     far = (jnp.arange(NY)[:, None] != jnp.arange(NY)[None, :]).astype(jnp.int32)
-    fits = jnp.max(mask * (pos + 1) * far[None, :, :, None]) <= EARLY + LATE
+    need = jnp.max(mask * (pos + 1) * far[None, :, :, None])
     mask = lax.dynamic_index_in_dim(mask, zl, 0, keepdims=False)
     pos = lax.dynamic_index_in_dim(pos, zl, 0, keepdims=False)
     sent = _lists(
@@ -119,32 +122,35 @@
     key = (source_y * 2 + other) * 16 + block
     slot = jnp.sum((key[:, None] == jnp.arange(my_pos.size)) * my_pos, axis=1)
     hop = (y - source_y) % NY
-    late, extra = (slot >= EARLY).astype(jnp.int32), (slot >= EARLY + LATE).astype(jnp.int32)
+    passed = [(slot >= start).astype(jnp.int32) for start in STARTS[1:]]
+    level = sum(passed)
+    at = slot - sum((start - before) * p for before, start, p in zip(STARTS, STARTS[1:], passed))
     near = (other * 2 + jnp.abs(block // 8 - k)) * 32 + block % 8
-    code = jnp.where(hop == 0, near, (3 + hop + 3 * late + 3 * extra) * 32 + slot - EARLY * late - LATE * extra)
+    code = jnp.where(hop == 0, near, (3 + hop + 3 * level) * 32 + at)
     code = jnp.roll(code.reshape(2, 16), -k, axis=0).reshape(-1)
-    lists = [part.reshape(-1) for part in jnp.split(sent, [EARLY, EARLY + LATE], axis=1)]
-    return (*lists, code.astype(jnp.int32), fits)
+    lists = [part.reshape(-1) for part in jnp.split(sent, STARTS[1:], axis=1)]
+    return (*lists, code.astype(jnp.int32), need)
 
 
 def _rows(i):
     return pl.ds(pl.multiple_of(i * B, B), B)
 
 
-def _core():
-    return lax.rem(lax.axis_index("col"), NK).reshape(1)
-
-
 def _fetch(code, options, dst, sem):
     place, at = code // 32, code % 32
-    for number, source, half in options:
-        test = place == number
-        if half is not None:
-            test = jnp.logical_and(test, at // 4 == half)
-
-        @pl.when(test)
-        def _(source=source):
-            pltpu.make_async_copy(source(at), dst, sem).start()
+    for group in options:
+        first, last = group[0][0], group[-1][0]
+
+        @pl.when(jnp.logical_and(place >= first, place <= last))
+        def _(group=group):
+            for number, source, half in group:
+                test = place == number
+                if half is not None:
+                    test = jnp.logical_and(test, at // 4 == half)
+
+                @pl.when(test)
+                def _(source=source):
+                    pltpu.make_async_copy(source(at), dst, sem).start()
 
 
 def _wait(ref, sem):
@@ -168,16 +174,16 @@
     return pl.CostEstimate(flops=flops, bytes_accessed=bytes_, transcendentals=0)
 
 
-def _gather(codes, slot_shape, slots, sources, options_of):
+def _gather(table, start, slot_shape, slots, sources, options_of):
     count = 3 * slots
 
-    def kernel(code_ref, k_ref, *refs):
+    def kernel(table_ref, *refs):
         ins, outs = refs[: len(sources)], refs[len(sources) : len(sources) + 3]
         buf, in_sem, out_sem = refs[len(sources) + 3 :]
-        options = options_of(ins, k_ref[0])
+        options = options_of(ins, table_ref[0])
 
         def load(s, _):
-            _fetch(code_ref[s], options, buf.at[s], in_sem.at[s])
+            _fetch(table_ref[start + s], options, buf.at[s], in_sem.at[s])
 
         lax.fori_loop(0, count, load, None)
         for hop, out in enumerate(outs):
@@ -200,7 +206,7 @@
     return pl.pallas_call(
         kernel,
         out_shape=[_f32(slots, *slot_shape)] * 3,
-        in_specs=[SMEM, SMEM] + [ANY] * len(sources),
+        in_specs=[SMEM] + [ANY] * len(sources),
         out_specs=[ANY] * 3,
         scratch_shapes=[
             pltpu.VMEM((count, *slot_shape), jnp.float32),
@@ -209,10 +215,10 @@
         ],
         compiler_params=_params(),
         cost_estimate=_cost(2 * size),
-    )(codes, _core(), *sources)
-
-
-def _pick(shapes, sources, picks_of):
+    )(table, *sources)
+
+
+def _pick(core, shapes, sources, picks_of):
     def kernel(k_ref, *refs):
         ins, outs = refs[: len(sources)], refs[len(sources) : len(sources) + len(shapes)]
         bufs = refs[len(sources) + len(shapes) : -2]
@@ -247,7 +253,7 @@
         + [pltpu.SemaphoreType.DMA((4,)), pltpu.SemaphoreType.DMA((4,))],
         compiler_params=_params(),
         cost_estimate=_cost(size),
-    )(_core(), *sources)
+    )(core, *sources)
 
 
 def _split(v):
@@ -283,125 +289,177 @@
     ]
 
 
-def beta_product(r, codes, mine, other, v, x0, q0, q1, x1, early, late, extra):
-    def kernel(code_ref, k_ref, mine_ref, other_ref, *refs):
-        out_mine, out_other, buf, sem = refs[14:]
-        options = _near(r, k_ref[0], *refs[0:5])
-        options += [(4 + i, lambda s, i=i: refs[5 + i].at[s, r], None) for i in range(3)]
-        options += [(7 + i, lambda s, i=i: refs[8 + i].at[s], None) for i in range(3)]
-        options += [(10 + i, lambda s, i=i: refs[11 + i].at[s, r], None) for i in range(3)]
+def beta_product(r, table, mine, other, v, x0, q0, q1, x1, early, late, extra):
+    def kernel(table_ref, *refs):
+        weights, ins, outs = refs[0:2], refs[2:-8], refs[-8:-6]
+        buf, w_buf, out_buf, sem, w_sem, out_sem = refs[-6:]
+        loads = [pltpu.make_async_copy(weights[i], w_buf.at[i], w_sem.at[i]) for i in range(2)]
+        for copy in loads:
+            copy.start()
+        options = [
+            _near(r, table_ref[0], *ins[0:5]),
+            [(4 + i, lambda s, i=i: ins[5 + i].at[s, r], None) for i in range(3)],
+            [(7 + i, lambda s, i=i: ins[8 + i].at[s], None) for i in range(3)],
+        ]
+        for n in range(len(EXTRA)):
+            options.append([(10 + i, lambda s, i=i: ins[11 + i].at[s, r], None) for i in range(3 * n, 3 * n + 3)])
 
         def load(n, _):
-            _fetch(code_ref[n], options, buf.at[n], sem.at[n])
+            _fetch(table_ref[BETA_CODE + n], options, buf.at[n], sem.at[n])
 
         lax.fori_loop(0, 32, load, None)
-        for first, w_ref, out in ((0, mine_ref, out_mine), (16, other_ref, out_other)):
-
-            def block(h, _, first=first, w_ref=w_ref, out=out):
-                n = first + 2 * h
-                w = jnp.concatenate([w_ref[h, 0], w_ref[h, 1]], axis=1)
+        for copy in loads:
+            copy.wait()
+        stores = []
+        for i in range(2):
+
+            def block(h, _, i=i):
+                n = 16 * i + 2 * h
+                w = jnp.concatenate([w_buf[i, h, 0], w_buf[i, h, 1]], axis=1)
                 _wait(buf.at[n], sem.at[n])
                 _wait(buf.at[n + 1], sem.at[n + 1])
                 blocks = jnp.concatenate([buf[n], buf[n + 1]], axis=1)
-                out[:, _rows(h)] = _dot3(blocks, w, ((1,), (1,)))
-
-            lax.fori_loop(0, 8, block, None, unroll=2)
+                out_buf[i, :, _rows(h)] = _dot3(blocks, w, ((1,), (1,)))
+
+            for part in range(2):
+                lax.fori_loop(4 * part, 4 * part + 4, block, None, unroll=2)
+                columns = slice(512 * part, 512 * part + 512)
+                copy = pltpu.make_async_copy(out_buf.at[i, :, columns], outs[i].at[:, columns], out_sem.at[2 * i + part])
+                copy.start()
+                stores.append(copy)
+        for copy in stores:
+            copy.wait()
 
     return pl.pallas_call(
         kernel,
         out_shape=[_f32(256, 1024)] * 2,
-        in_specs=[SMEM, SMEM, VMEM, VMEM] + [ANY] * 14,
-        out_specs=[VMEM, VMEM],
-        scratch_shapes=[pltpu.VMEM((32, 256, B), jnp.float32), pltpu.SemaphoreType.DMA((32,))],
+        in_specs=[SMEM] + [ANY] * (13 + len(extra)),
+        out_specs=[ANY, ANY],
+        scratch_shapes=[
+            pltpu.VMEM((32, 256, B), jnp.float32),
+            pltpu.VMEM((2, 8, 2, B, B), jnp.float32),
+            pltpu.VMEM((2, 256, 1024), jnp.float32),
+            pltpu.SemaphoreType.DMA((32,)),
+            pltpu.SemaphoreType.DMA((2,)),
+            pltpu.SemaphoreType.DMA((4,)),
+        ],
         compiler_params=_params(),
         cost_estimate=_cost(8 * 2**20, 3 * 32 * 2 * 256 * B * B),
-    )(codes, _core(), mine, other, v, x0, q0, q1, x1, *early, *late, *extra)
-
-
-def alpha_product(c, codes, values, v, q0, q1, own, late, tail=None):
-    def kernel(code_ref, k_ref, w_ref, *refs):
-        rest = refs[9:]
-        out, buf, sem = rest[-3:]
+    )(table, mine, other, v, x0, q0, q1, x1, *early, *late, *extra)
+
+
+def alpha_product(c, table, values, v, q0, q1, own, late, tail=None):
+    width = 512 if tail is None else 1024
+    extra = [] if tail is None else [tail[0], *tail[1], *tail[2]]
+
+    def body(table_ref, weights, ins, more, out, buf, w_buf, out_buf, sem, w_sem, out_sem, sum_buf=None, part_buf=None):
+        k = table_ref[0]
+        w_load = pltpu.make_async_copy(weights, w_buf, w_sem.at[0])
+        w_load.start()
         columns = pl.ds(c * 512, 512)
-        v_ref, q0_ref, q1_ref = refs[0:3]
         options = [
-            (0, lambda j: v_ref.at[_rows(j), columns], None),
-            (1, lambda j: q0_ref.at[_rows(j % 4)], 0),
-            (1, lambda j: q1_ref.at[_rows(j % 4)], 1),
+            [
+                (0, lambda j: ins[0].at[_rows(j), columns], None),
+                (1, lambda j: ins[1].at[_rows(j % 4)], 0),
+                (1, lambda j: ins[2].at[_rows(j % 4)], 1),
+            ],
+            [(2 + i, lambda s, i=i: ins[3 + i].at[s, :, columns], None) for i in range(3)],
+            [(5 + i, lambda s, i=i: ins[6 + i].at[s], None) for i in range(3)],
         ]
-        options += [(2 + i, lambda s, i=i: refs[3 + i].at[s, :, columns], None) for i in range(3)]
-        options += [(5 + i, lambda s, i=i: refs[6 + i].at[s], None) for i in range(3)]
 
         def load(n, _):
-            _fetch(code_ref[n], options, buf.at[n], sem.at[n])
+            _fetch(table_ref[ALPHA_CODE + n], options, buf.at[n], sem.at[n])
 
         lax.fori_loop(0, 16, load, None)
-        k = k_ref[0]
-        for g in range(8):
-            w = jnp.concatenate([w_ref[g, 0], w_ref[g, 1]], axis=1)
+        loads = [w_load]
+        if tail is not None:
+            terms = [(more[0], part_buf)]
+            for r in range(2):
+                terms.append((more[1 + r], sum_buf.at[_my_rows(r, k)]))
+                terms.append((more[3 + r], sum_buf.at[_my_rows(r, 1 - k)]))
+            for n, (source, target) in enumerate(terms):
+                copy = pltpu.make_async_copy(source, target, w_sem.at[1 + n])
+                copy.start()
+                loads.append(copy)
+        for copy in loads:
+            copy.wait()
+
+        def block(g, _):
+            w = jnp.concatenate([w_buf[g, 0], w_buf[g, 1]], axis=1)
             _wait(buf.at[2 * g], sem.at[2 * g])
             _wait(buf.at[2 * g + 1], sem.at[2 * g + 1])
             product = _dot3(w, jnp.concatenate([buf[2 * g], buf[2 * g + 1]], axis=0), ((1,), (0,)))
-            here = slice(g * B, (g + 1) * B)
+            here = _rows(g)
             if tail is None:
-                out[here] = product
-                continue
-            half, share, part = g // 4, (g % 4) // 2, slice((g % 2) * B, (g % 2 + 1) * B)
-
-            def finish(beta_ref, product=product, here=here, part=part):
+                out_buf[here] = product
+            else:
                 for n in range(2):
                     there = slice(n * 512, (n + 1) * 512)
-                    alpha = product if n == c else rest[0][here]
-                    out[here, there] = alpha + beta_ref[part, there]
-
-            @pl.when(k == share)
-            def _(half=half, finish=finish):
-                finish(rest[1 + half])
-
-            @pl.when(k != share)
-            def _(half=half, finish=finish):
-                finish(rest[3 + half])
-
-    extra = [] if tail is None else [tail[0], *tail[1], *tail[2]]
+                    alpha = product if n == c else part_buf[here]
+                    out_buf[here, there] = alpha + sum_buf[here, there]
+            pltpu.make_async_copy(out_buf.at[here], out.at[here], out_sem.at[g]).start()
+
+        lax.fori_loop(0, 8, block, None, unroll=2)
+
+        def finish(g, _):
+            _wait(out_buf.at[_rows(g)], out_sem.at[g])
+
+        lax.fori_loop(0, 8, finish, None)
+
+    def kernel(table_ref, weights, *refs):
+        more = len(extra)
+        body(table_ref, weights, refs[0:9], refs[9 : 9 + more], *refs[9 + more :])
+
+    scratch = [
+        pltpu.VMEM((16, B, 512), jnp.float32),
+        pltpu.VMEM((8, 2, B, B), jnp.float32),
+        pltpu.VMEM((1024, width), jnp.float32),
+        pltpu.SemaphoreType.DMA((16,)),
+        pltpu.SemaphoreType.DMA((6,)),
+        pltpu.SemaphoreType.DMA((8,)),
+    ]
+    if tail is not None:
+        scratch += [pltpu.VMEM((1024, 1024), jnp.float32), pltpu.VMEM((1024, 512), jnp.float32)]
     return pl.pallas_call(
         kernel,
-        out_shape=_f32(1024, 512 if tail is None else 1024),
-        in_specs=[SMEM, SMEM, VMEM] + [ANY] * 9 + [VMEM] * len(extra),
-        out_specs=VMEM,
-        scratch_shapes=[pltpu.VMEM((16, B, 512), jnp.float32), pltpu.SemaphoreType.DMA((16,))],
+        out_shape=_f32(1024, width),
+        in_specs=[SMEM] + [ANY] * (10 + len(extra)),
+        out_specs=ANY,
+        scratch_shapes=scratch,
         compiler_params=_params(),
         cost_estimate=_cost((7 if tail is None else 15) * 2**20, 3 * 16 * 2 * B * B * 512),
-    )(codes, _core(), values, v, q0, q1, *own, *late, *extra)
-
-
-def sigma_here(v, alpha_values, beta_values, alpha, beta):
-    alpha_own, alpha_late, alpha_code = alpha
-    beta_early, beta_late, beta_extra, beta_code, fits = beta
-
-    quadrants = [(0, 0), (0, 1), (1, 0), (1, 1)]
-    (half,) = _pick([(2, 256, 1024)], [v], lambda ins, k: [(ins[0].at[_my_rows(r, 1 - k)], 0, r) for r in range(2)])
+    )(table, values, v, q0, q1, *own, *late, *extra)
+
+
+def sigma_here(v, alpha_values, beta_values, core, table, need):
+    quadrants = [(0, 0), (1, 0), (0, 1), (1, 1)]
+
+    def quadrant(ins, r, c):
+        return ins[0].at[r * 512 : (r + 1) * 512, c * 512 : (c + 1) * 512]
+
+    half, piece = _pick(
+        core,
+        [(2, 256, 1024), (512, 512)],
+        [v],
+        lambda ins, k: [(ins[0].at[_my_rows(r, 1 - k)], 0, r) for r in range(2)] + [(quadrant(ins, 0, 0), 1, None)],
+    )
     x0 = _send(half, TO_CORE)
     pieces = _pick(
-        [(512, 512)] * 4,
-        [v],
-        lambda ins, k: [
-            (ins[0].at[r * 512 : (r + 1) * 512, c * 512 : (c + 1) * 512], n, None)
-            for n, (r, c) in enumerate(quadrants)
-        ],
+        core, [(512, 512)] * 3, [v], lambda ins, k: [(quadrant(ins, *q), n, None) for n, q in enumerate(quadrants[1:])]
     )
-    zl = {(r, c): _send(piece, TO_ZL) for (r, c), piece in zip(quadrants, pieces)}
+    zl = {(r, c): _send(p, TO_ZL) for (r, c), p in zip(quadrants, [piece, *pieces])}
     other_values = _send(beta_values, TO_CORE)
 
-    out = _gather(alpha_own, (B, 1024), 3, [v], lambda ins, k: [(0, lambda j: ins[0].at[_rows(j)], None)])
+    out = _gather(table, ALPHA_OWN, (B, 1024), 3, [v], lambda ins, k: [[(0, lambda j: ins[0].at[_rows(j)], None)]])
     own = _send_all(out, TO_X)
 
     def early_options(ins, k):
         def of_v(j):
             return ins[0].at[:, _half_rows(k), _rows(j)]
 
-        return [(0, of_v, None), (1, lambda j: ins[1].at[:, :, _rows(j)], None)]
-
-    out = _gather(beta_early, (2, 256, B), EARLY, [v.reshape(2, 512, 1024), x0], early_options)
+        return [[(0, of_v, None), (1, lambda j: ins[1].at[:, :, _rows(j)], None)]]
+
+    out = _gather(table, BETA_LISTS, (2, 256, B), EARLY, [v.reshape(2, 512, 1024), x0], early_options)
     early = _send_all(out, TO_Y)
 
     zh = {(r, c): _send(zl[(r, c)], TO_ZNEXT) for r, c in quadrants}
@@ -409,6 +467,7 @@
     x1, late, x_late = {}, {}, {}
     for r in range(2):
         (half,) = _pick(
+            core,
             [(2, 256, 512)],
             [zl[(r, 0)], zl[(r, 1)]],
             lambda ins, k: [(ins[c].at[_half_rows(1 - k)], 0, c) for c in range(2)],
@@ -416,47 +475,60 @@
         x1[r] = _send(half, TO_CORE)
     for n in range(2):
         out = _gather(
-            alpha_late,
+            table,
+            ALPHA_LATE,
             (B, 512),
             3,
             [zh[(0, n)], zh[(1, n)]],
-            lambda ins, k: [(0, lambda j, i=i: ins[i].at[_rows(j % 4)], i) for i in range(2)],
+            lambda ins, k: [[(0, lambda j, i=i: ins[i].at[_rows(j % 4)], i) for i in range(2)]],
         )
         x_late[n] = _send_all(out, TO_X)
         out = _gather(
-            beta_late, (256, B), LATE, [v, x0, zl[(n, 0)], zl[(n, 1)], x1[n]], lambda ins, k, n=n: _near(n, k, *ins)
+            table,
+            BETA_LISTS + 3 * STARTS[1],
+            (256, B),
+            LATE,
+            [v, x0, zl[(n, 0)], zl[(n, 1)], x1[n]],
+            lambda ins, k, n=n: [_near(n, k, *ins)],
         )
         late[n] = _send_all(out, TO_Y)
 
-    def send_extra():
+    def send_extra(start, slots):
         halves = []
         for r in range(2):
             halves.append(
                 _gather(
-                    beta_extra,
+                    table,
+                    BETA_LISTS + 3 * start,
                     (256, B),
-                    16 - EARLY - LATE,
+                    slots,
                     [v, x0, zl[(r, 0)], zl[(r, 1)], x1[r]],
-                    lambda ins, k, r=r: _near(r, k, *ins),
+                    lambda ins, k, r=r: [_near(r, k, *ins)],
                 )
             )
         return tuple(_send_all([jnp.stack(pair, axis=1) for pair in zip(*halves)], TO_Y))
 
-    def skip_extra():
-        return tuple(jnp.zeros((16 - EARLY - LATE, 2, 256, B), jnp.float32) for _ in HOPS)
-
-    extra = lax.cond(fits, skip_extra, send_extra)
+    def skip_extra(slots):
+        return tuple(jnp.zeros((slots, 2, 256, B), jnp.float32) for _ in HOPS)
+
+    extra = []
+    for start, slots in zip(STARTS[2:], EXTRA):
+        extra += lax.cond(
+            need > start,
+            lambda start=start, slots=slots: send_extra(start, slots),
+            lambda slots=slots: skip_extra(slots),
+        )
 
     ours, theirs = [], []
     for r in range(2):
         a, b = beta_product(
-            r, beta_code, beta_values, other_values, v, x0, zl[(r, 0)], zl[(r, 1)], x1[r], early, late[r], extra
+            r, table, beta_values, other_values, v, x0, zl[(r, 0)], zl[(r, 1)], x1[r], early, late[r], extra
         )
         ours.append(a)
         theirs.append(_send(b, TO_CORE))
-    part = alpha_product(0, alpha_code, alpha_values, v, zh[(0, 0)], zh[(1, 0)], own, x_late[0])
+    part = alpha_product(0, table, alpha_values, v, zh[(0, 0)], zh[(1, 0)], own, x_late[0])
     return alpha_product(
-        1, alpha_code, alpha_values, v, zh[(0, 1)], zh[(1, 1)], own, x_late[1], (part, ours, theirs)
+        1, table, alpha_values, v, zh[(0, 1)], zh[(1, 1)], own, x_late[1], (part, ours, theirs)
     )
 
 
@@ -464,9 +536,10 @@
     row, col = lax.axis_index("row"), lax.axis_index("col")
     x, zh = row // NZH, row % NZH
     zl, y, k = col // (NY * NK), (col // NK) % NY, col % NK
-    alpha = alpha_tables(links_alpha, x, zh)
-    beta = beta_tables(links_beta, zl, y, k)
-    return sigma_here(vector, alpha_values, beta_values, alpha, beta)
+    *beta, need = beta_tables(links_beta, zl, y, k)
+    core = k.reshape(1)
+    table = jnp.concatenate([core, *alpha_tables(links_alpha, x, zh), *beta])
+    return sigma_here(vector, alpha_values, beta_values, core, table, need)
 
 
 def solution(mesh):

time: 339 us -> 398 us (1.17)
  waiting for transfers between devices: 215 us -> 266 us
  starting transfers between devices: 37 us -> 49.2 us
  Pallas kernels: 72.8 us -> 67.8 us
    ppermute x32, waiting for transfers between devices: 215 us -> 266 us  [_send(): return lax.ppermute(value, AXES, pairs)]
    ppermute x32, starting transfers between devices: 37 us -> 49.2 us  [_send(): return lax.ppermute(value, AXES, pairs)]
  transfers between devices with their start and end apart: 32 -> 32, of which waited for: 16 -> 13; matrix products, arithmetic and copies ran while one was open for 3% -> 3% of each run, Pallas kernels for 18% -> 14%
where the time goes in v3:
time: 398 us; the launch traced here: 396 us
  waiting for transfers between devices  266 us (67%)
  Pallas kernels  67.8 us (17%)
  starting transfers between devices  49.2 us (12%)
  local copies, waits for them, and re-layouts  7.92 us (2%)
    ppermute x32, waiting for transfers between devices, _send(): return lax.ppermute(value, AXES, pairs)  266 us
    ppermute x32, starting transfers between devices, _send(): return lax.ppermute(value, AXES, pairs)  49.2 us
    pallas_call x6, Pallas kernels, _gather(): pl.pallas_call(kernel, out_shape=[_f32(slots, *slot_shape)] * 3, in_specs...  25.4 us
    pallas_call x2, Pallas kernels, beta_product(): pl.pallas_call(kernel, out_shape=[_f32(256, 1024)] * 2, in_specs=[SMEM] +...  18.6 us
    pallas_call x2, Pallas kernels, alpha_product(): pl.pallas_call(kernel, out_shape=_f32(1024, width), in_specs=[SMEM] + [AN...  13.6 us
    pallas_call x4, Pallas kernels, _pick(): pl.pallas_call(kernel, out_shape=[_f32(*shape) for shape in shapes], in_s...  10.2 us
  transfers between devices with their start and end apart: 32, of which 13 were waited for; matrix products, arithmetic and copies ran while one was open for 3% of the time, Pallas kernels for 14%

profile of v3, /device:TPU:9, one launch (start us, length us, event | category | flops | bytes accessed | tf_op | source)
XLA Modules:
  0.0 396.1 jit_solution(10294709914646833138)
XLA Ops:
  0.0 2.9 shard_map.55
  3.0 1.7 collective-permute-start.6
  4.7 3.0 shard_map.58
  7.8 1.4 collective-permute-start.18
  9.3 1.5 collective-permute-start.24
  15.3 12.4 %collective-permute-done.6.refs_1_.refs_3_.refs_5_ = f32[512,512]{1,0:T(8,128)} collective-permute-done((f32[512,512]{1,0:T(8,128)}, f32[512,512]{1,0:T(8,128)}, u32[]{:S(2)}, u32[]{:S(2)}) %collective-permute-start.6) | collective-permute-done | bytes 1048608 | tf_op jit(solution)/shard_map/ppermute | solution.py:48
  27.8 22.5 %collective-permute-done.16.refs_0_.refs_2_.refs_4_ = f32[512,512]{1,0:T(8,128)} collective-permute-done((f32[512,512]{1,0:T(8,128)}, f32[512,512]{1,0:T(8,128)}, u32[]{:S(2)}, u32[]{:S(2)}) %collective-permute-start.16) | collective-permute-done | bytes 1048608 | tf_op jit(solution)/shard_map/ppermute | solution.py:48
  50.2 2.1 shard_map.61
  52.4 2.4 collective-permute-start.25
  54.7 18.0 %collective-permute-done.18.refs_0_.refs_2_.refs_4_ = f32[512,512]{1,0:T(8,128)} collective-permute-done((f32[512,512]{1,0:T(8,128)}, f32[512,512]{1,0:T(8,128)}, u32[]{:S(2)}, u32[]{:S(2)}) %collective-permute-start.18) | collective-permute-done | bytes 1048608 | tf_op jit(solution)/shard_map/ppermute | solution.py:48
  72.7 22.5 %collective-permute-done.8.refs_1_.refs_3_.refs_5_ = f32[512,512]{1,0:T(8,128)} collective-permute-done((f32[512,512]{1,0:T(8,128)}, f32[512,512]{1,0:T(8,128)}, u32[]{:S(2)}, u32[]{:S(2)}) %collective-permute-start.8) | collective-permute-done | bytes 1048608 | tf_op jit(solution)/shard_map/ppermute | solution.py:48
  95.2 2.1 shard_map.64
  97.3 1.4 collective-permute-start.32
  100.3 5.1 %shard_map.56 = (f32[3,128,1024]{2,1,0:T(8,128)}, f32[3,128,1024]{2,1,0:T(8,128)}, f32[3,128,1024]{2,1,0:T(8,128)}) custom-call(s32[115]{0:T(128)S(1)} %concatenate.18.table_ref, f32[1024,1024]{1,0:T(8,128)} %refs_0_.17), custom_call_target="tpu_custom_call" | custom-call | bytes 9437184 | tf_op jit(solution)/shard_map/pallas_call | solution.py:206
  105.4 1.5 collective-permute-start.10
  106.9 2.1 collective-permute-start.11
  110.2 3.2 conditional.3
  113.5 2.1 conditional.2
  115.6 1.5 collective-permute-start.12
  118.0 3.7 collective-permute-start.19
  121.7 2.6 collective-permute-start.17
  124.3 3.9 shard_map.66
  128.3 4.1 %shard_map.63 = (f32[6,256,128]{2,1,0:T(8,128)}, f32[6,256,128]{2,1,0:T(8,128)}, f32[6,256,128]{2,1,0:T(8,128)}) custom-call(s32[115]{0:T(128)S(1)} %concatenate.18.table_ref, f32[1024,1024]{1,0:T(8,128)} %refs_0_.17, f32[2,256,1024]{2,1,0:T(8,128)} %collective-permute-done.24.refs_1_.refs_3_, f32[512,512]{1,0:T(8,128)} %collective-permute-done.16.refs_0_.refs_2_.refs_4_, ...), custom_call_target="tpu_custom_call" | custom-call | bytes 4718592 | tf_op jit(solution)/shard_map/pallas_call | solution.py:206
  132.3 10.6 %collective-permute-done.10.refs_3_ = f32[3,128,1024]{2,1,0:T(8,128)} collective-permute-done((f32[3,128,1024]{2,1,0:T(8,128)}, f32[3,128,1024]{2,1,0:T(8,128)}, u32[]{:S(2)}, u32[]{:S(2)}) %collective-permute-start.10) | collective-permute-done | bytes 1572896 | tf_op jit(solution)/shard_map/ppermute | solution.py:48
  144.2 33.2 %collective-permute-done.11.refs_4_ = f32[3,128,1024]{2,1,0:T(8,128)} collective-permute-done((f32[3,128,1024]{2,1,0:T(8,128)}, f32[3,128,1024]{2,1,0:T(8,128)}, u32[]{:S(2)}, u32[]{:S(2)}) %collective-permute-start.11) | collective-permute-done | bytes 1572896 | tf_op jit(solution)/shard_map/ppermute | solution.py:48
  177.4 2.0 collective-permute-start.34
  180.9 4.4 %shard_map.62 = (f32[5,2,256,128]{3,2,1,0:T(8,128)}, f32[5,2,256,128]{3,2,1,0:T(8,128)}, f32[5,2,256,128]{3,2,1,0:T(8,128)}) custom-call(s32[115]{0:T(128)S(1)} %concatenate.18.table_ref, f32[2,512,1024]{2,1,0:T(8,128)} %bitcast.55, f32[2,256,1024]{2,1,0:T(8,128)} %collective-permute-done.24.refs_1_.refs_3_), custom_call_target="tpu_custom_call" | custom-call | bytes 7864320 | tf_op jit(solution)/shard_map/pallas_call | solution.py:206
  185.6 2.8 collective-permute-start.27
  188.5 9.0 %collective-permute-done.34.refs_11_ = f32[6,256,128]{2,1,0:T(8,128)} collective-permute-done((f32[6,256,128]{2,1,0:T(8,128)}, f32[6,256,128]{2,1,0:T(8,128)}, u32[]{:S(2)}, u32[]{:S(2)}) %collective-permute-start.34) | collective-permute-done | bytes 786464 | tf_op jit(solution)/shard_map/ppermute | solution.py:48
  197.7 19.1 %collective-permute-done.35.refs_12_ = f32[6,256,128]{2,1,0:T(8,128)} collective-permute-done((f32[6,256,128]{2,1,0:T(8,128)}, f32[6,256,128]{2,1,0:T(8,128)}, u32[]{:S(2)}, u32[]{:S(2)}) %collective-permute-start.35) | collective-permute-done | bytes 786464 | tf_op jit(solution)/shard_map/ppermute | solution.py:48
  216.8 2.0 collective-permute-start.30
  218.8 68.7 %collective-permute-done.30.refs_11_ = f32[6,256,128]{2,1,0:T(8,128)} collective-permute-done((f32[6,256,128]{2,1,0:T(8,128)}, f32[6,256,128]{2,1,0:T(8,128)}, u32[]{:S(2)}, u32[]{:S(2)}) %collective-permute-start.30) | collective-permute-done | bytes 786464 | tf_op jit(solution)/shard_map/ppermute | solution.py:48
  287.5 4.1 %collective-permute-start.7 = (f32[512,512]{1,0:T(8,128)}, f32[512,512]{1,0:T(8,128)}, u32[]{:S(2)}, u32[]{:S(2)}) collective-permute-start(f32[512,512]{1,0:T(8,128)} %collective-permute-done.6.refs_1_.refs_3_.refs_5_), channel_id=1, source_target_pairs={{0,24},{1,25},{2,26},{3,27},{4,28},{5,29},{6,30},{7,31},{8,16},{9,... | collective-permute-start | bytes 3145736 | tf_op jit(solution)/shard_map/ppermute | solution.py:48
  291.5 13.9 %collective-permute-done.31.refs_12_ = f32[6,256,128]{2,1,0:T(8,128)} collective-permute-done((f32[6,256,128]{2,1,0:T(8,128)}, f32[6,256,128]{2,1,0:T(8,128)}, u32[]{:S(2)}, u32[]{:S(2)}) %collective-permute-start.31) | collective-permute-done | bytes 786464 | tf_op jit(solution)/shard_map/ppermute | solution.py:48
  305.4 4.1 %collective-permute-start.9 = (f32[512,512]{1,0:T(8,128)}, f32[512,512]{1,0:T(8,128)}, u32[]{:S(2)}, u32[]{:S(2)}) collective-permute-start(f32[512,512]{1,0:T(8,128)} %collective-permute-done.8.refs_1_.refs_3_.refs_5_), channel_id=1, source_target_pairs={{0,24},{1,25},{2,26},{3,27},{4,28},{5,29},{6,30},{7,31},{8,16},{9,... | collective-permute-start | bytes 3145736 | tf_op jit(solution)/shard_map/ppermute | solution.py:48
  309.5 3.9 shard_map.59
  313.7 2.5 collective-permute-start.22
  316.2 9.4 %shard_map.67 = (f32[256,1024]{1,0:T(8,128)}, f32[256,1024]{1,0:T(8,128)}) custom-call(s32[115]{0:T(128)S(1)} %concatenate.18.table_ref, f32[8,2,128,128]{3,2,1,0:T(8,128)} %refs_0_.16, f32[8,2,128,128]{3,2,1,0:T(8,128)} %collective-permute-done.23.refs_1_, f32[1024,1024]{1,0:T(8,128)} %refs_0_.17, f32[2,256,1024]{2,1,0:T(8,128)} %collective-permute-done.24.refs_1_.refs_3_, ...), custom_call_target="tpu_custom_call" | custom-call | flops 805306368 | bytes 8388608 | tf_op jit(solution)/shard_map/pallas_call | solution.py:333
  325.6 9.3 %shard_map.65 = (f32[256,1024]{1,0:T(8,128)}, f32[256,1024]{1,0:T(8,128)}) custom-call(s32[115]{0:T(128)S(1)} %concatenate.18.table_ref, f32[8,2,128,128]{3,2,1,0:T(8,128)} %refs_0_.16, f32[8,2,128,128]{3,2,1,0:T(8,128)} %collective-permute-done.23.refs_1_, f32[1024,1024]{1,0:T(8,128)} %refs_0_.17, f32[2,256,1024]{2,1,0:T(8,128)} %collective-permute-done.24.refs_1_.refs_3_, ...), custom_call_target="tpu_custom_call" | custom-call | flops 805306368 | bytes 8388608 | tf_op jit(solution)/shard_map/pallas_call | solution.py:333
  334.9 1.6 collective-permute-start.37
  336.5 1.9 collective-permute-start.36
  338.4 4.0 %shard_map.57 = (f32[3,128,512]{2,1,0:T(8,128)}, f32[3,128,512]{2,1,0:T(8,128)}, f32[3,128,512]{2,1,0:T(8,128)}) custom-call(s32[115]{0:T(128)S(1)} %concatenate.18.table_ref, f32[512,512]{1,0:T(8,128)} %collective-permute-done.7.refs_0_.refs_1_, f32[512,512]{1,0:T(8,128)} %collective-permute-done.9.refs_1_.refs_2_), custom_call_target="tpu_custom_call" | custom-call | bytes 4718592 | tf_op jit(solution)/shard_map/pallas_call | solution.py:206
  342.4 7.8 %collective-permute-done.20.refs_6_ = f32[3,128,512]{2,1,0:T(8,128)} collective-permute-done((f32[3,128,512]{2,1,0:T(8,128)}, f32[3,128,512]{2,1,0:T(8,128)}, u32[]{:S(2)}, u32[]{:S(2)}) %collective-permute-start.20) | collective-permute-done | bytes 786464 | tf_op jit(solution)/shard_map/ppermute | solution.py:48
  350.8 3.0 collective-permute-start.15
  353.9 5.2 %shard_map.60.refs_9_ = f32[1024,512]{1,0:T(8,128)} custom-call(s32[115]{0:T(128)S(1)} %concatenate.18.table_ref, f32[8,2,128,128]{3,2,1,0:T(8,128)} %weights.3, f32[1024,1024]{1,0:T(8,128)} %refs_0_.17, f32[512,512]{1,0:T(8,128)} %collective-permute-done.17.refs_0_.refs_1_, f32[512,512]{1,0:T(8,128)} %collective-permute-done.19.refs_1_.refs_2_, ...), custom_call_target="tpu_custom_call" | custom-call | flops 805306368 | bytes 7340032 | tf_op jit(solution)/shard_map/pallas_call | solution.py:423
  359.0 26.9 %collective-permute-done.13.refs_6_ = f32[3,128,512]{2,1,0:T(8,128)S(1)} collective-permute-done((f32[3,128,512]{2,1,0:T(8,128)}, f32[3,128,512]{2,1,0:T(8,128)S(1)}, u32[]{:S(2)}, u32[]{:S(2)}) %collective-permute-start.13) | collective-permute-done | bytes 786464 | tf_op jit(solution)/shard_map/ppermute | solution.py:48
  385.9 1.7 collective-permute-done.15.refs_8_
  387.6 8.4 %shard_map.68 = f32[1024,1024]{1,0:T(8,128)} custom-call(s32[115]{0:T(128)S(1)} %concatenate.18.table_ref, f32[8,2,128,128]{3,2,1,0:T(8,128)} %weights.3, f32[1024,1024]{1,0:T(8,128)} %refs_0_.17, f32[512,512]{1,0:T(8,128)} %collective-permute-done.7.refs_0_.refs_1_, f32[512,512]{1,0:T(8,128)} %collective-permute-done.9.refs_1_.refs_2_, ...), custom_call_target="tpu_custom_call" | custom-call | flops 805306368 | bytes 15728640 | tf_op jit(solution)/shard_map/pallas_call | solution.py:423
  (114 shorter events, 16.3 us)
Async XLA Ops:
  2.9 7.9 %copy-start.10 = (s32[128,2]{0,1:T(2,128)S(1)}, s32[128,2]{0,1:T(2,128)}, u32[]{:S(2)}) copy-start(s32[128,2]{0,1:T(2,128)} %param.12) | copy-start | bytes 3076
  3.0 11.0 %copy-start.11 = (s32[64,2]{0,1:T(2,128)S(1)}, s32[64,2]{0,1:T(2,128)}, u32[]{:S(2)}) copy-start(s32[64,2]{0,1:T(2,128)} %param.10) | copy-start | bytes 1540
  3.0 24.8 %collective-permute-start.6 = (f32[512,512]{1,0:T(8,128)}, f32[512,512]{1,0:T(8,128)}, u32[]{:S(2)}, u32[]{:S(2)}) collective-permute-start(f32[512,512]{1,0:T(8,128)} %get-tuple-element.104), channel_id=1, source_target_pairs={{0,8},{1,9},{2,10},{3,11},{4,12},{5,13},{6,14},{7,15},{8,0},{9,1},... | collective-permute-start | bytes 3145736 | tf_op jit(solution)/shard_map/ppermute | solution.py:48
  7.7 42.5 %collective-permute-start.16 = (f32[512,512]{1,0:T(8,128)}, f32[512,512]{1,0:T(8,128)}, u32[]{:S(2)}, u32[]{:S(2)}) collective-permute-start(f32[512,512]{1,0:T(8,128)} %get-tuple-element.112), channel_id=1, source_target_pairs={{0,8},{1,9},{2,10},{3,11},{4,12},{5,13},{6,14},{7,15},{8,0},{9,1},... | collective-permute-start | bytes 3145736 | tf_op jit(solution)/shard_map/ppermute | solution.py:48
  7.8 64.9 %collective-permute-start.18 = (f32[512,512]{1,0:T(8,128)}, f32[512,512]{1,0:T(8,128)}, u32[]{:S(2)}, u32[]{:S(2)}) collective-permute-start(f32[512,512]{1,0:T(8,128)} %get-tuple-element.113), channel_id=1, source_target_pairs={{0,8},{1,9},{2,10},{3,11},{4,12},{5,13},{6,14},{7,15},{8,0},{9,1},... | collective-permute-start | bytes 3145736 | tf_op jit(solution)/shard_map/ppermute | solution.py:48
  9.2 85.9 %collective-permute-start.8 = (f32[512,512]{1,0:T(8,128)}, f32[512,512]{1,0:T(8,128)}, u32[]{:S(2)}, u32[]{:S(2)}) collective-permute-start(f32[512,512]{1,0:T(8,128)} %get-tuple-element.105), channel_id=1, source_target_pairs={{0,8},{1,9},{2,10},{3,11},{4,12},{5,13},{6,14},{7,15},{8,0},{9,1},... | collective-permute-start | bytes 3145736 | tf_op jit(solution)/shard_map/ppermute | solution.py:48
  9.3 100.9 %collective-permute-start.24 = (f32[2,256,1024]{2,1,0:T(8,128)}, f32[2,256,1024]{2,1,0:T(8,128)}, u32[]{:S(2)}, u32[]{:S(2)}) collective-permute-start(f32[2,256,1024]{2,1,0:T(8,128)} %get-tuple-element.117), channel_id=1, source_target_pairs={{0,1},{1,0},{2,3},{3,2},{4,5},{5,4},{6,7},{7,6},{8,9},{9,8},{10,11... | collective-permute-start | bytes 6291464 | tf_op jit(solution)/shard_map/ppermute | solution.py:48
  52.4 57.8 %collective-permute-start.25 = (f32[2,256,512]{2,1,0:T(8,128)}, f32[2,256,512]{2,1,0:T(8,128)}, u32[]{:S(2)}, u32[]{:S(2)}) collective-permute-start(f32[2,256,512]{2,1,0:T(8,128)} %shard_map.61), channel_id=1, source_target_pairs={{0,1},{1,0},{2,3},{3,2},{4,5},{5,4},{6,7},{7,6},{8,9},{9,8},{10,11... | collective-permute-start | bytes 3145736 | tf_op jit(solution)/shard_map/ppermute | solution.py:48
  97.3 12.9 %collective-permute-start.32 = (f32[2,256,512]{2,1,0:T(8,128)}, f32[2,256,512]{2,1,0:T(8,128)}, u32[]{:S(2)}, u32[]{:S(2)}) collective-permute-start(f32[2,256,512]{2,1,0:T(8,128)} %shard_map.64), channel_id=1, source_target_pairs={{0,1},{1,0},{2,3},{3,2},{4,5},{5,4},{6,7},{7,6},{8,9},{9,8},{10,11... | collective-permute-start | bytes 3145736 | tf_op jit(solution)/shard_map/ppermute | solution.py:48
  105.4 37.5 %collective-permute-start.10 = (f32[3,128,1024]{2,1,0:T(8,128)}, f32[3,128,1024]{2,1,0:T(8,128)}, u32[]{:S(2)}, u32[]{:S(2)}) collective-permute-start(f32[3,128,1024]{2,1,0:T(8,128)} %get-tuple-element.106), channel_id=1, source_target_pairs={{0,32},{1,33},{2,34},{3,35},{4,36},{5,37},{6,38},{7,39},{8,40},{9,... | collective-permute-start | bytes 4718600 | tf_op jit(solution)/shard_map/ppermute | solution.py:48
  106.9 70.5 %collective-permute-start.11 = (f32[3,128,1024]{2,1,0:T(8,128)}, f32[3,128,1024]{2,1,0:T(8,128)}, u32[]{:S(2)}, u32[]{:S(2)}) collective-permute-start(f32[3,128,1024]{2,1,0:T(8,128)} %get-tuple-element.107), channel_id=1, source_target_pairs={{0,64},{1,65},{2,66},{3,67},{4,68},{5,69},{6,70},{7,71},{8,72},{9,... | collective-permute-start | bytes 4718600 | tf_op jit(solution)/shard_map/ppermute | solution.py:48
  115.6 63.8 %collective-permute-start.12 = (f32[3,128,1024]{2,1,0:T(8,128)}, f32[3,128,1024]{2,1,0:T(8,128)}, u32[]{:S(2)}, u32[]{:S(2)}) collective-permute-start(f32[3,128,1024]{2,1,0:T(8,128)} %get-tuple-element.108), channel_id=1, source_target_pairs={{0,96},{1,97},{2,98},{3,99},{4,100},{5,101},{6,102},{7,103},{8,104... | collective-permute-start | bytes 4718600 | tf_op jit(solution)/shard_map/ppermute | solution.py:48
  117.1 4.6 %collective-permute-start.23 = (f32[8,2,128,128]{3,2,1,0:T(8,128)}, f32[8,2,128,128]{3,2,1,0:T(8,128)}, u32[]{:S(2)}, u32[]{:S(2)}) collective-permute-start(f32[8,2,128,128]{3,2,1,0:T(8,128)} %refs_0_.16), channel_id=1, source_target_pairs={{0,1},{1,0},{2,3},{3,2},{4,5},{5,4},{6,7},{7,6},{8,9},{9,8},{10,11... | collective-permute-start | bytes 3145736 | tf_op jit(solution)/shard_map/ppermute | solution.py:48
  118.0 62.5 %collective-permute-start.19 = (f32[512,512]{1,0:T(8,128)}, f32[512,512]{1,0:T(8,128)}, u32[]{:S(2)}, u32[]{:S(2)}) collective-permute-start(f32[512,512]{1,0:T(8,128)} %collective-permute-done.18.refs_0_.refs_2_.refs_4_), channel_id=1, source_target_pairs={{0,24},{1,25},{2,26},{3,27},{4,28},{5,29},{6,30},{7,31},{8,16},{9,... | collective-permute-start | bytes 3145736 | tf_op jit(solution)/shard_map/ppermute | solution.py:48
  121.7 63.7 %collective-permute-start.17 = (f32[512,512]{1,0:T(8,128)}, f32[512,512]{1,0:T(8,128)}, u32[]{:S(2)}, u32[]{:S(2)}) collective-permute-start(f32[512,512]{1,0:T(8,128)} %collective-permute-done.16.refs_0_.refs_2_.refs_4_), channel_id=1, source_target_pairs={{0,24},{1,25},{2,26},{3,27},{4,28},{5,29},{6,30},{7,31},{8,16},{9,... | collective-permute-start | bytes 3145736 | tf_op jit(solution)/shard_map/ppermute | solution.py:48
  142.9 42.7 %collective-permute-start.33 = (f32[6,256,128]{2,1,0:T(8,128)}, f32[6,256,128]{2,1,0:T(8,128)S(1)}, u32[]{:S(2)}, u32[]{:S(2)}) collective-permute-start(f32[6,256,128]{2,1,0:T(8,128)} %get-tuple-element.131), channel_id=1, source_target_pairs={{0,2},{1,3},{2,4},{3,5},{4,6},{5,7},{6,0},{7,1},{8,10},{9,11},{10,... | collective-permute-start | bytes 2359304 | tf_op jit(solution)/shard_map/ppermute | solution.py:48
  177.4 20.1 %collective-permute-start.34 = (f32[6,256,128]{2,1,0:T(8,128)}, f32[6,256,128]{2,1,0:T(8,128)}, u32[]{:S(2)}, u32[]{:S(2)}) collective-permute-start(f32[6,256,128]{2,1,0:T(8,128)} %get-tuple-element.132), channel_id=1, source_target_pairs={{0,4},{1,5},{2,6},{3,7},{4,0},{5,1},{6,2},{7,3},{8,12},{9,13},{10,... | collective-permute-start | bytes 2359304 | tf_op jit(solution)/shard_map/ppermute | solution.py:48
  179.4 37.3 %collective-permute-start.35 = (f32[6,256,128]{2,1,0:T(8,128)}, f32[6,256,128]{2,1,0:T(8,128)}, u32[]{:S(2)}, u32[]{:S(2)}) collective-permute-start(f32[6,256,128]{2,1,0:T(8,128)} %get-tuple-element.133), channel_id=1, source_target_pairs={{0,6},{1,7},{2,0},{3,1},{4,2},{5,3},{6,4},{7,5},{8,14},{9,15},{10,... | collective-permute-start | bytes 2359304 | tf_op jit(solution)/shard_map/ppermute | solution.py:48
  180.5 38.3 %collective-permute-start.29 = (f32[6,256,128]{2,1,0:T(8,128)}, f32[6,256,128]{2,1,0:T(8,128)}, u32[]{:S(2)}, u32[]{:S(2)}) collective-permute-start(f32[6,256,128]{2,1,0:T(8,128)} %get-tuple-element.121), channel_id=1, source_target_pairs={{0,2},{1,3},{2,4},{3,5},{4,6},{5,7},{6,0},{7,1},{8,10},{9,11},{10,... | collective-permute-start | bytes 2359304 | tf_op jit(solution)/shard_map/ppermute | solution.py:48
  185.3 128.1 %collective-permute-start.26 = (f32[5,2,256,128]{3,2,1,0:T(8,128)}, f32[5,2,256,128]{3,2,1,0:T(8,128)}, u32[]{:S(2)}, u32[]{:S(2)}) collective-permute-start(f32[5,2,256,128]{3,2,1,0:T(8,128)} %get-tuple-element.118), channel_id=1, source_target_pairs={{0,2},{1,3},{2,4},{3,5},{4,6},{5,7},{6,0},{7,1},{8,10},{9,11},{10,... | collective-permute-start | bytes 3932168 | tf_op jit(solution)/shard_map/ppermute | solution.py:48
  185.6 130.6 %copy-start = (f32[6,256,128]{2,1,0:T(8,128)}, f32[6,256,128]{2,1,0:T(8,128)S(1)}, u32[]{:S(2)}) copy-start(f32[6,256,128]{2,1,0:T(8,128)S(1)} %collective-permute-done.33.refs_10_) | copy-start | bytes 2359300
  185.6 127.9 %collective-permute-start.27 = (f32[5,2,256,128]{3,2,1,0:T(8,128)}, f32[5,2,256,128]{3,2,1,0:T(8,128)}, u32[]{:S(2)}, u32[]{:S(2)}) collective-permute-start(f32[5,2,256,128]{3,2,1,0:T(8,128)} %get-tuple-element.119), channel_id=1, source_target_pairs={{0,4},{1,5},{2,6},{3,7},{4,0},{5,1},{6,2},{7,3},{8,12},{9,13},{10,... | collective-permute-start | bytes 3932168 | tf_op jit(solution)/shard_map/ppermute | solution.py:48
  197.5 116.2 %collective-permute-start.28 = (f32[5,2,256,128]{3,2,1,0:T(8,128)}, f32[5,2,256,128]{3,2,1,0:T(8,128)}, u32[]{:S(2)}, u32[]{:S(2)}) collective-permute-start(f32[5,2,256,128]{3,2,1,0:T(8,128)} %get-tuple-element.120), channel_id=1, source_target_pairs={{0,6},{1,7},{2,0},{3,1},{4,2},{5,3},{6,4},{7,5},{8,14},{9,15},{10,... | collective-permute-start | bytes 3932168 | tf_op jit(solution)/shard_map/ppermute | solution.py:48
  216.8 70.7 %collective-permute-start.30 = (f32[6,256,128]{2,1,0:T(8,128)}, f32[6,256,128]{2,1,0:T(8,128)}, u32[]{:S(2)}, u32[]{:S(2)}) collective-permute-start(f32[6,256,128]{2,1,0:T(8,128)} %get-tuple-element.122), channel_id=1, source_target_pairs={{0,4},{1,5},{2,6},{3,7},{4,0},{5,1},{6,2},{7,3},{8,12},{9,13},{10,... | collective-permute-start | bytes 2359304 | tf_op jit(solution)/shard_map/ppermute | solution.py:48
  218.8 86.7 %collective-permute-start.31 = (f32[6,256,128]{2,1,0:T(8,128)}, f32[6,256,128]{2,1,0:T(8,128)}, u32[]{:S(2)}, u32[]{:S(2)}) collective-permute-start(f32[6,256,128]{2,1,0:T(8,128)} %get-tuple-element.123), channel_id=1, source_target_pairs={{0,6},{1,7},{2,0},{3,1},{4,2},{5,3},{6,4},{7,5},{8,14},{9,15},{10,... | collective-permute-start | bytes 2359304 | tf_op jit(solution)/shard_map/ppermute | solution.py:48
  287.5 47.4 %collective-permute-start.7 = (f32[512,512]{1,0:T(8,128)}, f32[512,512]{1,0:T(8,128)}, u32[]{:S(2)}, u32[]{:S(2)}) collective-permute-start(f32[512,512]{1,0:T(8,128)} %collective-permute-done.6.refs_1_.refs_3_.refs_5_), channel_id=1, source_target_pairs={{0,24},{1,25},{2,26},{3,27},{4,28},{5,29},{6,30},{7,31},{8,16},{9,... | collective-permute-start | bytes 3145736 | tf_op jit(solution)/shard_map/ppermute | solution.py:48
  305.4 31.1 %collective-permute-start.9 = (f32[512,512]{1,0:T(8,128)}, f32[512,512]{1,0:T(8,128)}, u32[]{:S(2)}, u32[]{:S(2)}) collective-permute-start(f32[512,512]{1,0:T(8,128)} %collective-permute-done.8.refs_1_.refs_3_.refs_5_), channel_id=1, source_target_pairs={{0,24},{1,25},{2,26},{3,27},{4,28},{5,29},{6,30},{7,31},{8,16},{9,... | collective-permute-start | bytes 3145736 | tf_op jit(solution)/shard_map/ppermute | solution.py:48
  313.4 36.8 %collective-permute-start.20 = (f32[3,128,512]{2,1,0:T(8,128)}, f32[3,128,512]{2,1,0:T(8,128)}, u32[]{:S(2)}, u32[]{:S(2)}) collective-permute-start(f32[3,128,512]{2,1,0:T(8,128)} %get-tuple-element.114), channel_id=1, source_target_pairs={{0,32},{1,33},{2,34},{3,35},{4,36},{5,37},{6,38},{7,39},{8,40},{9,... | collective-permute-start | bytes 2359304 | tf_op jit(solution)/shard_map/ppermute | solution.py:48
  313.5 36.7 %collective-permute-start.21 = (f32[3,128,512]{2,1,0:T(8,128)}, f32[3,128,512]{2,1,0:T(8,128)}, u32[]{:S(2)}, u32[]{:S(2)}) collective-permute-start(f32[3,128,512]{2,1,0:T(8,128)} %get-tuple-element.115), channel_id=1, source_target_pairs={{0,64},{1,65},{2,66},{3,67},{4,68},{5,69},{6,70},{7,71},{8,72},{9,... | collective-permute-start | bytes 2359304 | tf_op jit(solution)/shard_map/ppermute | solution.py:48
  313.7 37.1 %collective-permute-start.22 = (f32[3,128,512]{2,1,0:T(8,128)}, f32[3,128,512]{2,1,0:T(8,128)}, u32[]{:S(2)}, u32[]{:S(2)}) collective-permute-start(f32[3,128,512]{2,1,0:T(8,128)} %get-tuple-element.116), channel_id=1, source_target_pairs={{0,96},{1,97},{2,98},{3,99},{4,100},{5,101},{6,102},{7,103},{8,104... | collective-permute-start | bytes 2359304 | tf_op jit(solution)/shard_map/ppermute | solution.py:48
  334.9 52.7 %collective-permute-start.37 = (f32[256,1024]{1,0:T(8,128)}, f32[256,1024]{1,0:T(8,128)}, u32[]{:S(2)}, u32[]{:S(2)}) collective-permute-start(f32[256,1024]{1,0:T(8,128)} %get-tuple-element.136), channel_id=1, source_target_pairs={{0,1},{1,0},{2,3},{3,2},{4,5},{5,4},{6,7},{7,6},{8,9},{9,8},{10,11... | collective-permute-start | bytes 3145736 | tf_op jit(solution)/shard_map/ppermute | solution.py:48
  336.5 51.1 %collective-permute-start.36 = (f32[256,1024]{1,0:T(8,128)}, f32[256,1024]{1,0:T(8,128)}, u32[]{:S(2)}, u32[]{:S(2)}) collective-permute-start(f32[256,1024]{1,0:T(8,128)} %get-tuple-element.135), channel_id=1, source_target_pairs={{0,1},{1,0},{2,3},{3,2},{4,5},{5,4},{6,7},{7,6},{8,9},{9,8},{10,11... | collective-permute-start | bytes 3145736 | tf_op jit(solution)/shard_map/ppermute | solution.py:48
  350.2 35.7 %collective-permute-start.13 = (f32[3,128,512]{2,1,0:T(8,128)}, f32[3,128,512]{2,1,0:T(8,128)S(1)}, u32[]{:S(2)}, u32[]{:S(2)}) collective-permute-start(f32[3,128,512]{2,1,0:T(8,128)} %get-tuple-element.109), channel_id=1, source_target_pairs={{0,32},{1,33},{2,34},{3,35},{4,36},{5,37},{6,38},{7,39},{8,40},{9,... | collective-permute-start | bytes 2359304 | tf_op jit(solution)/shard_map/ppermute | solution.py:48
  350.2 35.7 %collective-permute-start.14 = (f32[3,128,512]{2,1,0:T(8,128)}, f32[3,128,512]{2,1,0:T(8,128)}, u32[]{:S(2)}, u32[]{:S(2)}) collective-permute-start(f32[3,128,512]{2,1,0:T(8,128)} %get-tuple-element.110), channel_id=1, source_target_pairs={{0,64},{1,65},{2,66},{3,67},{4,68},{5,69},{6,70},{7,71},{8,72},{9,... | collective-permute-start | bytes 2359304 | tf_op jit(solution)/shard_map/ppermute | solution.py:48
  350.8 36.8 %collective-permute-start.15 = (f32[3,128,512]{2,1,0:T(8,128)}, f32[3,128,512]{2,1,0:T(8,128)}, u32[]{:S(2)}, u32[]{:S(2)}) collective-permute-start(f32[3,128,512]{2,1,0:T(8,128)} %get-tuple-element.111), channel_id=1, source_target_pairs={{0,96},{1,97},{2,98},{3,99},{4,100},{5,101},{6,102},{7,103},{8,104... | collective-permute-start | bytes 2359304 | tf_op jit(solution)/shard_map/ppermute | solution.py:48
  385.9 1.7 copy-start.1

commit v4 on v3

v4 whole, which is shorter than its diff:
```python
import jax
import jax.numpy as jnp
from jax import lax
from jax.experimental import pallas as pl
from jax.experimental.pallas import tpu as pltpu
from jax.sharding import PartitionSpec as P


B = 128
AXES = ("row", "col")
HOPS = (1, 2, 3)
STARTS, SLOTS = (0, 5, 11, 12), (5, 6, 1, 4)
EARLY, LATE, *EXTRA = SLOTS
ALPHA_ROW, BETA_ROW, CORE, NEED = 3, 7, 126, 127
NX, NZH, NZL, NY, NK = 4, 2, 2, 4, 2


def _index(x, zh, zl, y, k):
    return (x * NZH + zh) * (NZL * NY * NK) + (zl * NY + y) * NK + k


def _pairs(move):
    pairs = []
    for x in range(NX):
        for zh in range(NZH):
            for zl in range(NZL):
                for y in range(NY):
                    for k in range(NK):
                        here = (x, zh, zl, y, k)
                        pairs.append((_index(*here), _index(*move(*here))))
    return pairs


def _z_next(x, zh, zl, y, k):
    z = (2 * zh + zl + (1 if zl == 1 else -1)) % 4
    return (x, z // 2, z % 2, y, k)


TO_CORE = _pairs(lambda x, zh, zl, y, k: (x, zh, zl, y, 1 - k))
TO_ZL = _pairs(lambda x, zh, zl, y, k: (x, zh, 1 - zl, y, k))
TO_ZNEXT = _pairs(_z_next)
TO_X = {d: _pairs(lambda x, zh, zl, y, k, d=d: ((x + d) % NX, zh, zl, y, k)) for d in HOPS}
TO_Y = {d: _pairs(lambda x, zh, zl, y, k, d=d: (x, zh, zl, (y + d) % NY, k)) for d in HOPS}


def _send(value, pairs):
    return lax.ppermute(value, AXES, pairs)


def _send_all(payloads, routes):
    return [_send(value, routes[d]) for d, value in zip(HOPS, payloads)]


def _row_sum(v):
    return jnp.sum(v.astype(jnp.float32), axis=1, keepdims=True).astype(jnp.int32)


def _members(entries, count, lane):
    member = jnp.zeros((8, 128), jnp.int32)
    for n in range(count):
        member = jnp.where(entries[:, n : n + 1] == lane, 1, member)
    return member


def _ranks(member, group, lane):
    ahead, total, step = member, member, 1
    while step < group:
        ahead = ahead + jnp.where((lane & (group - 1)) >= step, pltpu.roll(ahead, step, 1), 0)
        total = total + jnp.where((lane & step) > 0, pltpu.roll(total, step, 1), pltpu.roll(total, 128 - step, 1))
        step *= 2
    return ahead - member, total


def _lookup(codes, entries):
    return jnp.take_along_axis(codes, entries, axis=1)


def _position():
    row, col = lax.axis_index("row"), lax.axis_index("col")
    return row >> 1, row & 1, col >> 3, (col >> 1) & 3, col & 1


def _tables(alpha_ref, beta_ref, out_ref, pad_ref):
    x, zh, zl, y, k = _position()
    lane = lax.broadcasted_iota(jnp.int32, (8, 128), 1)
    row = lax.broadcasted_iota(jnp.int32, (8, 128), 0)

    pad_ref[...] = jnp.zeros_like(pad_ref)
    pad_ref[0, :, 0:32] = beta_ref[...]
    pad_ref[1, :, 0:16] = alpha_ref[...]
    wanted = pad_ref[0]
    member = _members(wanted, 32, lane)
    rank, total = _ranks(member, 16, lane)
    source_y = (lane >> 4) & 3
    other = (lane >> 6) ^ (row >> 2)
    near = (other * 2 + (((lane >> 3) & 1) ^ k)) * 32 + (lane & 7)
    pos = jnp.where(other == 1, jnp.maximum(pltpu.roll(total, 64, 1), EARLY) + rank, rank)
    hop = ((row & 3) - source_y) & 3
    reach = jnp.where((hop > 0) & (member > 0), pos + 1, 0).astype(jnp.float32)
    need = jnp.max(jnp.max(reach, axis=1, keepdims=True), axis=0, keepdims=True).astype(jnp.int32)
    level, at = jnp.zeros_like(pos), pos
    for before, start in zip(STARTS, STARTS[1:]):
        level = level + jnp.where(pos >= start, 1, 0)
        at = at - jnp.where(pos >= start, start - before, 0)
    beta_codes = _lookup(jnp.where(hop == 0, near, (3 + hop + 3 * level) * 32 + at), wanted)
    sent = jnp.where((member > 0) & (source_y == y), pos, -1)
    beta_lists = jnp.zeros_like(pos)
    for n in range(16):
        beta_lists = jnp.where(lane == n, _row_sum(jnp.where(sent == n, near, 0)), beta_lists)

    wanted = pad_ref[1]
    member = _members(wanted, 16, lane)
    rank, _ = _ranks(member, 8, lane)
    other = ((lane >> 3) & 1) ^ (row & 1)
    hop = ((row >> 1) - (lane >> 4)) & 3
    alpha_codes = _lookup(jnp.where(hop == 0, other * 32 + (lane & 7), (1 + hop + 3 * other) * 32 + rank), wanted)
    sent = jnp.where((member > 0) & ((lane >> 4) == x), rank + 3 * other, -1)
    alpha_lists = jnp.zeros_like(pos)
    for n in range(6):
        alpha_lists = jnp.where(lane == n, _row_sum(jnp.where(sent == n, lane & 7, 0)), alpha_lists)

    def pick(v, at):
        return jnp.sum(jnp.where(row == at, v, 0).astype(jnp.float32), axis=0, keepdims=True).astype(jnp.int32)

    for n, hop in enumerate(HOPS):
        out_ref[n : n + 1] = pick(alpha_lists, ((x + hop) & 3) * 2 + zh)
        out_ref[4 + n : 5 + n] = pick(beta_lists, zl * 4 + ((y + hop) & 3))
    codes = pick(alpha_codes, x * 2 + zh)
    codes = jnp.where(lane[0:1] == NEED, need, codes)
    out_ref[ALPHA_ROW : ALPHA_ROW + 1] = jnp.where(lane[0:1] == CORE, k, codes)
    out_ref[BETA_ROW : BETA_ROW + 1] = pick(beta_codes, zl * 4 + y)


def route_table(links_alpha, links_beta):
    return pl.pallas_call(
        _tables,
        name="route_table",
        out_shape=jax.ShapeDtypeStruct((8, 128), jnp.int32),
        in_specs=[VMEM, VMEM],
        out_specs=VMEM,
        scratch_shapes=[pltpu.VMEM((2, 8, 128), jnp.int32)],
        compiler_params=_params(),
        cost_estimate=_cost(12288),
    )(links_alpha.reshape(8, 16), links_beta.reshape(8, 32))


def _rows(i):
    return pl.ds(pl.multiple_of(i * B, B), B)


def _fetch(code, options, dst, sem):
    place, at = code >> 5, code & 31
    for group in options:
        first, last = group[0][0], group[-1][0]

        @pl.when(jnp.logical_and(place >= first, place <= last))
        def _(group=group):
            for number, source, half in group:
                test = place == number
                if half is not None:
                    test = jnp.logical_and(test, (at >> 2) == half)

                @pl.when(test)
                def _(source=source):
                    pltpu.make_async_copy(source(at), dst, sem).start()


def _wait(ref, sem):
    pltpu.make_async_copy(ref, ref, sem).wait()


ANY = pl.BlockSpec(memory_space=pl.ANY)
SMEM = pl.BlockSpec(memory_space=pltpu.SMEM)
VMEM = pl.BlockSpec(memory_space=pltpu.VMEM)


def _f32(*shape):
    return jax.ShapeDtypeStruct(shape, jnp.float32)


def _params():
    return pltpu.CompilerParams(vmem_limit_bytes=63 * 2**20)


def _cost(bytes_, flops=0):
    return pl.CostEstimate(flops=flops, bytes_accessed=bytes_, transcendentals=0)


def _gather(table, first_row, start, slot_shape, slots, sources, options_of):
    count = 3 * slots

    def kernel(table_ref, *refs):
        ins, outs = refs[: len(sources)], refs[len(sources) : len(sources) + 3]
        buf, in_sem, out_sem = refs[len(sources) + 3 :]
        options = options_of(ins, table_ref[ALPHA_ROW, CORE])

        for hop in range(3):

            def load(s, _, hop=hop):
                n = hop * slots + s
                _fetch(table_ref[first_row + hop, start + s], options, buf.at[n], in_sem.at[n])

            lax.fori_loop(0, slots, load, None)
        for hop, out in enumerate(outs):

            def store(s, _, hop=hop, out=out):
                n = hop * slots + s
                _wait(buf.at[n], in_sem.at[n])
                pltpu.make_async_copy(buf.at[n], out.at[s], out_sem.at[n]).start()

            lax.fori_loop(0, slots, store, None)

        def finish(s, _):
            _wait(buf.at[s], out_sem.at[s])

        lax.fori_loop(0, count, finish, None)

    size = 4 * count
    for n in slot_shape:
        size *= n
    return pl.pallas_call(
        kernel,
        out_shape=[_f32(slots, *slot_shape)] * 3,
        in_specs=[SMEM] + [ANY] * len(sources),
        out_specs=[ANY] * 3,
        scratch_shapes=[
            pltpu.VMEM((count, *slot_shape), jnp.float32),
            pltpu.SemaphoreType.DMA((count,)),
            pltpu.SemaphoreType.DMA((count,)),
        ],
        compiler_params=_params(),
        cost_estimate=_cost(2 * size),
    )(table, *sources)


def _pick(shapes, sources, picks_of):
    def kernel(*refs):
        ins, outs = refs[: len(sources)], refs[len(sources) : len(sources) + len(shapes)]
        bufs = refs[len(sources) + len(shapes) : -2]
        in_sem, out_sem = refs[-2:]
        loads, stores = [], []
        for n, (source, number, at) in enumerate(picks_of(ins, _position()[4])):
            buf, out = bufs[number], outs[number]
            if at is not None:
                buf, out = buf.at[at], out.at[at]
            loads.append(pltpu.make_async_copy(source, buf, in_sem.at[n]))
            stores.append(pltpu.make_async_copy(buf, out, out_sem.at[n]))
        for copy in loads:
            copy.start()
        for load, store in zip(loads, stores):
            load.wait()
            store.start()
        for copy in stores:
            copy.wait()

    size = 0
    for shape in shapes:
        words = 1
        for n in shape:
            words *= n
        size += 8 * words
    return pl.pallas_call(
        kernel,
        out_shape=[_f32(*shape) for shape in shapes],
        in_specs=[ANY] * len(sources),
        out_specs=[ANY] * len(shapes),
        scratch_shapes=[pltpu.VMEM(shape, jnp.float32) for shape in shapes]
        + [pltpu.SemaphoreType.DMA((6,)), pltpu.SemaphoreType.DMA((6,))],
        compiler_params=_params(),
        cost_estimate=_cost(size),
    )(*sources)


def _split(v):
    high = v.astype(jnp.bfloat16)
    return high, (v - high.astype(jnp.float32)).astype(jnp.bfloat16)


def _dot3(a, b, dims):
    (da,), (db,) = dims
    ah, al = _split(a)
    bh, bl = _split(b)
    left, right = jnp.concatenate([al, ah, ah], axis=da), jnp.concatenate([bh, bl, bh], axis=db)
    return lax.dot_general(left, right, (dims, ((), ())), preferred_element_type=jnp.float32)


def _my_rows(r, k):
    return pl.ds(pl.multiple_of(r * 512 + k * 256, 256), 256)


def _half_rows(k):
    return pl.ds(pl.multiple_of(k * 256, 256), 256)


def _near(r, k, v, x0, q0, q1, x1):
    return [
        (0, lambda j: v.at[_my_rows(r, k), _rows(j)], None),
        (1, lambda j: x0.at[r, :, _rows(j)], None),
        (2, lambda j: q0.at[_half_rows(k), _rows(j & 3)], 0),
        (2, lambda j: q1.at[_half_rows(k), _rows(j & 3)], 1),
        (3, lambda j: x1.at[j >> 2, :, _rows(j & 3)], None),
    ]


def beta_product(r, table, mine, other, v, x0, q0, q1, x1, early, late, extra):
    def kernel(table_ref, *refs):
        weights, ins, outs = refs[0:2], refs[2:-8], refs[-8:-6]
        buf, w_buf, out_buf, sem, w_sem, out_sem = refs[-6:]
        k = table_ref[ALPHA_ROW, CORE]
        loads = [pltpu.make_async_copy(weights[i], w_buf.at[i], w_sem.at[i]) for i in range(2)]
        for copy in loads:
            copy.start()
        options = [
            _near(r, k, *ins[0:5]),
            [(4 + i, lambda s, i=i: ins[5 + i].at[s, r], None) for i in range(3)],
            [(7 + i, lambda s, i=i: ins[8 + i].at[s], None) for i in range(3)],
        ]
        for n in range(len(EXTRA)):
            options.append([(10 + i, lambda s, i=i: ins[11 + i].at[s, r], None) for i in range(3 * n, 3 * n + 3)])

        def load(n, _=None):
            _fetch(table_ref[BETA_ROW, (n + 16 * k) & 31], options, buf.at[n], sem.at[n])

        lax.fori_loop(0, 16, load, None)
        for copy in loads:
            copy.wait()
        stores = []
        for part in range(4):
            i = part >> 1
            for n in range(8 * part, 8 * part + 8):
                _wait(buf.at[n], sem.at[n])
            for h in range(4 * part, 4 * part + 4):
                n = 2 * h
                if n < 16:
                    load(n + 16)
                    load(n + 17)
                w = jnp.concatenate([w_buf[i, h & 7, 0], w_buf[i, h & 7, 1]], axis=1)
                blocks = jnp.concatenate([buf[n], buf[n + 1]], axis=1)
                out_buf[i, :, (h & 7) * B : (h & 7) * B + B] = _dot3(blocks, w, ((1,), (1,)))
            columns = slice(512 * (part & 1), 512 * (part & 1) + 512)
            copy = pltpu.make_async_copy(out_buf.at[i, :, columns], outs[i].at[:, columns], out_sem.at[part])
            copy.start()
            stores.append(copy)
        for copy in stores:
            copy.wait()

    return pl.pallas_call(
        kernel,
        out_shape=[_f32(256, 1024)] * 2,
        in_specs=[SMEM] + [ANY] * (13 + len(extra)),
        out_specs=[ANY, ANY],
        scratch_shapes=[
            pltpu.VMEM((32, 256, B), jnp.float32),
            pltpu.VMEM((2, 8, 2, B, B), jnp.float32),
            pltpu.VMEM((2, 256, 1024), jnp.float32),
            pltpu.SemaphoreType.DMA((32,)),
            pltpu.SemaphoreType.DMA((2,)),
            pltpu.SemaphoreType.DMA((4,)),
        ],
        compiler_params=_params(),
        cost_estimate=_cost(8 * 2**20, 3 * 32 * 2 * 256 * B * B),
    )(table, mine, other, v, x0, q0, q1, x1, *early, *late, *extra)


def fold(r, part, ours, theirs, total=None):
    def kernel(part_ref, ours_ref, theirs_ref, *refs):
        out = refs[-5]
        a_buf, s_buf, in_sem, out_sem = refs[-4:]
        k = _position()[4]
        shares = ((ours_ref, k), (theirs_ref, 1 - k))
        loads = []
        for n, (source, share) in enumerate(shares):
            loads.append(pltpu.make_async_copy(part_ref.at[_my_rows(r, share)], a_buf.at[n], in_sem.at[2 * n]))
            loads.append(pltpu.make_async_copy(source, s_buf.at[n], in_sem.at[2 * n + 1]))
        for copy in loads:
            copy.start()
        stores = []
        for n, (_, share) in enumerate(shares):
            loads[2 * n].wait()
            loads[2 * n + 1].wait()
            s_buf[n, :, 0:512] = s_buf[n, :, 0:512] + a_buf[n]
            stores.append(pltpu.make_async_copy(s_buf.at[n], out.at[_my_rows(r, share)], out_sem.at[n]))
            stores[n].start()
        for copy in stores:
            copy.wait()

    more = [] if total is None else [total]
    return pl.pallas_call(
        kernel,
        out_shape=_f32(1024, 1024),
        in_specs=[ANY] * (3 + len(more)),
        out_specs=ANY,
        scratch_shapes=[
            pltpu.VMEM((2, 256, 512), jnp.float32),
            pltpu.VMEM((2, 256, 1024), jnp.float32),
            pltpu.SemaphoreType.DMA((4,)),
            pltpu.SemaphoreType.DMA((2,)),
        ],
        input_output_aliases={3: 0} if more else {},
        compiler_params=_params(),
        cost_estimate=_cost(5 * 2**20),
    )(part, ours, theirs, *more)


def alpha_product(c, table, values, v, q0, q1, own, late, total=None):
    more = [] if total is None else [total]
    columns = pl.ds(c * 512, 512)

    def kernel(table_ref, weights, *refs):
        ins, out = refs[0:9], refs[9 + len(more)]
        buf, w_buf, out_buf, sem, w_sem, out_sem = refs[10 + len(more) :]
        loads = [pltpu.make_async_copy(weights, w_buf, w_sem.at[0])]
        if more:
            loads.append(pltpu.make_async_copy(refs[9].at[:, columns], out_buf, w_sem.at[1]))
        for copy in loads:
            copy.start()
        options = [
            [
                (0, lambda j: ins[0].at[_rows(j), columns], None),
                (1, lambda j: ins[1].at[_rows(j & 3)], 0),
                (1, lambda j: ins[2].at[_rows(j & 3)], 1),
            ],
            [(2 + i, lambda s, i=i: ins[3 + i].at[s, :, columns], None) for i in range(3)],
            [(5 + i, lambda s, i=i: ins[6 + i].at[s], None) for i in range(3)],
        ]

        def load(n, _=None):
            _fetch(table_ref[ALPHA_ROW, n], options, buf.at[n], sem.at[n])

        lax.fori_loop(0, 8, load, None)
        for copy in loads:
            copy.wait()
        stores = []
        for part in range(4):
            for n in range(4 * part, 4 * part + 4):
                _wait(buf.at[n], sem.at[n])
            for g in range(2 * part, 2 * part + 2):
                n = 2 * g
                if n < 8:
                    load(n + 8)
                    load(n + 9)
                w = jnp.concatenate([w_buf[g, 0], w_buf[g, 1]], axis=1)
                product = _dot3(w, jnp.concatenate([buf[n], buf[n + 1]], axis=0), ((1,), (0,)))
                here = slice(g * B, g * B + B)
                out_buf[here] = out_buf[here] + product if more else product
            here = slice(part * 256, part * 256 + 256)
            target = out.at[here, columns] if more else out.at[here]
            stores.append(pltpu.make_async_copy(out_buf.at[here], target, out_sem.at[part]))
            stores[part].start()
        for copy in stores:
            copy.wait()

    return pl.pallas_call(
        kernel,
        out_shape=_f32(1024, 1024 if more else 512),
        in_specs=[SMEM] + [ANY] * (10 + len(more)),
        out_specs=ANY,
        scratch_shapes=[
            pltpu.VMEM((16, B, 512), jnp.float32),
            pltpu.VMEM((8, 2, B, B), jnp.float32),
            pltpu.VMEM((1024, 512), jnp.float32),
            pltpu.SemaphoreType.DMA((16,)),
            pltpu.SemaphoreType.DMA((2,)),
            pltpu.SemaphoreType.DMA((4,)),
        ],
        input_output_aliases={11: 0} if more else {},
        compiler_params=_params(),
        cost_estimate=_cost((9 if more else 7) * 2**20, 3 * 16 * 2 * B * B * 512),
    )(table, values, v, q0, q1, *own, *late, *more)


def sigma_here(v, alpha_values, beta_values, table):
    need = table[ALPHA_ROW, NEED]

    quadrants = [(0, 0), (1, 0), (0, 1), (1, 1)]

    def quadrant(ins, r, c):
        return ins[0].at[r * 512 : (r + 1) * 512, c * 512 : (c + 1) * 512]

    half, *pieces = _pick(
        [(2, 256, 1024)] + [(512, 512)] * 3,
        [v],
        lambda ins, k: [(ins[0].at[_my_rows(r, 1 - k)], 0, r) for r in range(2)]
        + [(quadrant(ins, *q), 1 + n, None) for n, q in enumerate(quadrants[1:])],
    )
    x0 = _send(half, TO_CORE)
    zl = {(r, c): _send(p, TO_ZL) for (r, c), p in zip(quadrants, [v[:512, :512], *pieces])}
    other_values = _send(beta_values, TO_CORE)

    out = _gather(table, 0, 0, (B, 1024), 3, [v], lambda ins, k: [[(0, lambda j: ins[0].at[_rows(j)], None)]])
    own = _send_all(out, TO_X)

    def early_options(ins, k):
        def of_v(j):
            return ins[0].at[:, _half_rows(k), _rows(j)]

        return [[(0, of_v, None), (1, lambda j: ins[1].at[:, :, _rows(j)], None)]]

    out = _gather(table, 4, 0, (2, 256, B), EARLY, [v.reshape(2, 512, 1024), x0], early_options)
    early = _send_all(out, TO_Y)

    zh = {(r, c): _send(zl[(r, c)], TO_ZNEXT) for r, c in quadrants}

    x1, late, x_late = {}, {}, {}
    for r in range(2):
        (half,) = _pick(
            [(2, 256, 512)],
            [zl[(r, 0)], zl[(r, 1)]],
            lambda ins, k: [(ins[c].at[_half_rows(1 - k)], 0, c) for c in range(2)],
        )
        x1[r] = _send(half, TO_CORE)
    for n in range(2):
        out = _gather(
            table,
            0,
            3,
            (B, 512),
            3,
            [zh[(0, n)], zh[(1, n)]],
            lambda ins, k: [[(0, lambda j, i=i: ins[i].at[_rows(j & 3)], i) for i in range(2)]],
        )
        x_late[n] = _send_all(out, TO_X)
        out = _gather(
            table,
            4,
            STARTS[1],
            (256, B),
            LATE,
            [v, x0, zl[(n, 0)], zl[(n, 1)], x1[n]],
            lambda ins, k, n=n: [_near(n, k, *ins)],
        )
        late[n] = _send_all(out, TO_Y)

    def send_extra(start, slots):
        halves = []
        for r in range(2):
            halves.append(
                _gather(
                    table,
                    4,
                    start,
                    (256, B),
                    slots,
                    [v, x0, zl[(r, 0)], zl[(r, 1)], x1[r]],
                    lambda ins, k, r=r: [_near(r, k, *ins)],
                )
            )
        return tuple(_send_all([jnp.stack(pair, axis=1) for pair in zip(*halves)], TO_Y))

    def skip_extra(slots):
        shapes = tuple(_f32(slots, 2, 256, B) for _ in HOPS)
        return pl.pallas_call(lambda *refs: None, out_shape=shapes, out_specs=(ANY,) * 3)()

    extra = []
    for start, slots in zip(STARTS[2:], EXTRA):
        extra += lax.cond(
            need > start,
            lambda start=start, slots=slots: send_extra(start, slots),
            lambda slots=slots: skip_extra(slots),
        )

    part = alpha_product(0, table, alpha_values, v, zh[(0, 0)], zh[(1, 0)], own, x_late[0])
    total = None
    for r in range(2):
        ours, other = beta_product(
            r, table, beta_values, other_values, v, x0, zl[(r, 0)], zl[(r, 1)], x1[r], early, late[r], extra
        )
        total = fold(r, part, ours, _send(other, TO_CORE), total)
    return alpha_product(1, table, alpha_values, v, zh[(0, 1)], zh[(1, 1)], own, x_late[1], total)


def per_device(vector, links_alpha, alpha_values, links_beta, beta_values):
    table = route_table(links_alpha, links_beta)
    return sigma_here(vector, alpha_values, beta_values, table)


def solution(mesh):
    placed = (P("row", "col"), P(), P("row", None, None, None), P(), P("col", None, None, None))
    return jax.shard_map(per_device, mesh=mesh, in_specs=placed, out_specs=P("row", "col"), check_vma=False)
```

time: 398 us -> 373 us (0.937)
  waiting for transfers between devices: 266 us -> 253 us
  starting transfers between devices: 49.2 us -> 45 us
    ppermute x32, waiting for transfers between devices: 266 us -> 253 us  [_send(): return lax.ppermute(value, AXES, pairs)]
    pallas_call x2, Pallas kernels: 18.6 us -> 12.9 us  [beta_product(): pl.pallas_call(kernel, out_shape=[_f32(256, 1024)] * 2, in_specs=[SMEM] +...]
    another operation x8 -> x0, local copies, waits for them, and re-layouts: 5.53 us -> none
    pallas_call x2 -> x7, Pallas kernels: 13.6 us -> 19 us  [the longest x2 11.8 us: alpha_product(): pl.pallas_call(kernel, out_shape=_f32(1024, 1024 if more else 512), in_sp...]
    ppermute x32, starting transfers between devices: 49.2 us -> 45 us  [_send(): return lax.ppermute(value, AXES, pairs)]
    pallas_call x4 -> x3, Pallas kernels: 10.2 us -> 8.72 us  [_pick(): pl.pallas_call(kernel, out_shape=[_f32(*shape) for shape in shapes], in_s...]
  transfers between devices with their start and end apart: 32 -> 32, of which waited for: 13 -> 15; matrix products, arithmetic and copies ran while one was open for 3% -> 1% of each run, Pallas kernels for 14% -> 15%
where the time goes in v4:
time: 373 us; the launch traced here: 370 us
  waiting for transfers between devices  253 us (68%)
  Pallas kernels  66.7 us (18%)
  starting transfers between devices  45 us (12%)
  local copies, waits for them, and re-layouts  4.42 us (1%)
    ppermute x32, waiting for transfers between devices, _send(): return lax.ppermute(value, AXES, pairs)  253 us
    ppermute x32, starting transfers between devices, _send(): return lax.ppermute(value, AXES, pairs)  45 us
    pallas_call x6, Pallas kernels, _gather(): pl.pallas_call(kernel, out_shape=[_f32(slots, *slot_shape)] * 3, in_specs...  26.1 us
    pallas_call x2, Pallas kernels, beta_product(): pl.pallas_call(kernel, out_shape=[_f32(256, 1024)] * 2, in_specs=[SMEM] +...  12.9 us
    pallas_call x2, Pallas kernels, alpha_product(): pl.pallas_call(kernel, out_shape=_f32(1024, 1024 if more else 512), in_sp...  11.8 us
    pallas_call x3, Pallas kernels, _pick(): pl.pallas_call(kernel, out_shape=[_f32(*shape) for shape in shapes], in_s...  8.72 us
  transfers between devices with their start and end apart: 32, of which 15 were waited for; matrix products, arithmetic and copies ran while one was open for 1% of the time, Pallas kernels for 15%

profile of v4, /device:TPU:9, one launch (start us, length us, event | category | flops | bytes accessed | tf_op | source)
XLA Modules:
  0.0 370.3 jit_solution(9000310353030156078)
XLA Ops:
  0.0 4.4 %shard_map.55 = (f32[2,256,1024]{2,1,0:T(8,128)}, f32[512,512]{1,0:T(8,128)}, f32[512,512]{1,0:T(8,128)}, f32[512,512]{1,0:T(8,128)}) custom-call(f32[1024,1024]{1,0:T(8,128)} %refs_0_.15), custom_call_target="tpu_custom_call" | custom-call | bytes 10485760 | tf_op jit(solution)/shard_map/pallas_call | solution.py:262
  4.4 1.7 collective-permute-start.18
  6.2 1.4 collective-permute-start.6
  7.6 2.3 slice.6
  10.0 1.5 collective-permute-start.24
  11.5 17.7 %collective-permute-done.18.refs_0_.refs_2_.refs_4_ = f32[512,512]{1,0:T(8,128)} collective-permute-done((f32[512,512]{1,0:T(8,128)}, f32[512,512]{1,0:T(8,128)}, u32[]{:S(2)}, u32[]{:S(2)}) %collective-permute-start.18) | collective-permute-done | bytes 1048608 | tf_op jit(solution)/shard_map/ppermute | solution.py:47
  29.2 22.5 %collective-permute-done.8.refs_1_.refs_3_.refs_5_ = f32[512,512]{1,0:T(8,128)} collective-permute-done((f32[512,512]{1,0:T(8,128)}, f32[512,512]{1,0:T(8,128)}, u32[]{:S(2)}, u32[]{:S(2)}) %collective-permute-start.8) | collective-permute-done | bytes 1048608 | tf_op jit(solution)/shard_map/ppermute | solution.py:47
  51.7 2.1 shard_map.60
  53.8 2.4 collective-permute-start.25
  56.2 17.9 %collective-permute-done.6.refs_1_.refs_3_.refs_5_ = f32[512,512]{1,0:T(8,128)} collective-permute-done((f32[512,512]{1,0:T(8,128)}, f32[512,512]{1,0:T(8,128)}, u32[]{:S(2)}, u32[]{:S(2)}) %collective-permute-start.6) | collective-permute-done | bytes 1048608 | tf_op jit(solution)/shard_map/ppermute | solution.py:47
  74.1 22.5 %collective-permute-done.16.refs_0_.refs_2_.refs_4_ = f32[512,512]{1,0:T(8,128)} collective-permute-done((f32[512,512]{1,0:T(8,128)}, f32[512,512]{1,0:T(8,128)}, u32[]{:S(2)}, u32[]{:S(2)}) %collective-permute-start.16) | collective-permute-done | bytes 1048608 | tf_op jit(solution)/shard_map/ppermute | solution.py:47
  96.6 2.2 shard_map.63
  98.8 1.4 collective-permute-start.32
  101.8 1.3 route_table.1.table_ref
  103.1 5.2 %shard_map.56 = (f32[3,128,1024]{2,1,0:T(8,128)}, f32[3,128,1024]{2,1,0:T(8,128)}, f32[3,128,1024]{2,1,0:T(8,128)}) custom-call(s32[8,128]{1,0:T(8,128)S(1)} %route_table.1.table_ref, f32[1024,1024]{1,0:T(8,128)} %refs_0_.15), custom_call_target="tpu_custom_call" | custom-call | bytes 9437184 | tf_op jit(solution)/shard_map/pallas_call | solution.py:221
  108.3 1.5 collective-permute-start.10
  109.8 2.0 collective-permute-start.11
  113.6 1.6 collective-permute-start.12
  116.0 3.7 collective-permute-start.19
  119.7 2.6 collective-permute-start.17
  122.3 4.3 %shard_map.65 = (f32[6,256,128]{2,1,0:T(8,128)}, f32[6,256,128]{2,1,0:T(8,128)}, f32[6,256,128]{2,1,0:T(8,128)}) custom-call(s32[8,128]{1,0:T(8,128)S(1)} %route_table.1.table_ref, f32[1024,1024]{1,0:T(8,128)} %refs_0_.15, f32[2,256,1024]{2,1,0:T(8,128)} %collective-permute-done.24.refs_1_.refs_3_, ...), custom_call_target="tpu_custom_call" | custom-call | bytes 4718592 | tf_op jit(solution)/shard_map/pallas_call | solution.py:221
  126.7 4.1 %shard_map.62 = (f32[6,256,128]{2,1,0:T(8,128)}, f32[6,256,128]{2,1,0:T(8,128)}, f32[6,256,128]{2,1,0:T(8,128)}) custom-call(s32[8,128]{1,0:T(8,128)S(1)} %route_table.1.table_ref, f32[1024,1024]{1,0:T(8,128)} %refs_0_.15, f32[2,256,1024]{2,1,0:T(8,128)} %collective-permute-done.24.refs_1_.refs_3_, ...), custom_call_target="tpu_custom_call" | custom-call | bytes 4718592 | tf_op jit(solution)/shard_map/pallas_call | solution.py:221
  130.8 15.1 %collective-permute-done.10.refs_3_ = f32[3,128,1024]{2,1,0:T(8,128)} collective-permute-done((f32[3,128,1024]{2,1,0:T(8,128)}, f32[3,128,1024]{2,1,0:T(8,128)}, u32[]{:S(2)}, u32[]{:S(2)}) %collective-permute-start.10) | collective-permute-done | bytes 1572896 | tf_op jit(solution)/shard_map/ppermute | solution.py:47
  147.1 33.1 %collective-permute-done.11.refs_4_ = f32[3,128,1024]{2,1,0:T(8,128)} collective-permute-done((f32[3,128,1024]{2,1,0:T(8,128)}, f32[3,128,1024]{2,1,0:T(8,128)}, u32[]{:S(2)}, u32[]{:S(2)}) %collective-permute-start.11) | collective-permute-done | bytes 1572896 | tf_op jit(solution)/shard_map/ppermute | solution.py:47
  180.3 2.0 collective-permute-start.35
  183.8 4.5 %shard_map.61 = (f32[5,2,256,128]{3,2,1,0:T(8,128)}, f32[5,2,256,128]{3,2,1,0:T(8,128)}, f32[5,2,256,128]{3,2,1,0:T(8,128)}) custom-call(s32[8,128]{1,0:T(8,128)S(1)} %route_table.1.table_ref, f32[2,512,1024]{2,1,0:T(8,128)} %bitcast.15, f32[2,256,1024]{2,1,0:T(8,128)} %collective-permute-done.24.refs_1_.refs_3_), custom_call_target="tpu_custom_call" | custom-call | bytes 7864320 | tf_op jit(solution)/shard_map/pallas_call | solution.py:221
  188.4 2.8 collective-permute-start.30
  191.2 9.2 %collective-permute-done.35.refs_11_ = f32[6,256,128]{2,1,0:T(8,128)} collective-permute-done((f32[6,256,128]{2,1,0:T(8,128)}, f32[6,256,128]{2,1,0:T(8,128)}, u32[]{:S(2)}, u32[]{:S(2)}) %collective-permute-start.35) | collective-permute-done | bytes 786464 | tf_op jit(solution)/shard_map/ppermute | solution.py:47
  200.6 19.1 %collective-permute-done.36.refs_12_ = f32[6,256,128]{2,1,0:T(8,128)} collective-permute-done((f32[6,256,128]{2,1,0:T(8,128)}, f32[6,256,128]{2,1,0:T(8,128)}, u32[]{:S(2)}, u32[]{:S(2)}) %collective-permute-start.36) | collective-permute-done | bytes 786464 | tf_op jit(solution)/shard_map/ppermute | solution.py:47
  219.6 2.0 collective-permute-start.27
  221.6 12.5 %collective-permute-done.30.refs_11_ = f32[6,256,128]{2,1,0:T(8,128)} collective-permute-done((f32[6,256,128]{2,1,0:T(8,128)}, f32[6,256,128]{2,1,0:T(8,128)}, u32[]{:S(2)}, u32[]{:S(2)}) %collective-permute-start.30) | collective-permute-done | bytes 786464 | tf_op jit(solution)/shard_map/ppermute | solution.py:47
  234.1 4.1 %collective-permute-start.7 = (f32[512,512]{1,0:T(8,128)}, f32[512,512]{1,0:T(8,128)}, u32[]{:S(2)}, u32[]{:S(2)}) collective-permute-start(f32[512,512]{1,0:T(8,128)} %collective-permute-done.6.refs_1_.refs_3_.refs_5_), channel_id=1, source_target_pairs={{0,24},{1,25},{2,26},{3,27},{4,28},{5,29},{6,30},{7,31},{8,16},{9,... | collective-permute-start | bytes 3145736 | tf_op jit(solution)/shard_map/ppermute | solution.py:47
  238.2 15.0 %collective-permute-done.31.refs_12_ = f32[6,256,128]{2,1,0:T(8,128)} collective-permute-done((f32[6,256,128]{2,1,0:T(8,128)}, f32[6,256,128]{2,1,0:T(8,128)}, u32[]{:S(2)}, u32[]{:S(2)}) %collective-permute-start.31) | collective-permute-done | bytes 786464 | tf_op jit(solution)/shard_map/ppermute | solution.py:47
  253.3 4.1 %collective-permute-start.9 = (f32[512,512]{1,0:T(8,128)}, f32[512,512]{1,0:T(8,128)}, u32[]{:S(2)}, u32[]{:S(2)}) collective-permute-start(f32[512,512]{1,0:T(8,128)} %collective-permute-done.8.refs_1_.refs_3_.refs_5_), channel_id=1, source_target_pairs={{0,24},{1,25},{2,26},{3,27},{4,28},{5,29},{6,30},{7,31},{8,16},{9,... | collective-permute-start | bytes 3145736 | tf_op jit(solution)/shard_map/ppermute | solution.py:47
  257.4 3.9 %shard_map.58 = (f32[3,128,512]{2,1,0:T(8,128)}, f32[3,128,512]{2,1,0:T(8,128)}, f32[3,128,512]{2,1,0:T(8,128)}) custom-call(s32[8,128]{1,0:T(8,128)S(1)} %route_table.1.table_ref, f32[512,512]{1,0:T(8,128)} %collective-permute-done.17.refs_0_.refs_1_, f32[512,512]{1,0:T(8,128)} %collective-permute-done.19.refs_1_.refs_2_), custom_call_target="tpu_custom_call" | custom-call | bytes 4718592 | tf_op jit(solution)/shard_map/pallas_call | solution.py:221
  261.4 17.8 %collective-permute-done.27.refs_8_ = f32[5,2,256,128]{3,2,1,0:T(8,128)} collective-permute-done((f32[5,2,256,128]{3,2,1,0:T(8,128)}, f32[5,2,256,128]{3,2,1,0:T(8,128)}, u32[]{:S(2)}, u32[]{:S(2)}) %collective-permute-start.27) | collective-permute-done | bytes 1310752 | tf_op jit(solution)/shard_map/ppermute | solution.py:47
  280.1 28.3 %collective-permute-done.28.refs_9_ = f32[5,2,256,128]{3,2,1,0:T(8,128)} collective-permute-done((f32[5,2,256,128]{3,2,1,0:T(8,128)}, f32[5,2,256,128]{3,2,1,0:T(8,128)}, u32[]{:S(2)}, u32[]{:S(2)}) %collective-permute-start.28) | collective-permute-done | bytes 1310752 | tf_op jit(solution)/shard_map/ppermute | solution.py:47
  308.3 6.4 %shard_map.66 = (f32[256,1024]{1,0:T(8,128)}, f32[256,1024]{1,0:T(8,128)}) custom-call(s32[8,128]{1,0:T(8,128)S(1)} %route_table.1.table_ref, f32[8,2,128,128]{3,2,1,0:T(8,128)} %refs_0_.14, f32[8,2,128,128]{3,2,1,0:T(8,128)} %collective-permute-done.23.refs_1_, f32[1024,1024]{1,0:T(8,128)} %refs_0_.15, ...), custom_call_target="tpu_custom_call" | custom-call | flops 805306368 | bytes 8388608 | tf_op jit(solution)/shard_map/pallas_call | solution.py:347
  314.7 6.5 %shard_map.64 = (f32[256,1024]{1,0:T(8,128)}, f32[256,1024]{1,0:T(8,128)}) custom-call(s32[8,128]{1,0:T(8,128)S(1)} %route_table.1.table_ref, f32[8,2,128,128]{3,2,1,0:T(8,128)} %refs_0_.14, f32[8,2,128,128]{3,2,1,0:T(8,128)} %collective-permute-done.23.refs_1_, f32[1024,1024]{1,0:T(8,128)} %refs_0_.15, ...), custom_call_target="tpu_custom_call" | custom-call | flops 805306368 | bytes 8388608 | tf_op jit(solution)/shard_map/pallas_call | solution.py:347
  322.3 4.1 %shard_map.57 = (f32[3,128,512]{2,1,0:T(8,128)}, f32[3,128,512]{2,1,0:T(8,128)}, f32[3,128,512]{2,1,0:T(8,128)}) custom-call(s32[8,128]{1,0:T(8,128)S(1)} %route_table.1.table_ref, f32[512,512]{1,0:T(8,128)} %collective-permute-done.7.refs_0_.refs_1_, f32[512,512]{1,0:T(8,128)} %collective-permute-done.9.refs_1_.refs_2_), custom_call_target="tpu_custom_call" | custom-call | bytes 4718592 | tf_op jit(solution)/shard_map/pallas_call | solution.py:221
  326.4 1.5 collective-permute-start.13
  328.8 1.6 collective-permute-start.15
  330.4 5.6 %shard_map.59.part_ref = f32[1024,512]{1,0:T(8,128)} custom-call(s32[8,128]{1,0:T(8,128)S(1)} %route_table.1.table_ref, f32[8,2,128,128]{3,2,1,0:T(8,128)} %weights.3, f32[1024,1024]{1,0:T(8,128)} %refs_0_.15, f32[512,512]{1,0:T(8,128)} %collective-permute-done.17.refs_0_.refs_1_, f32[512,512]{1,0:T(8,128)} %collective-permute-done.19.refs_1_.refs_2_, ...), custom_call_target="tpu_custom_call" | custom-call | flops 805306368 | bytes 7340032 | tf_op jit(solution)/shard_map/pallas_call | solution.py:453
  336.0 2.9 shard_map.67.refs_0_
  338.9 3.0 shard_map.68.refs_9_
  341.9 5.1 %collective-permute-done.13.refs_6_ = f32[3,128,512]{2,1,0:T(8,128)S(1)} collective-permute-done((f32[3,128,512]{2,1,0:T(8,128)}, f32[3,128,512]{2,1,0:T(8,128)S(1)}, u32[]{:S(2)}, u32[]{:S(2)}) %collective-permute-start.13) | collective-permute-done | bytes 786464 | tf_op jit(solution)/shard_map/ppermute | solution.py:47
  347.0 16.3 %collective-permute-done.14.refs_7_ = f32[3,128,512]{2,1,0:T(8,128)} collective-permute-done((f32[3,128,512]{2,1,0:T(8,128)}, f32[3,128,512]{2,1,0:T(8,128)}, u32[]{:S(2)}, u32[]{:S(2)}) %collective-permute-start.14) | collective-permute-done | bytes 786464 | tf_op jit(solution)/shard_map/ppermute | solution.py:47
  363.9 6.2 %shard_map.69 = f32[1024,1024]{1,0:T(8,128)} custom-call(s32[8,128]{1,0:T(8,128)S(1)} %route_table.1.table_ref, f32[8,2,128,128]{3,2,1,0:T(8,128)} %weights.3, f32[1024,1024]{1,0:T(8,128)} %refs_0_.15, f32[512,512]{1,0:T(8,128)} %collective-permute-done.7.refs_0_.refs_1_, ...), custom_call_target="tpu_custom_call", output_to_operand_aliasing={{}: (11, {})} | custom-call | flops 805306368 | bytes 9437184 | tf_op jit(solution)/shard_map/pallas_call | solution.py:453
  (50 shorter events, 9.9 us)
Async XLA Ops:
  4.4 24.8 %collective-permute-start.18 = (f32[512,512]{1,0:T(8,128)}, f32[512,512]{1,0:T(8,128)}, u32[]{:S(2)}, u32[]{:S(2)}) collective-permute-start(f32[512,512]{1,0:T(8,128)} %get-tuple-element.111), channel_id=1, source_target_pairs={{0,8},{1,9},{2,10},{3,11},{4,12},{5,13},{6,14},{7,15},{8,0},{9,1},... | collective-permute-start | bytes 3145736 | tf_op jit(solution)/shard_map/ppermute | solution.py:47
  6.1 45.5 %collective-permute-start.8 = (f32[512,512]{1,0:T(8,128)}, f32[512,512]{1,0:T(8,128)}, u32[]{:S(2)}, u32[]{:S(2)}) collective-permute-start(f32[512,512]{1,0:T(8,128)} %get-tuple-element.104), channel_id=1, source_target_pairs={{0,8},{1,9},{2,10},{3,11},{4,12},{5,13},{6,14},{7,15},{8,0},{9,1},... | collective-permute-start | bytes 3145736 | tf_op jit(solution)/shard_map/ppermute | solution.py:47
  6.2 67.9 %collective-permute-start.6 = (f32[512,512]{1,0:T(8,128)}, f32[512,512]{1,0:T(8,128)}, u32[]{:S(2)}, u32[]{:S(2)}) collective-permute-start(f32[512,512]{1,0:T(8,128)} %get-tuple-element.103), channel_id=1, source_target_pairs={{0,8},{1,9},{2,10},{3,11},{4,12},{5,13},{6,14},{7,15},{8,0},{9,1},... | collective-permute-start | bytes 3145736 | tf_op jit(solution)/shard_map/ppermute | solution.py:47
  9.9 86.7 %collective-permute-start.16 = (f32[512,512]{1,0:T(8,128)}, f32[512,512]{1,0:T(8,128)}, u32[]{:S(2)}, u32[]{:S(2)}) collective-permute-start(f32[512,512]{1,0:T(8,128)} %slice.6), channel_id=1, source_target_pairs={{0,8},{1,9},{2,10},{3,11},{4,12},{5,13},{6,14},{7,15},{8,0},{9,1},... | collective-permute-start | bytes 3145736 | tf_op jit(solution)/shard_map/ppermute | solution.py:47
  10.0 103.5 %collective-permute-start.24 = (f32[2,256,1024]{2,1,0:T(8,128)}, f32[2,256,1024]{2,1,0:T(8,128)}, u32[]{:S(2)}, u32[]{:S(2)}) collective-permute-start(f32[2,256,1024]{2,1,0:T(8,128)} %get-tuple-element.115), channel_id=1, source_target_pairs={{0,1},{1,0},{2,3},{3,2},{4,5},{5,4},{6,7},{7,6},{8,9},{9,8},{10,11... | collective-permute-start | bytes 6291464 | tf_op jit(solution)/shard_map/ppermute | solution.py:47
  53.8 46.4 %copy-start.10 = (s32[128,2]{0,1:T(2,128)S(1)}, s32[128,2]{0,1:T(2,128)}, u32[]{:S(2)}) copy-start(s32[128,2]{0,1:T(2,128)} %param.12) | copy-start | bytes 3076
  53.8 47.2 %copy-start.11 = (s32[64,2]{0,1:T(2,128)S(1)}, s32[64,2]{0,1:T(2,128)}, u32[]{:S(2)}) copy-start(s32[64,2]{0,1:T(2,128)} %param.10) | copy-start | bytes 1540
  53.8 59.6 %collective-permute-start.25 = (f32[2,256,512]{2,1,0:T(8,128)}, f32[2,256,512]{2,1,0:T(8,128)}, u32[]{:S(2)}, u32[]{:S(2)}) collective-permute-start(f32[2,256,512]{2,1,0:T(8,128)} %shard_map.60), channel_id=1, source_target_pairs={{0,1},{1,0},{2,3},{3,2},{4,5},{5,4},{6,7},{7,6},{8,9},{9,8},{10,11... | collective-permute-start | bytes 3145736 | tf_op jit(solution)/shard_map/ppermute | solution.py:47
  98.8 14.7 %collective-permute-start.32 = (f32[2,256,512]{2,1,0:T(8,128)}, f32[2,256,512]{2,1,0:T(8,128)}, u32[]{:S(2)}, u32[]{:S(2)}) collective-permute-start(f32[2,256,512]{2,1,0:T(8,128)} %shard_map.63), channel_id=1, source_target_pairs={{0,1},{1,0},{2,3},{3,2},{4,5},{5,4},{6,7},{7,6},{8,9},{9,8},{10,11... | collective-permute-start | bytes 3145736 | tf_op jit(solution)/shard_map/ppermute | solution.py:47
  108.3 37.5 %collective-permute-start.10 = (f32[3,128,1024]{2,1,0:T(8,128)}, f32[3,128,1024]{2,1,0:T(8,128)}, u32[]{:S(2)}, u32[]{:S(2)}) collective-permute-start(f32[3,128,1024]{2,1,0:T(8,128)} %get-tuple-element.105), channel_id=1, source_target_pairs={{0,32},{1,33},{2,34},{3,35},{4,36},{5,37},{6,38},{7,39},{8,40},{9,... | collective-permute-start | bytes 4718600 | tf_op jit(solution)/shard_map/ppermute | solution.py:47
  109.8 70.5 %collective-permute-start.11 = (f32[3,128,1024]{2,1,0:T(8,128)}, f32[3,128,1024]{2,1,0:T(8,128)}, u32[]{:S(2)}, u32[]{:S(2)}) collective-permute-start(f32[3,128,1024]{2,1,0:T(8,128)} %get-tuple-element.106), channel_id=1, source_target_pairs={{0,64},{1,65},{2,66},{3,67},{4,68},{5,69},{6,70},{7,71},{8,72},{9,... | collective-permute-start | bytes 4718600 | tf_op jit(solution)/shard_map/ppermute | solution.py:47
  113.6 68.8 %collective-permute-start.12 = (f32[3,128,1024]{2,1,0:T(8,128)}, f32[3,128,1024]{2,1,0:T(8,128)}, u32[]{:S(2)}, u32[]{:S(2)}) collective-permute-start(f32[3,128,1024]{2,1,0:T(8,128)} %get-tuple-element.107), channel_id=1, source_target_pairs={{0,96},{1,97},{2,98},{3,99},{4,100},{5,101},{6,102},{7,103},{8,104... | collective-permute-start | bytes 4718600 | tf_op jit(solution)/shard_map/ppermute | solution.py:47
  115.2 4.6 %collective-permute-start.23 = (f32[8,2,128,128]{3,2,1,0:T(8,128)}, f32[8,2,128,128]{3,2,1,0:T(8,128)}, u32[]{:S(2)}, u32[]{:S(2)}) collective-permute-start(f32[8,2,128,128]{3,2,1,0:T(8,128)} %refs_0_.14), channel_id=1, source_target_pairs={{0,1},{1,0},{2,3},{3,2},{4,5},{5,4},{6,7},{7,6},{8,9},{9,8},{10,11... | collective-permute-start | bytes 3145736 | tf_op jit(solution)/shard_map/ppermute | solution.py:47
  116.0 67.4 %collective-permute-start.19 = (f32[512,512]{1,0:T(8,128)}, f32[512,512]{1,0:T(8,128)}, u32[]{:S(2)}, u32[]{:S(2)}) collective-permute-start(f32[512,512]{1,0:T(8,128)} %collective-permute-done.18.refs_0_.refs_2_.refs_4_), channel_id=1, source_target_pairs={{0,24},{1,25},{2,26},{3,27},{4,28},{5,29},{6,30},{7,31},{8,16},{9,... | collective-permute-start | bytes 3145736 | tf_op jit(solution)/shard_map/ppermute | solution.py:47
  119.7 68.6 %collective-permute-start.17 = (f32[512,512]{1,0:T(8,128)}, f32[512,512]{1,0:T(8,128)}, u32[]{:S(2)}, u32[]{:S(2)}) collective-permute-start(f32[512,512]{1,0:T(8,128)} %collective-permute-done.16.refs_0_.refs_2_.refs_4_), channel_id=1, source_target_pairs={{0,24},{1,25},{2,26},{3,27},{4,28},{5,29},{6,30},{7,31},{8,16},{9,... | collective-permute-start | bytes 3145736 | tf_op jit(solution)/shard_map/ppermute | solution.py:47
  145.9 42.5 %collective-permute-start.34 = (f32[6,256,128]{2,1,0:T(8,128)}, f32[6,256,128]{2,1,0:T(8,128)S(1)}, u32[]{:S(2)}, u32[]{:S(2)}) collective-permute-start(f32[6,256,128]{2,1,0:T(8,128)} %get-tuple-element.130), channel_id=1, source_target_pairs={{0,2},{1,3},{2,4},{3,5},{4,6},{5,7},{6,0},{7,1},{8,10},{9,11},{10,... | collective-permute-start | bytes 2359304 | tf_op jit(solution)/shard_map/ppermute | solution.py:47
  180.3 20.1 %collective-permute-start.35 = (f32[6,256,128]{2,1,0:T(8,128)}, f32[6,256,128]{2,1,0:T(8,128)}, u32[]{:S(2)}, u32[]{:S(2)}) collective-permute-start(f32[6,256,128]{2,1,0:T(8,128)} %get-tuple-element.131), channel_id=1, source_target_pairs={{0,4},{1,5},{2,6},{3,7},{4,0},{5,1},{6,2},{7,3},{8,12},{9,13},{10,... | collective-permute-start | bytes 2359304 | tf_op jit(solution)/shard_map/ppermute | solution.py:47
  182.3 37.3 %collective-permute-start.36 = (f32[6,256,128]{2,1,0:T(8,128)}, f32[6,256,128]{2,1,0:T(8,128)}, u32[]{:S(2)}, u32[]{:S(2)}) collective-permute-start(f32[6,256,128]{2,1,0:T(8,128)} %get-tuple-element.132), channel_id=1, source_target_pairs={{0,6},{1,7},{2,0},{3,1},{4,2},{5,3},{6,4},{7,5},{8,14},{9,15},{10,... | collective-permute-start | bytes 2359304 | tf_op jit(solution)/shard_map/ppermute | solution.py:47
  183.4 38.3 %collective-permute-start.29 = (f32[6,256,128]{2,1,0:T(8,128)}, f32[6,256,128]{2,1,0:T(8,128)}, u32[]{:S(2)}, u32[]{:S(2)}) collective-permute-start(f32[6,256,128]{2,1,0:T(8,128)} %get-tuple-element.119), channel_id=1, source_target_pairs={{0,2},{1,3},{2,4},{3,5},{4,6},{5,7},{6,0},{7,1},{8,10},{9,11},{10,... | collective-permute-start | bytes 2359304 | tf_op jit(solution)/shard_map/ppermute | solution.py:47
  188.3 73.0 %collective-permute-start.26 = (f32[5,2,256,128]{3,2,1,0:T(8,128)}, f32[5,2,256,128]{3,2,1,0:T(8,128)}, u32[]{:S(2)}, u32[]{:S(2)}) collective-permute-start(f32[5,2,256,128]{3,2,1,0:T(8,128)} %get-tuple-element.116), channel_id=1, source_target_pairs={{0,2},{1,3},{2,4},{3,5},{4,6},{5,7},{6,0},{7,1},{8,10},{9,11},{10,... | collective-permute-start | bytes 3932168 | tf_op jit(solution)/shard_map/ppermute | solution.py:47
  188.4 119.9 %copy-start = (f32[6,256,128]{2,1,0:T(8,128)}, f32[6,256,128]{2,1,0:T(8,128)S(1)}, u32[]{:S(2)}) copy-start(f32[6,256,128]{2,1,0:T(8,128)S(1)} %collective-permute-done.34.refs_10_) | copy-start | bytes 2359300
  188.4 45.7 %collective-permute-start.30 = (f32[6,256,128]{2,1,0:T(8,128)}, f32[6,256,128]{2,1,0:T(8,128)}, u32[]{:S(2)}, u32[]{:S(2)}) collective-permute-start(f32[6,256,128]{2,1,0:T(8,128)} %get-tuple-element.120), channel_id=1, source_target_pairs={{0,4},{1,5},{2,6},{3,7},{4,0},{5,1},{6,2},{7,3},{8,12},{9,13},{10,... | collective-permute-start | bytes 2359304 | tf_op jit(solution)/shard_map/ppermute | solution.py:47
  200.4 52.9 %collective-permute-start.31 = (f32[6,256,128]{2,1,0:T(8,128)}, f32[6,256,128]{2,1,0:T(8,128)}, u32[]{:S(2)}, u32[]{:S(2)}) collective-permute-start(f32[6,256,128]{2,1,0:T(8,128)} %get-tuple-element.121), channel_id=1, source_target_pairs={{0,6},{1,7},{2,0},{3,1},{4,2},{5,3},{6,4},{7,5},{8,14},{9,15},{10,... | collective-permute-start | bytes 2359304 | tf_op jit(solution)/shard_map/ppermute | solution.py:47
  219.6 59.5 %collective-permute-start.27 = (f32[5,2,256,128]{3,2,1,0:T(8,128)}, f32[5,2,256,128]{3,2,1,0:T(8,128)}, u32[]{:S(2)}, u32[]{:S(2)}) collective-permute-start(f32[5,2,256,128]{3,2,1,0:T(8,128)} %get-tuple-element.117), channel_id=1, source_target_pairs={{0,4},{1,5},{2,6},{3,7},{4,0},{5,1},{6,2},{7,3},{8,12},{9,13},{10,... | collective-permute-start | bytes 3932168 | tf_op jit(solution)/shard_map/ppermute | solution.py:47
  221.6 86.7 %collective-permute-start.28 = (f32[5,2,256,128]{3,2,1,0:T(8,128)}, f32[5,2,256,128]{3,2,1,0:T(8,128)}, u32[]{:S(2)}, u32[]{:S(2)}) collective-permute-start(f32[5,2,256,128]{3,2,1,0:T(8,128)} %get-tuple-element.118), channel_id=1, source_target_pairs={{0,6},{1,7},{2,0},{3,1},{4,2},{5,3},{6,4},{7,5},{8,14},{9,15},{10,... | collective-permute-start | bytes 3932168 | tf_op jit(solution)/shard_map/ppermute | solution.py:47
  234.1 87.1 %collective-permute-start.7 = (f32[512,512]{1,0:T(8,128)}, f32[512,512]{1,0:T(8,128)}, u32[]{:S(2)}, u32[]{:S(2)}) collective-permute-start(f32[512,512]{1,0:T(8,128)} %collective-permute-done.6.refs_1_.refs_3_.refs_5_), channel_id=1, source_target_pairs={{0,24},{1,25},{2,26},{3,27},{4,28},{5,29},{6,30},{7,31},{8,16},{9,... | collective-permute-start | bytes 3145736 | tf_op jit(solution)/shard_map/ppermute | solution.py:47
  253.3 68.9 %collective-permute-start.9 = (f32[512,512]{1,0:T(8,128)}, f32[512,512]{1,0:T(8,128)}, u32[]{:S(2)}, u32[]{:S(2)}) collective-permute-start(f32[512,512]{1,0:T(8,128)} %collective-permute-done.8.refs_1_.refs_3_.refs_5_), channel_id=1, source_target_pairs={{0,24},{1,25},{2,26},{3,27},{4,28},{5,29},{6,30},{7,31},{8,16},{9,... | collective-permute-start | bytes 3145736 | tf_op jit(solution)/shard_map/ppermute | solution.py:47
  261.3 65.1 %collective-permute-start.20 = (f32[3,128,512]{2,1,0:T(8,128)}, f32[3,128,512]{2,1,0:T(8,128)}, u32[]{:S(2)}, u32[]{:S(2)}) collective-permute-start(f32[3,128,512]{2,1,0:T(8,128)} %get-tuple-element.112), channel_id=1, source_target_pairs={{0,32},{1,33},{2,34},{3,35},{4,36},{5,37},{6,38},{7,39},{8,40},{9,... | collective-permute-start | bytes 2359304 | tf_op jit(solution)/shard_map/ppermute | solution.py:47
  279.1 48.8 %collective-permute-start.21 = (f32[3,128,512]{2,1,0:T(8,128)}, f32[3,128,512]{2,1,0:T(8,128)}, u32[]{:S(2)}, u32[]{:S(2)}) collective-permute-start(f32[3,128,512]{2,1,0:T(8,128)} %get-tuple-element.113), channel_id=1, source_target_pairs={{0,64},{1,65},{2,66},{3,67},{4,68},{5,69},{6,70},{7,71},{8,72},{9,... | collective-permute-start | bytes 2359304 | tf_op jit(solution)/shard_map/ppermute | solution.py:47
  308.3 20.5 %collective-permute-start.22 = (f32[3,128,512]{2,1,0:T(8,128)}, f32[3,128,512]{2,1,0:T(8,128)}, u32[]{:S(2)}, u32[]{:S(2)}) collective-permute-start(f32[3,128,512]{2,1,0:T(8,128)} %get-tuple-element.114), channel_id=1, source_target_pairs={{0,96},{1,97},{2,98},{3,99},{4,100},{5,101},{6,102},{7,103},{8,104... | collective-permute-start | bytes 2359304 | tf_op jit(solution)/shard_map/ppermute | solution.py:47
  321.2 14.7 %collective-permute-start.37 = (f32[256,1024]{1,0:T(8,128)}, f32[256,1024]{1,0:T(8,128)}, u32[]{:S(2)}, u32[]{:S(2)}) collective-permute-start(f32[256,1024]{1,0:T(8,128)} %get-tuple-element.134), channel_id=1, source_target_pairs={{0,1},{1,0},{2,3},{3,2},{4,5},{5,4},{6,7},{7,6},{8,9},{9,8},{10,11... | collective-permute-start | bytes 3145736 | tf_op jit(solution)/shard_map/ppermute | solution.py:47
  322.2 16.8 %collective-permute-start.33 = (f32[256,1024]{1,0:T(8,128)}, f32[256,1024]{1,0:T(8,128)}, u32[]{:S(2)}, u32[]{:S(2)}) collective-permute-start(f32[256,1024]{1,0:T(8,128)} %get-tuple-element.129), channel_id=1, source_target_pairs={{0,1},{1,0},{2,3},{3,2},{4,5},{5,4},{6,7},{7,6},{8,9},{9,8},{10,11... | collective-permute-start | bytes 3145736 | tf_op jit(solution)/shard_map/ppermute | solution.py:47
  326.4 20.5 %collective-permute-start.13 = (f32[3,128,512]{2,1,0:T(8,128)}, f32[3,128,512]{2,1,0:T(8,128)S(1)}, u32[]{:S(2)}, u32[]{:S(2)}) collective-permute-start(f32[3,128,512]{2,1,0:T(8,128)} %get-tuple-element.108), channel_id=1, source_target_pairs={{0,32},{1,33},{2,34},{3,35},{4,36},{5,37},{6,38},{7,39},{8,40},{9,... | collective-permute-start | bytes 2359304 | tf_op jit(solution)/shard_map/ppermute | solution.py:47
  327.9 35.3 %collective-permute-start.14 = (f32[3,128,512]{2,1,0:T(8,128)}, f32[3,128,512]{2,1,0:T(8,128)}, u32[]{:S(2)}, u32[]{:S(2)}) collective-permute-start(f32[3,128,512]{2,1,0:T(8,128)} %get-tuple-element.109), channel_id=1, source_target_pairs={{0,64},{1,65},{2,66},{3,67},{4,68},{5,69},{6,70},{7,71},{8,72},{9,... | collective-permute-start | bytes 2359304 | tf_op jit(solution)/shard_map/ppermute | solution.py:47
  328.8 35.1 %collective-permute-start.15 = (f32[3,128,512]{2,1,0:T(8,128)}, f32[3,128,512]{2,1,0:T(8,128)}, u32[]{:S(2)}, u32[]{:S(2)}) collective-permute-start(f32[3,128,512]{2,1,0:T(8,128)} %get-tuple-element.110), channel_id=1, source_target_pairs={{0,96},{1,97},{2,98},{3,99},{4,100},{5,101},{6,102},{7,103},{8,104... | collective-permute-start | bytes 2359304 | tf_op jit(solution)/shard_map/ppermute | solution.py:47
  347.0 16.9 %copy-start.1 = (f32[3,128,512]{2,1,0:T(8,128)}, f32[3,128,512]{2,1,0:T(8,128)S(1)}, u32[]{:S(2)}) copy-start(f32[3,128,512]{2,1,0:T(8,128)S(1)} %collective-permute-done.13.refs_6_) | copy-start | bytes 2359300

commit v5 on v4

--- a/solution.py
+++ b/solution.py
@@ -178,8 +178,8 @@
     return jax.ShapeDtypeStruct(shape, jnp.float32)
 
 
-def _params():
-    return pltpu.CompilerParams(vmem_limit_bytes=63 * 2**20)
+def _params(mib=16):
+    return pltpu.CompilerParams(vmem_limit_bytes=mib * 2**20)
 
 
 def _cost(bytes_, flops=0):
@@ -357,7 +357,7 @@
             pltpu.SemaphoreType.DMA((2,)),
             pltpu.SemaphoreType.DMA((4,)),
         ],
-        compiler_params=_params(),
+        compiler_params=_params(63),
         cost_estimate=_cost(8 * 2**20, 3 * 32 * 2 * 256 * B * B),
     )(table, mine, other, v, x0, q0, q1, x1, *early, *late, *extra)
 
@@ -397,7 +397,7 @@
             pltpu.SemaphoreType.DMA((2,)),
         ],
         input_output_aliases={3: 0} if more else {},
-        compiler_params=_params(),
+        compiler_params=_params(63),
         cost_estimate=_cost(5 * 2**20),
     )(part, ours, theirs, *more)
 
@@ -464,7 +464,7 @@
             pltpu.SemaphoreType.DMA((4,)),
         ],
         input_output_aliases={11: 0} if more else {},
-        compiler_params=_params(),
+        compiler_params=_params(63),
         cost_estimate=_cost((9 if more else 7) * 2**20, 3 * 16 * 2 * B * B * 512),
     )(table, values, v, q0, q1, *own, *late, *more)
 

time: 373 us -> 371 us (level)
  Pallas kernels: 66.7 us -> 61.6 us
  local copies, waits for them, and re-layouts: 4.42 us -> 9.04 us
    unnamed x10 -> x46, local copies, waits for them, and re-layouts: 0.23 us -> 7.03 us
  transfers between devices with their start and end apart: 32 -> 32, of which waited for: 15 -> 14; matrix products, arithmetic and copies ran while one was open for 1% -> 1% of each run, Pallas kernels for 15% -> 14%
where the time goes in v5:
time: 371 us; the launch traced here: 369 us
  waiting for transfers between devices  254 us (68%)
  Pallas kernels  61.6 us (17%)
  starting transfers between devices  42.4 us (11%)
  local copies, waits for them, and re-layouts  9.04 us (2%)
    ppermute x32, waiting for transfers between devices, _send(): return lax.ppermute(value, AXES, pairs)  254 us
    ppermute x32, starting transfers between devices, _send(): return lax.ppermute(value, AXES, pairs)  42.4 us
    pallas_call x6, Pallas kernels, _gather(): pl.pallas_call(kernel, out_shape=[_f32(slots, *slot_shape)] * 3, in_specs...  24.1 us
    pallas_call x2, Pallas kernels, beta_product(): pl.pallas_call(kernel, out_shape=[_f32(256, 1024)] * 2, in_specs=[SMEM] +...  13 us
    pallas_call x2, Pallas kernels, alpha_product(): pl.pallas_call(kernel, out_shape=_f32(1024, 1024 if more else 512), in_sp...  11.8 us
  transfers between devices with their start and end apart: 32, of which 14 were waited for; matrix products, arithmetic and copies ran while one was open for 1% of the time, Pallas kernels for 14%

profile of v5, /device:TPU:9, one launch (start us, length us, event | category | flops | bytes accessed | tf_op | source)
XLA Modules:
  0.0 368.6 jit_solution(14039707620168238407)
XLA Ops:
  0.0 3.4 shard_map.55
  3.4 1.7 collective-permute-start.18
  5.2 1.4 collective-permute-start.6
  6.6 1.3 slice.6
  8.1 1.5 collective-permute-start.24
  9.6 18.3 %collective-permute-done.18.refs_0_.refs_2_.refs_4_ = f32[512,512]{1,0:T(8,128)S(1)} collective-permute-done((f32[512,512]{1,0:T(8,128)S(1)}, f32[512,512]{1,0:T(8,128)S(1)}, u32[]{:S(2)}, u32[]{:S(2)}) %collective-permute-start.18) | collective-permute-done | bytes 1048608 | tf_op jit(solution)/shard_map/ppermute | solution.py:47
  27.9 22.6 %collective-permute-done.8.refs_1_.refs_3_.refs_5_ = f32[512,512]{1,0:T(8,128)} collective-permute-done((f32[512,512]{1,0:T(8,128)S(1)}, f32[512,512]{1,0:T(8,128)}, u32[]{:S(2)}, u32[]{:S(2)}) %collective-permute-start.8) | collective-permute-done | bytes 1048608 | tf_op jit(solution)/shard_map/ppermute | solution.py:47
  50.5 1.2 shard_map.60
  51.7 2.4 collective-permute-start.25
  54.1 18.8 %collective-permute-done.6.refs_1_.refs_3_.refs_5_ = f32[512,512]{1,0:T(8,128)} collective-permute-done((f32[512,512]{1,0:T(8,128)S(1)}, f32[512,512]{1,0:T(8,128)}, u32[]{:S(2)}, u32[]{:S(2)}) %collective-permute-start.6) | collective-permute-done | bytes 1048608 | tf_op jit(solution)/shard_map/ppermute | solution.py:47
  73.0 22.4 %collective-permute-done.16.refs_0_.refs_2_.refs_4_ = f32[512,512]{1,0:T(8,128)S(1)} collective-permute-done((f32[512,512]{1,0:T(8,128)S(1)}, f32[512,512]{1,0:T(8,128)S(1)}, u32[]{:S(2)}, u32[]{:S(2)}) %collective-permute-start.16) | collective-permute-done | bytes 1048608 | tf_op jit(solution)/shard_map/ppermute | solution.py:47
  95.3 1.6 shard_map.63
  96.9 1.4 collective-permute-start.32
  99.4 4.6 %shard_map.56 = (f32[3,128,1024]{2,1,0:T(8,128)}, f32[3,128,1024]{2,1,0:T(8,128)}, f32[3,128,1024]{2,1,0:T(8,128)S(1)}) custom-call(s32[8,128]{1,0:T(8,128)S(1)} %route_table.1.table_ref, f32[1024,1024]{1,0:T(8,128)} %refs_0_.15), custom_call_target="tpu_custom_call" | custom-call | bytes 9437184 | tf_op jit(solution)/shard_map/pallas_call | solution.py:221
  104.0 1.2 copy-done.2
  105.1 1.2 collective-permute-start.10
  106.3 2.4 collective-permute-start.11
  111.7 1.4 copy-done.3
  113.1 1.2 collective-permute-start.12
  115.2 3.7 collective-permute-start.19
  118.8 2.6 collective-permute-start.17
  121.5 5.4 %shard_map.65 = (f32[6,256,128]{2,1,0:T(8,128)S(1)}, f32[6,256,128]{2,1,0:T(8,128)S(1)}, f32[6,256,128]{2,1,0:T(8,128)S(1)}) custom-call(s32[8,128]{1,0:T(8,128)S(1)} %route_table.1.table_ref, f32[1024,1024]{1,0:T(8,128)} %refs_0_.15, f32[2,256,1024]{2,1,0:T(8,128)} %collective-permute-done.24.refs_1_.refs_3_, f32[512,512]{1,0:T(8,128)} %copy-done.8, ...), custom_call_target="tpu_custom_call" | custom-call | bytes 4718592 | tf_op jit(solution)/shard_map/pallas_call | solution.py:221
  126.9 5.1 %shard_map.62 = (f32[6,256,128]{2,1,0:T(8,128)S(1)}, f32[6,256,128]{2,1,0:T(8,128)S(1)}, f32[6,256,128]{2,1,0:T(8,128)S(1)}) custom-call(s32[8,128]{1,0:T(8,128)S(1)} %route_table.1.table_ref, f32[1024,1024]{1,0:T(8,128)S(1)} %copy-done.4, f32[2,256,1024]{2,1,0:T(8,128)} %collective-permute-done.24.refs_1_.refs_3_, ...), custom_call_target="tpu_custom_call" | custom-call | bytes 4718592 | tf_op jit(solution)/shard_map/pallas_call | solution.py:221
  132.0 10.6 %collective-permute-done.10.refs_3_ = f32[3,128,1024]{2,1,0:T(8,128)} collective-permute-done((f32[3,128,1024]{2,1,0:T(8,128)}, f32[3,128,1024]{2,1,0:T(8,128)}, u32[]{:S(2)}, u32[]{:S(2)}) %collective-permute-start.10) | collective-permute-done | bytes 1572896 | tf_op jit(solution)/shard_map/ppermute | solution.py:47
  142.6 1.3 collective-permute-start.34
  143.9 33.3 %collective-permute-done.11.refs_4_ = f32[3,128,1024]{2,1,0:T(8,128)} collective-permute-done((f32[3,128,1024]{2,1,0:T(8,128)}, f32[3,128,1024]{2,1,0:T(8,128)}, u32[]{:S(2)}, u32[]{:S(2)}) %collective-permute-start.11) | collective-permute-done | bytes 1572896 | tf_op jit(solution)/shard_map/ppermute | solution.py:47
  177.2 2.0 collective-permute-start.35
  180.7 2.6 shard_map.61
  183.4 2.9 collective-permute-start.30
  186.3 10.6 %collective-permute-done.35.refs_11_ = f32[6,256,128]{2,1,0:T(8,128)S(1)} collective-permute-done((f32[6,256,128]{2,1,0:T(8,128)S(1)}, f32[6,256,128]{2,1,0:T(8,128)S(1)}, u32[]{:S(2)}, u32[]{:S(2)}) %collective-permute-start.35) | collective-permute-done | bytes 786464 | tf_op jit(solution)/shard_map/ppermute | solution.py:47
  197.1 19.1 %collective-permute-done.36.refs_12_ = f32[6,256,128]{2,1,0:T(8,128)S(1)} collective-permute-done((f32[6,256,128]{2,1,0:T(8,128)S(1)}, f32[6,256,128]{2,1,0:T(8,128)S(1)}, u32[]{:S(2)}, u32[]{:S(2)}) %collective-permute-start.36) | collective-permute-done | bytes 786464 | tf_op jit(solution)/shard_map/ppermute | solution.py:47
  216.2 2.0 collective-permute-start.27
  218.2 12.5 %collective-permute-done.30.refs_11_ = f32[6,256,128]{2,1,0:T(8,128)S(1)} collective-permute-done((f32[6,256,128]{2,1,0:T(8,128)S(1)}, f32[6,256,128]{2,1,0:T(8,128)S(1)}, u32[]{:S(2)}, u32[]{:S(2)}) %collective-permute-start.30) | collective-permute-done | bytes 786464 | tf_op jit(solution)/shard_map/ppermute | solution.py:47
  230.7 3.7 collective-permute-start.7
  234.4 15.6 %collective-permute-done.31.refs_12_ = f32[6,256,128]{2,1,0:T(8,128)S(1)} collective-permute-done((f32[6,256,128]{2,1,0:T(8,128)S(1)}, f32[6,256,128]{2,1,0:T(8,128)S(1)}, u32[]{:S(2)}, u32[]{:S(2)}) %collective-permute-start.31) | collective-permute-done | bytes 786464 | tf_op jit(solution)/shard_map/ppermute | solution.py:47
  250.9 3.7 collective-permute-start.9
  254.5 2.3 shard_map.58
  257.0 18.8 %collective-permute-done.27.refs_8_ = f32[5,2,256,128]{3,2,1,0:T(8,128)S(1)} collective-permute-done((f32[5,2,256,128]{3,2,1,0:T(8,128)S(1)}, f32[5,2,256,128]{3,2,1,0:T(8,128)S(1)}, u32[]{:S(2)}, u32[]{:S(2)}) %collective-permute-start.27) | collective-permute-done | bytes 1310752 | tf_op jit(solution)/shard_map/ppermute | solution.py:47
  276.4 28.5 %collective-permute-done.28.refs_9_ = f32[5,2,256,128]{3,2,1,0:T(8,128)S(1)} collective-permute-done((f32[5,2,256,128]{3,2,1,0:T(8,128)S(1)}, f32[5,2,256,128]{3,2,1,0:T(8,128)S(1)}, u32[]{:S(2)}, u32[]{:S(2)}) %collective-permute-start.28) | collective-permute-done | bytes 1310752 | tf_op jit(solution)/shard_map/ppermute | solution.py:47
  305.9 6.4 %shard_map.66 = (f32[256,1024]{1,0:T(8,128)}, f32[256,1024]{1,0:T(8,128)}) custom-call(s32[8,128]{1,0:T(8,128)S(1)} %route_table.1.table_ref, f32[8,2,128,128]{3,2,1,0:T(8,128)} %refs_0_.14, f32[8,2,128,128]{3,2,1,0:T(8,128)} %collective-permute-done.23.refs_1_, f32[1024,1024]{1,0:T(8,128)} %refs_0_.15, ...), custom_call_target="tpu_custom_call" | custom-call | flops 805306368 | bytes 8388608 | tf_op jit(solution)/shard_map/pallas_call | solution.py:347
  312.4 6.5 %shard_map.64 = (f32[256,1024]{1,0:T(8,128)}, f32[256,1024]{1,0:T(8,128)}) custom-call(s32[8,128]{1,0:T(8,128)S(1)} %route_table.1.table_ref, f32[8,2,128,128]{3,2,1,0:T(8,128)} %refs_0_.14, f32[8,2,128,128]{3,2,1,0:T(8,128)} %collective-permute-done.23.refs_1_, f32[1024,1024]{1,0:T(8,128)} %refs_0_.15, ...), custom_call_target="tpu_custom_call" | custom-call | flops 805306368 | bytes 8388608 | tf_op jit(solution)/shard_map/pallas_call | solution.py:347
  319.8 4.0 %shard_map.57 = (f32[3,128,512]{2,1,0:T(8,128)}, f32[3,128,512]{2,1,0:T(8,128)}, f32[3,128,512]{2,1,0:T(8,128)}) custom-call(s32[8,128]{1,0:T(8,128)S(1)} %route_table.1.table_ref, f32[512,512]{1,0:T(8,128)} %collective-permute-done.7.refs_0_.refs_1_, f32[512,512]{1,0:T(8,128)} %collective-permute-done.9.refs_1_.refs_2_), custom_call_target="tpu_custom_call" | custom-call | bytes 4718592 | tf_op jit(solution)/shard_map/pallas_call | solution.py:221
  324.9 2.0 collective-permute-start.15
  326.9 5.6 %shard_map.59.part_ref = f32[1024,512]{1,0:T(8,128)} custom-call(s32[8,128]{1,0:T(8,128)S(1)} %route_table.1.table_ref, f32[8,2,128,128]{3,2,1,0:T(8,128)} %weights.3, f32[1024,1024]{1,0:T(8,128)} %refs_0_.15, f32[512,512]{1,0:T(8,128)} %copy-done.1, f32[512,512]{1,0:T(8,128)} %copy-done, f32[3,128,1024]{2,1,0:T(8,128)} %collective-permute-done.10.refs_3_, ...), custom_call_target="tpu_custom_call" | custom-call | flops 805306368 | bytes 7340032 | tf_op jit(solution)/shard_map/pallas_call | solution.py:453
  332.5 2.9 shard_map.67.refs_0_
  335.5 3.0 shard_map.68.refs_9_
  338.4 22.6 %collective-permute-done.13.refs_6_ = f32[3,128,512]{2,1,0:T(8,128)} collective-permute-done((f32[3,128,512]{2,1,0:T(8,128)}, f32[3,128,512]{2,1,0:T(8,128)}, u32[]{:S(2)}, u32[]{:S(2)}) %collective-permute-start.13) | collective-permute-done | bytes 786464 | tf_op jit(solution)/shard_map/ppermute | solution.py:47
  362.2 6.2 %shard_map.69 = f32[1024,1024]{1,0:T(8,128)} custom-call(s32[8,128]{1,0:T(8,128)S(1)} %route_table.1.table_ref, f32[8,2,128,128]{3,2,1,0:T(8,128)} %weights.3, f32[1024,1024]{1,0:T(8,128)} %refs_0_.15, f32[512,512]{1,0:T(8,128)} %collective-permute-done.7.refs_0_.refs_1_, ...), custom_call_target="tpu_custom_call", output_to_operand_aliasing={{}: (11, {})} | custom-call | flops 805306368 | bytes 9437184 | tf_op jit(solution)/shard_map/pallas_call | solution.py:453
  (86 shorter events, 11.7 us)
Async XLA Ops:
  3.4 24.5 %collective-permute-start.18 = (f32[512,512]{1,0:T(8,128)S(1)}, f32[512,512]{1,0:T(8,128)S(1)}, u32[]{:S(2)}, u32[]{:S(2)}) collective-permute-start(f32[512,512]{1,0:T(8,128)S(1)} %get-tuple-element.111), channel_id=1, source_target_pairs={{0,8},{1,9},{2,10},{3,11},{4,12},{5,13},{6,14},{7,15},{8,0},{9,1},... | collective-permute-start | bytes 3145736 | tf_op jit(solution)/shard_map/ppermute | solution.py:47
  5.2 45.3 %collective-permute-start.8 = (f32[512,512]{1,0:T(8,128)S(1)}, f32[512,512]{1,0:T(8,128)}, u32[]{:S(2)}, u32[]{:S(2)}) collective-permute-start(f32[512,512]{1,0:T(8,128)S(1)} %get-tuple-element.104), channel_id=1, source_target_pairs={{0,8},{1,9},{2,10},{3,11},{4,12},{5,13},{6,14},{7,15},{8,0},{9,1},... | collective-permute-start | bytes 3145736 | tf_op jit(solution)/shard_map/ppermute | solution.py:47
  5.2 67.7 %collective-permute-start.6 = (f32[512,512]{1,0:T(8,128)S(1)}, f32[512,512]{1,0:T(8,128)}, u32[]{:S(2)}, u32[]{:S(2)}) collective-permute-start(f32[512,512]{1,0:T(8,128)S(1)} %get-tuple-element.103), channel_id=1, source_target_pairs={{0,8},{1,9},{2,10},{3,11},{4,12},{5,13},{6,14},{7,15},{8,0},{9,1},... | collective-permute-start | bytes 3145736 | tf_op jit(solution)/shard_map/ppermute | solution.py:47
  7.9 87.4 %collective-permute-start.16 = (f32[512,512]{1,0:T(8,128)S(1)}, f32[512,512]{1,0:T(8,128)S(1)}, u32[]{:S(2)}, u32[]{:S(2)}) collective-permute-start(f32[512,512]{1,0:T(8,128)S(1)} %slice.6), channel_id=1, source_target_pairs={{0,8},{1,9},{2,10},{3,11},{4,12},{5,13},{6,14},{7,15},{8,0},{9,1},... | collective-permute-start | bytes 3145736 | tf_op jit(solution)/shard_map/ppermute | solution.py:47
  8.1 102.3 %collective-permute-start.24 = (f32[2,256,1024]{2,1,0:T(8,128)}, f32[2,256,1024]{2,1,0:T(8,128)}, u32[]{:S(2)}, u32[]{:S(2)}) collective-permute-start(f32[2,256,1024]{2,1,0:T(8,128)} %get-tuple-element.115), channel_id=1, source_target_pairs={{0,1},{1,0},{2,3},{3,2},{4,5},{5,4},{6,7},{7,6},{8,9},{9,8},{10,11... | collective-permute-start | bytes 6291464 | tf_op jit(solution)/shard_map/ppermute | solution.py:47
  27.9 99.0 %copy-start.7 = (f32[512,512]{1,0:T(8,128)}, f32[512,512]{1,0:T(8,128)S(1)}, u32[]{:S(2)}) copy-start(f32[512,512]{1,0:T(8,128)S(1)} %collective-permute-done.18.refs_0_.refs_2_.refs_4_) | copy-start | bytes 3145732
  51.7 46.6 %copy-start.22 = (s32[128,2]{0,1:T(2,128)S(1)}, s32[128,2]{0,1:T(2,128)}, u32[]{:S(2)}) copy-start(s32[128,2]{0,1:T(2,128)} %param.12) | copy-start | bytes 3076
  51.7 46.8 %copy-start.23 = (s32[64,2]{0,1:T(2,128)S(1)}, s32[64,2]{0,1:T(2,128)}, u32[]{:S(2)}) copy-start(s32[64,2]{0,1:T(2,128)} %param.10) | copy-start | bytes 1540
  51.7 58.6 %collective-permute-start.25 = (f32[2,256,512]{2,1,0:T(8,128)S(1)}, f32[2,256,512]{2,1,0:T(8,128)}, u32[]{:S(2)}, u32[]{:S(2)}) collective-permute-start(f32[2,256,512]{2,1,0:T(8,128)S(1)} %shard_map.60), channel_id=1, source_target_pairs={{0,1},{1,0},{2,3},{3,2},{4,5},{5,4},{6,7},{7,6},{8,9},{9,8},{10,11... | collective-permute-start | bytes 3145736 | tf_op jit(solution)/shard_map/ppermute | solution.py:47
  95.3 1.6 copy-start.8
  96.9 13.4 %collective-permute-start.32 = (f32[2,256,512]{2,1,0:T(8,128)S(1)}, f32[2,256,512]{2,1,0:T(8,128)}, u32[]{:S(2)}, u32[]{:S(2)}) collective-permute-start(f32[2,256,512]{2,1,0:T(8,128)S(1)} %shard_map.63), channel_id=1, source_target_pairs={{0,1},{1,0},{2,3},{3,2},{4,5},{5,4},{6,7},{7,6},{8,9},{9,8},{10,11... | collective-permute-start | bytes 3145736 | tf_op jit(solution)/shard_map/ppermute | solution.py:47
  105.1 37.5 %collective-permute-start.10 = (f32[3,128,1024]{2,1,0:T(8,128)}, f32[3,128,1024]{2,1,0:T(8,128)}, u32[]{:S(2)}, u32[]{:S(2)}) collective-permute-start(f32[3,128,1024]{2,1,0:T(8,128)} %get-tuple-element.105), channel_id=1, source_target_pairs={{0,32},{1,33},{2,34},{3,35},{4,36},{5,37},{6,38},{7,39},{8,40},{9,... | collective-permute-start | bytes 4718600 | tf_op jit(solution)/shard_map/ppermute | solution.py:47
  106.3 70.9 %collective-permute-start.11 = (f32[3,128,1024]{2,1,0:T(8,128)}, f32[3,128,1024]{2,1,0:T(8,128)}, u32[]{:S(2)}, u32[]{:S(2)}) collective-permute-start(f32[3,128,1024]{2,1,0:T(8,128)} %get-tuple-element.106), channel_id=1, source_target_pairs={{0,64},{1,65},{2,66},{3,67},{4,68},{5,69},{6,70},{7,71},{8,72},{9,... | collective-permute-start | bytes 4718600 | tf_op jit(solution)/shard_map/ppermute | solution.py:47
  111.7 1.4 copy-start.3
  113.1 66.0 %collective-permute-start.12 = (f32[3,128,1024]{2,1,0:T(8,128)S(1)}, f32[3,128,1024]{2,1,0:T(8,128)S(1)}, u32[]{:S(2)}, u32[]{:S(2)}) collective-permute-start(f32[3,128,1024]{2,1,0:T(8,128)S(1)} %copy-done.3), channel_id=1, source_target_pairs={{0,96},{1,97},{2,98},{3,99},{4,100},{5,101},{6,102},{7,103},{8,104... | collective-permute-start | bytes 4718600 | tf_op jit(solution)/shard_map/ppermute | solution.py:47
  114.3 4.5 %collective-permute-start.23 = (f32[8,2,128,128]{3,2,1,0:T(8,128)}, f32[8,2,128,128]{3,2,1,0:T(8,128)}, u32[]{:S(2)}, u32[]{:S(2)}) collective-permute-start(f32[8,2,128,128]{3,2,1,0:T(8,128)} %refs_0_.14), channel_id=1, source_target_pairs={{0,1},{1,0},{2,3},{3,2},{4,5},{5,4},{6,7},{7,6},{8,9},{9,8},{10,11... | collective-permute-start | bytes 3145736 | tf_op jit(solution)/shard_map/ppermute | solution.py:47
  115.2 65.1 %collective-permute-start.19 = (f32[512,512]{1,0:T(8,128)S(1)}, f32[512,512]{1,0:T(8,128)S(1)}, u32[]{:S(2)}, u32[]{:S(2)}) collective-permute-start(f32[512,512]{1,0:T(8,128)S(1)} %collective-permute-done.18.refs_0_.refs_2_.refs_4_), channel_id=1, source_target_pairs={{0,24},{1,25},{2,26},{3,27},{4,28},{5,29},{6,30},{7,31},{8,16},{9,... | collective-permute-start | bytes 3145736 | tf_op jit(solution)/shard_map/ppermute | solution.py:47
  118.8 64.5 %collective-permute-start.17 = (f32[512,512]{1,0:T(8,128)}, f32[512,512]{1,0:T(8,128)S(1)}, u32[]{:S(2)}, u32[]{:S(2)}) collective-permute-start(f32[512,512]{1,0:T(8,128)} %copy-done.8), channel_id=1, source_target_pairs={{0,24},{1,25},{2,26},{3,27},{4,28},{5,29},{6,30},{7,31},{8,16},{9,... | collective-permute-start | bytes 3145736 | tf_op jit(solution)/shard_map/ppermute | solution.py:47
  121.5 5.4 %copy-start.4 = (f32[1024,1024]{1,0:T(8,128)S(1)}, f32[1024,1024]{1,0:T(8,128)}, u32[]{:S(2)}) copy-start(f32[1024,1024]{1,0:T(8,128)} %refs_0_.15) | copy-start | bytes 12582916
  142.6 40.8 %collective-permute-start.34 = (f32[6,256,128]{2,1,0:T(8,128)S(1)}, f32[6,256,128]{2,1,0:T(8,128)S(1)}, u32[]{:S(2)}, u32[]{:S(2)}) collective-permute-start(f32[6,256,128]{2,1,0:T(8,128)S(1)} %get-tuple-element.130), channel_id=1, source_target_pairs={{0,2},{1,3},{2,4},{3,5},{4,6},{5,7},{6,0},{7,1},{8,10},{9,11},{10,... | collective-permute-start | bytes 2359304 | tf_op jit(solution)/shard_map/ppermute | solution.py:47
  177.2 19.8 %collective-permute-start.35 = (f32[6,256,128]{2,1,0:T(8,128)S(1)}, f32[6,256,128]{2,1,0:T(8,128)S(1)}, u32[]{:S(2)}, u32[]{:S(2)}) collective-permute-start(f32[6,256,128]{2,1,0:T(8,128)S(1)} %get-tuple-element.131), channel_id=1, source_target_pairs={{0,4},{1,5},{2,6},{3,7},{4,0},{5,1},{6,2},{7,3},{8,12},{9,13},{10,... | collective-permute-start | bytes 2359304 | tf_op jit(solution)/shard_map/ppermute | solution.py:47
  179.2 4.1 %copy-start.9 = (f32[3,128,1024]{2,1,0:T(8,128)}, f32[3,128,1024]{2,1,0:T(8,128)S(1)}, u32[]{:S(2)}) copy-start(f32[3,128,1024]{2,1,0:T(8,128)S(1)} %collective-permute-done.12.refs_5_) | copy-start | bytes 4718596
  179.2 37.0 %collective-permute-start.36 = (f32[6,256,128]{2,1,0:T(8,128)S(1)}, f32[6,256,128]{2,1,0:T(8,128)S(1)}, u32[]{:S(2)}, u32[]{:S(2)}) collective-permute-start(f32[6,256,128]{2,1,0:T(8,128)S(1)} %get-tuple-element.132), channel_id=1, source_target_pairs={{0,6},{1,7},{2,0},{3,1},{4,2},{5,3},{6,4},{7,5},{8,14},{9,15},{10,... | collective-permute-start | bytes 2359304 | tf_op jit(solution)/shard_map/ppermute | solution.py:47
  180.3 74.3 %copy-start = (f32[512,512]{1,0:T(8,128)}, f32[512,512]{1,0:T(8,128)S(1)}, u32[]{:S(2)}) copy-start(f32[512,512]{1,0:T(8,128)S(1)} %collective-permute-done.19.refs_1_.refs_2_) | copy-start | bytes 3145732
  180.3 37.9 %collective-permute-start.29 = (f32[6,256,128]{2,1,0:T(8,128)S(1)}, f32[6,256,128]{2,1,0:T(8,128)S(1)}, u32[]{:S(2)}, u32[]{:S(2)}) collective-permute-start(f32[6,256,128]{2,1,0:T(8,128)S(1)} %get-tuple-element.119), channel_id=1, source_target_pairs={{0,2},{1,3},{2,4},{3,5},{4,6},{5,7},{6,0},{7,1},{8,10},{9,11},{10,... | collective-permute-start | bytes 2359304 | tf_op jit(solution)/shard_map/ppermute | solution.py:47
  183.3 73.5 %copy-start.1 = (f32[512,512]{1,0:T(8,128)}, f32[512,512]{1,0:T(8,128)S(1)}, u32[]{:S(2)}) copy-start(f32[512,512]{1,0:T(8,128)S(1)} %collective-permute-done.17.refs_0_.refs_1_) | copy-start | bytes 3145732
  183.3 73.5 %collective-permute-start.26 = (f32[5,2,256,128]{3,2,1,0:T(8,128)S(1)}, f32[5,2,256,128]{3,2,1,0:T(8,128)S(1)}, u32[]{:S(2)}, u32[]{:S(2)}) collective-permute-start(f32[5,2,256,128]{3,2,1,0:T(8,128)S(1)} %get-tuple-element.116), channel_id=1, source_target_pairs={{0,2},{1,3},{2,4},{3,5},{4,6},{5,7},{6,0},{7,1},{8,10},{9,11},{10,... | collective-permute-start | bytes 3932168 | tf_op jit(solution)/shard_map/ppermute | solution.py:47
  183.4 122.5 %copy-start.15 = (f32[6,256,128]{2,1,0:T(8,128)}, f32[6,256,128]{2,1,0:T(8,128)S(1)}, u32[]{:S(2)}) copy-start(f32[6,256,128]{2,1,0:T(8,128)S(1)} %collective-permute-done.34.refs_10_) | copy-start | bytes 2359300
  183.4 47.2 %collective-permute-start.30 = (f32[6,256,128]{2,1,0:T(8,128)S(1)}, f32[6,256,128]{2,1,0:T(8,128)S(1)}, u32[]{:S(2)}, u32[]{:S(2)}) collective-permute-start(f32[6,256,128]{2,1,0:T(8,128)S(1)} %get-tuple-element.120), channel_id=1, source_target_pairs={{0,4},{1,5},{2,6},{3,7},{4,0},{5,1},{6,2},{7,3},{8,12},{9,13},{10,... | collective-permute-start | bytes 2359304 | tf_op jit(solution)/shard_map/ppermute | solution.py:47
  196.9 109.0 %copy-start.16 = (f32[6,256,128]{2,1,0:T(8,128)}, f32[6,256,128]{2,1,0:T(8,128)S(1)}, u32[]{:S(2)}) copy-start(f32[6,256,128]{2,1,0:T(8,128)S(1)} %collective-permute-done.35.refs_11_) | copy-start | bytes 2359300
  196.9 53.0 %collective-permute-start.31 = (f32[6,256,128]{2,1,0:T(8,128)S(1)}, f32[6,256,128]{2,1,0:T(8,128)S(1)}, u32[]{:S(2)}, u32[]{:S(2)}) collective-permute-start(f32[6,256,128]{2,1,0:T(8,128)S(1)} %get-tuple-element.121), channel_id=1, source_target_pairs={{0,6},{1,7},{2,0},{3,1},{4,2},{5,3},{6,4},{7,5},{8,14},{9,15},{10,... | collective-permute-start | bytes 2359304 | tf_op jit(solution)/shard_map/ppermute | solution.py:47
  216.2 89.8 %copy-start.18 = (f32[6,256,128]{2,1,0:T(8,128)}, f32[6,256,128]{2,1,0:T(8,128)S(1)}, u32[]{:S(2)}) copy-start(f32[6,256,128]{2,1,0:T(8,128)S(1)} %collective-permute-done.36.refs_12_) | copy-start | bytes 2359300
  216.2 59.6 %collective-permute-start.27 = (f32[5,2,256,128]{3,2,1,0:T(8,128)S(1)}, f32[5,2,256,128]{3,2,1,0:T(8,128)S(1)}, u32[]{:S(2)}, u32[]{:S(2)}) collective-permute-start(f32[5,2,256,128]{3,2,1,0:T(8,128)S(1)} %get-tuple-element.117), channel_id=1, source_target_pairs={{0,4},{1,5},{2,6},{3,7},{4,0},{5,1},{6,2},{7,3},{8,12},{9,13},{10,... | collective-permute-start | bytes 3932168 | tf_op jit(solution)/shard_map/ppermute | solution.py:47
  218.2 87.7 %copy-start.17 = (f32[6,256,128]{2,1,0:T(8,128)}, f32[6,256,128]{2,1,0:T(8,128)S(1)}, u32[]{:S(2)}) copy-start(f32[6,256,128]{2,1,0:T(8,128)S(1)} %collective-permute-done.29.refs_10_) | copy-start | bytes 2359300
  218.2 86.7 %collective-permute-start.28 = (f32[5,2,256,128]{3,2,1,0:T(8,128)S(1)}, f32[5,2,256,128]{3,2,1,0:T(8,128)S(1)}, u32[]{:S(2)}, u32[]{:S(2)}) collective-permute-start(f32[5,2,256,128]{3,2,1,0:T(8,128)S(1)} %get-tuple-element.118), channel_id=1, source_target_pairs={{0,6},{1,7},{2,0},{3,1},{4,2},{5,3},{6,4},{7,5},{8,14},{9,15},{10,... | collective-permute-start | bytes 3932168 | tf_op jit(solution)/shard_map/ppermute | solution.py:47
  230.7 19.3 %copy-start.19 = (f32[6,256,128]{2,1,0:T(8,128)}, f32[6,256,128]{2,1,0:T(8,128)S(1)}, u32[]{:S(2)}) copy-start(f32[6,256,128]{2,1,0:T(8,128)S(1)} %collective-permute-done.30.refs_11_) | copy-start | bytes 2359300
  230.7 88.2 %collective-permute-start.7 = (f32[512,512]{1,0:T(8,128)}, f32[512,512]{1,0:T(8,128)}, u32[]{:S(2)}, u32[]{:S(2)}) collective-permute-start(f32[512,512]{1,0:T(8,128)} %collective-permute-done.6.refs_1_.refs_3_.refs_5_), channel_id=1, source_target_pairs={{0,24},{1,25},{2,26},{3,27},{4,28},{5,29},{6,30},{7,31},{8,16},{9,... | collective-permute-start | bytes 3145736 | tf_op jit(solution)/shard_map/ppermute | solution.py:47
  250.9 68.8 %collective-permute-start.9 = (f32[512,512]{1,0:T(8,128)}, f32[512,512]{1,0:T(8,128)}, u32[]{:S(2)}, u32[]{:S(2)}) collective-permute-start(f32[512,512]{1,0:T(8,128)} %collective-permute-done.8.refs_1_.refs_3_.refs_5_), channel_id=1, source_target_pairs={{0,24},{1,25},{2,26},{3,27},{4,28},{5,29},{6,30},{7,31},{8,16},{9,... | collective-permute-start | bytes 3145736 | tf_op jit(solution)/shard_map/ppermute | solution.py:47
  256.9 48.0 %copy-start.10 = (f32[5,2,256,128]{3,2,1,0:T(8,128)}, f32[5,2,256,128]{3,2,1,0:T(8,128)S(1)}, u32[]{:S(2)}) copy-start(f32[5,2,256,128]{3,2,1,0:T(8,128)S(1)} %collective-permute-done.26.refs_7_) | copy-start | bytes 3932164
  256.9 67.0 %collective-permute-start.20 = (f32[3,128,512]{2,1,0:T(8,128)}, f32[3,128,512]{2,1,0:T(8,128)}, u32[]{:S(2)}, u32[]{:S(2)}) collective-permute-start(f32[3,128,512]{2,1,0:T(8,128)} %get-tuple-element.112), channel_id=1, source_target_pairs={{0,32},{1,33},{2,34},{3,35},{4,36},{5,37},{6,38},{7,39},{8,40},{9,... | collective-permute-start | bytes 2359304 | tf_op jit(solution)/shard_map/ppermute | solution.py:47
  275.8 29.1 %copy-start.11 = (f32[5,2,256,128]{3,2,1,0:T(8,128)}, f32[5,2,256,128]{3,2,1,0:T(8,128)S(1)}, u32[]{:S(2)}) copy-start(f32[5,2,256,128]{3,2,1,0:T(8,128)S(1)} %collective-permute-done.27.refs_8_) | copy-start | bytes 3932164
  275.8 48.7 %collective-permute-start.21 = (f32[3,128,512]{2,1,0:T(8,128)}, f32[3,128,512]{2,1,0:T(8,128)}, u32[]{:S(2)}, u32[]{:S(2)}) collective-permute-start(f32[3,128,512]{2,1,0:T(8,128)} %get-tuple-element.113), channel_id=1, source_target_pairs={{0,64},{1,65},{2,66},{3,67},{4,68},{5,69},{6,70},{7,71},{8,72},{9,... | collective-permute-start | bytes 2359304 | tf_op jit(solution)/shard_map/ppermute | solution.py:47
  304.9 20.1 %collective-permute-start.22 = (f32[3,128,512]{2,1,0:T(8,128)S(1)}, f32[3,128,512]{2,1,0:T(8,128)}, u32[]{:S(2)}, u32[]{:S(2)}) collective-permute-start(f32[3,128,512]{2,1,0:T(8,128)S(1)} %get-tuple-element.114), channel_id=1, source_target_pairs={{0,96},{1,97},{2,98},{3,99},{4,100},{5,101},{6,102},{7,103},{8,104... | collective-permute-start | bytes 2359304 | tf_op jit(solution)/shard_map/ppermute | solution.py:47
  318.9 13.6 %collective-permute-start.37 = (f32[256,1024]{1,0:T(8,128)}, f32[256,1024]{1,0:T(8,128)}, u32[]{:S(2)}, u32[]{:S(2)}) collective-permute-start(f32[256,1024]{1,0:T(8,128)} %get-tuple-element.134), channel_id=1, source_target_pairs={{0,1},{1,0},{2,3},{3,2},{4,5},{5,4},{6,7},{7,6},{8,9},{9,8},{10,11... | collective-permute-start | bytes 3145736 | tf_op jit(solution)/shard_map/ppermute | solution.py:47
  319.7 15.8 %collective-permute-start.33 = (f32[256,1024]{1,0:T(8,128)}, f32[256,1024]{1,0:T(8,128)}, u32[]{:S(2)}, u32[]{:S(2)}) collective-permute-start(f32[256,1024]{1,0:T(8,128)} %get-tuple-element.129), channel_id=1, source_target_pairs={{0,1},{1,0},{2,3},{3,2},{4,5},{5,4},{6,7},{7,6},{8,9},{9,8},{10,11... | collective-permute-start | bytes 3145736 | tf_op jit(solution)/shard_map/ppermute | solution.py:47
  323.8 37.1 %collective-permute-start.13 = (f32[3,128,512]{2,1,0:T(8,128)}, f32[3,128,512]{2,1,0:T(8,128)}, u32[]{:S(2)}, u32[]{:S(2)}) collective-permute-start(f32[3,128,512]{2,1,0:T(8,128)} %get-tuple-element.108), channel_id=1, source_target_pairs={{0,32},{1,33},{2,34},{3,35},{4,36},{5,37},{6,38},{7,39},{8,40},{9,... | collective-permute-start | bytes 2359304 | tf_op jit(solution)/shard_map/ppermute | solution.py:47
  324.4 36.6 %collective-permute-start.14 = (f32[3,128,512]{2,1,0:T(8,128)}, f32[3,128,512]{2,1,0:T(8,128)}, u32[]{:S(2)}, u32[]{:S(2)}) collective-permute-start(f32[3,128,512]{2,1,0:T(8,128)} %get-tuple-element.109), channel_id=1, source_target_pairs={{0,64},{1,65},{2,66},{3,67},{4,68},{5,69},{6,70},{7,71},{8,72},{9,... | collective-permute-start | bytes 2359304 | tf_op jit(solution)/shard_map/ppermute | solution.py:47
  324.9 36.4 %collective-permute-start.15 = (f32[3,128,512]{2,1,0:T(8,128)}, f32[3,128,512]{2,1,0:T(8,128)S(1)}, u32[]{:S(2)}, u32[]{:S(2)}) collective-permute-start(f32[3,128,512]{2,1,0:T(8,128)} %get-tuple-element.110), channel_id=1, source_target_pairs={{0,96},{1,97},{2,98},{3,99},{4,100},{5,101},{6,102},{7,103},{8,104... | collective-permute-start | bytes 2359304 | tf_op jit(solution)/shard_map/ppermute | solution.py:47
  (6 other events, 6.4 us)
